TPU v7x, 32 devices: a whole 2x2x4 slice. The times are simulated.
32 devices in a mesh: seq: 4 (over z), dp: 8 (over y, x, core).
Axes of the slice: x: 2, y: 2, z: 4, core: 2. Of those that a mesh axis runs over, the one named last changes fastest.
Arguments:
- stream: float32 [8, 512, 1152], P('dp', 'seq'), may hold values from -50 to 50
- stream_grad: float32 [8, 512, 1152], P('dp', 'seq'), may hold values from -6 to 6
- lengths: int32 [8, 4], P('dp'), may hold values from 1 to 384, 512 in all within a row
- w_qkv: bfloat16 [1152, 1536], P(('seq', 'dp')), may hold values from -0.1875 to 0.1875
- w_out: bfloat16 [1024, 1152], P(('seq', 'dp')), may hold values from -0.1875 to 0.1875
- w_gate: bfloat16 [6912, 1152], P(('seq', 'dp')), may hold values from -0.1875 to 0.1875
- w_up: bfloat16 [6912, 1152], P(('seq', 'dp')), may hold values from -0.1875 to 0.1875
- w_down: bfloat16 [6912, 1152], P(('seq', 'dp')), may hold values from -0.078125 to 0.078125
- g_attn_in: float32 [1152], replicated, may hold values from 0.25 to 1.75
- g_query: float32 [256], replicated, may hold values from 0.25 to 1.75
- g_key: float32 [256], replicated, may hold values from 0.25 to 1.75
- g_attn_out: float32 [1152], replicated, may hold values from 0.25 to 1.75
- g_ffn_in: float32 [1152], replicated, may hold values from 0.25 to 1.75
- g_ffn_out: float32 [1152], replicated, may hold values from 0.25 to 1.75
Outputs:
- result: float32 [8, 512, 1152], P('dp', 'seq')
- input_grad: float32 [8, 512, 1152], P('dp', 'seq')
- grad_w_qkv: float32 [1152, 1536], P(('seq', 'dp'))
- grad_w_out: float32 [1024, 1152], P(('seq', 'dp'))
- grad_w_gate: float32 [6912, 1152], P(('seq', 'dp'))
- grad_w_up: float32 [6912, 1152], P(('seq', 'dp'))
- grad_w_down: float32 [6912, 1152], P(('seq', 'dp'))
- grad_g_attn_in: float32 [1152], P(('seq', 'dp'))
- grad_g_query: float32 [256], P(('seq', 'dp'))
- grad_g_key: float32 [256], P(('seq', 'dp'))
- grad_g_attn_out: float32 [1152], P(('seq', 'dp'))
- grad_g_ffn_in: float32 [1152], P(('seq', 'dp'))
- grad_g_ffn_out: float32 [1152], P(('seq', 'dp'))
Inputs may be any that keep to these rules, and one draw needn't show every extreme that they name: Each row lists the lengths of the 4 sequences packed in order into one group; they sum to 512.
All inputs are finite; a program needn't handle non-finite values.
Results may differ from a plain program's by a relative error of at most 0.015.
Values may be sent and summed in bfloat16 or wider, within the bound.
A program may use at most 128 MiB of HBM per device.

v0:
```python
import math

import jax
import jax.numpy as jnp
from jax import lax
from jax.sharding import PartitionSpec as P

HEADS = 4
HEAD_DIM = 256
WINDOW = 512


EPSILON = 1e-06
GELU_SLOPE = math.sqrt(2.0 / math.pi)
GELU_CUBIC = 0.044715


def passed_along(value, axis, by):
    length = lax.axis_size(axis)
    pairs = [(i, i + by) for i in range(length) if 0 <= i + by < length]
    return lax.ppermute(value, axis, pairs)


def inv_root(vector):
    return lax.rsqrt(jnp.mean(vector * vector, axis=-1, keepdims=True) + EPSILON)


def norm_back(grad, unit_part, root_part, gain):
    scaled = grad * gain
    return root_part * (scaled - unit_part * jnp.mean(scaled * unit_part, axis=-1, keepdims=True))


def gelu_pair(gate):
    inner = jnp.tanh(GELU_SLOPE * (gate + GELU_CUBIC * gate * gate * gate))
    gelu_value = 0.5 * gate * (1.0 + inner)
    gelu_slope = 0.5 * (1.0 + inner) + 0.5 * gate * (1.0 - inner * inner) * GELU_SLOPE * (
        1.0 + 3.0 * GELU_CUBIC * gate * gate
    )
    return (gelu_value, gelu_slope)


def turn_half(vector):
    half = vector.shape[-1] // 2
    return jnp.concatenate([-vector[..., half:], vector[..., :half]], axis=-1)


def seq_begin(index, starts):
    return jnp.max(jnp.where(starts[None, :] <= index[:, None], starts[None, :], 0), axis=1)


def rope_tables(position, head):
    freq = jnp.exp(-math.log(10000.0) * jnp.arange(head // 2, dtype=jnp.float32) * (2.0 / head))
    angle = position[:, None] * freq[None, :]
    angle = jnp.concatenate([angle, angle], axis=1)
    return (jnp.cos(angle), jnp.sin(angle))


def dot32(left, right):
    return jnp.dot(left, right, preferred_element_type=jnp.float32)


def contract_rows(left, right):
    return lax.dot_general(
        left, right, (((0,), (0,)), ((), ())), preferred_element_type=jnp.float32
    )


def contract_cols(left, right):
    return lax.dot_general(
        left, right, (((1,), (1,)), ((), ())), preferred_element_type=jnp.float32
    )


def ffn_forward_fold(tokens_b, pieces):
    gate_rows, up_rows, down_rows = pieces
    gate_part = contract_cols(tokens_b, gate_rows)
    up_part = contract_cols(tokens_b, up_rows)
    gelu_value, gelu_slope = gelu_pair(gate_part)
    hidden = (gelu_value * up_part).astype(jnp.bfloat16)
    out_total = dot32(hidden, down_rows)
    return (out_total, gate_part, up_part)


def ffn_backward_fold(grad_b, gate_all, up_all, pieces):
    gate_rows, up_rows, down_rows = pieces
    hidden_grad = contract_cols(grad_b, down_rows)
    gelu_value, gelu_slope = gelu_pair(gate_all)
    dgate_b = (hidden_grad * up_all * gelu_slope).astype(jnp.bfloat16)
    dup_b = (hidden_grad * gelu_value).astype(jnp.bfloat16)
    in_total = dot32(dgate_b, gate_rows) + dot32(dup_b, up_rows)
    return (in_total, dgate_b, dup_b)


def ffn_weight_terms(tokens_b, grad_b, gate_all, up_all, dgate_all, dup_all):
    gelu_value, gelu_slope = gelu_pair(gate_all)
    hidden = (gelu_value * up_all).astype(jnp.bfloat16)
    return jnp.concatenate(
        [
            contract_rows(dgate_all, tokens_b),
            contract_rows(dup_all, tokens_b),
            contract_rows(hidden, grad_b),
        ],
        axis=1,
    )


def local(
    stream,
    stream_grad,
    lengths,
    w_qkv,
    w_out,
    w_gate,
    w_up,
    w_down,
    g_attn_in,
    g_query,
    g_key,
    g_attn_out,
    g_ffn_in,
    g_ffn_out,
):
    rows_in = stream[0]
    rows_grad = stream_grad[0]
    lens = lengths[0]
    rows = rows_in.shape[0]
    width = rows_in.shape[1]
    qwidth = HEADS * HEAD_DIM
    hops = (WINDOW + rows - 2) // rows
    keys = (hops + 1) * rows
    scale = 1.0 / math.sqrt(HEAD_DIM)
    qkv_full, out_full = (
        lax.all_gather(w_qkv, ("seq", "dp"), axis=0, tiled=True),
        lax.all_gather(w_out, ("seq", "dp"), axis=0, tiled=True),
    )
    block_id = lax.axis_index("seq")
    starts = jnp.cumsum(lens) - lens
    own_index = block_id * rows + jnp.arange(rows, dtype=jnp.int32)
    key_index = block_id * rows - hops * rows + jnp.arange(keys, dtype=jnp.int32)
    own_begin = seq_begin(own_index, starts)
    key_begin = seq_begin(key_index, starts)
    mask = (
        (key_index[None, :] >= 0)
        & (key_begin[None, :] == own_begin[:, None])
        & (key_index[None, :] <= own_index[:, None])
        & (own_index[:, None] - key_index[None, :] < WINDOW)
    )
    full_mask = mask[:, None, :]
    cos_t, sin_t = rope_tables((own_index - own_begin).astype(jnp.float32), HEAD_DIM)
    root_attn = inv_root(rows_in)
    unit_attn = rows_in * root_attn
    attn_input = (unit_attn * g_attn_in).astype(jnp.bfloat16)
    projected = dot32(attn_input, qkv_full)
    query = projected[:, :qwidth].reshape(rows, HEADS, HEAD_DIM)
    key_raw = projected[:, qwidth : qwidth + HEAD_DIM]
    value_raw = projected[:, qwidth + HEAD_DIM :]
    root_query = inv_root(query)
    unit_query = query * root_query
    query_norm = unit_query * g_query
    root_key = inv_root(key_raw)
    unit_key = key_raw * root_key
    key_norm = unit_key * g_key
    query_rot = query_norm * cos_t[:, None, :] + turn_half(query_norm) * sin_t[:, None, :]
    key_rot = key_norm * cos_t + turn_half(key_norm) * sin_t
    query_b = query_rot.astype(jnp.bfloat16)
    kv_own = jnp.concatenate([key_rot.astype(jnp.bfloat16), value_raw.astype(jnp.bfloat16)], axis=1)
    earlier = []
    for hop in range(hops, 0, -1):
        earlier.append(passed_along(kv_own, "seq", hop))
    kv_all = jnp.concatenate(earlier + [kv_own], axis=0)
    keys_b = kv_all[:, :HEAD_DIM]
    values_b = kv_all[:, HEAD_DIM:]
    scores = jnp.einsum("rhd,kd->rhk", query_b, keys_b, preferred_element_type=jnp.float32) * scale
    logsum = jnp.log(jnp.sum(jnp.where(full_mask, jnp.exp(scores), 0.0), axis=-1))
    probs = jnp.where(full_mask, jnp.exp(scores - logsum[..., None]), 0.0)
    probs_b = probs.astype(jnp.bfloat16)
    mixed = jnp.einsum("rhk,kd->rhd", probs_b, values_b, preferred_element_type=jnp.float32)
    mixed_b = mixed.reshape(rows, qwidth).astype(jnp.bfloat16)
    attn_out = dot32(mixed_b, out_full)
    root_post = inv_root(attn_out)
    unit_post = attn_out * root_post
    hidden_in = rows_in + unit_post * g_attn_out
    root_ffn = inv_root(hidden_in)
    unit_ffn = hidden_in * root_ffn
    ffn_input = (unit_ffn * g_ffn_in).astype(jnp.bfloat16)
    tokens_b = lax.all_gather(ffn_input, "seq", axis=0, tiled=True)
    out_part, gate_all, up_all = ffn_forward_fold(
        tokens_b,
        (
            lax.all_gather(w_gate, "dp", axis=0, tiled=True),
            lax.all_gather(w_up, "dp", axis=0, tiled=True),
            lax.all_gather(w_down, "dp", axis=0, tiled=True),
        ),
    )
    ffn_out = lax.psum_scatter(out_part, "seq", scatter_dimension=0, tiled=True)
    root_out = inv_root(ffn_out)
    unit_out = ffn_out * root_out
    result = hidden_in + unit_out * g_ffn_out
    grad_g_ffn_out = jnp.sum(rows_grad * unit_out, axis=0)
    ffn_grad_b = norm_back(rows_grad, unit_out, root_out, g_ffn_out).astype(jnp.bfloat16)
    grads_b = lax.all_gather(ffn_grad_b, "seq", axis=0, tiled=True)
    in_part, dgate_all, dup_all = ffn_backward_fold(
        grads_b,
        gate_all,
        up_all,
        (
            lax.all_gather(w_gate, "dp", axis=0, tiled=True),
            lax.all_gather(w_up, "dp", axis=0, tiled=True),
            lax.all_gather(w_down, "dp", axis=0, tiled=True),
        ),
    )
    ffn_in_grad = lax.psum_scatter(in_part, "seq", scatter_dimension=0, tiled=True)
    ffn_terms = lax.psum_scatter(
        ffn_weight_terms(tokens_b, grads_b, gate_all, up_all, dgate_all, dup_all).astype(
            jnp.bfloat16
        ),
        "dp",
        scatter_dimension=0,
        tiled=True,
    ).astype(jnp.float32)
    grad_w_gate = ffn_terms[:, :width]
    grad_w_up = ffn_terms[:, width : 2 * width]
    grad_w_down = ffn_terms[:, 2 * width :]
    grad_g_ffn_in = jnp.sum(ffn_in_grad * unit_ffn, axis=0)
    hidden_grad_in = rows_grad + norm_back(ffn_in_grad, unit_ffn, root_ffn, g_ffn_in)
    grad_g_attn_out = jnp.sum(hidden_grad_in * unit_post, axis=0)
    attn_grad_b = norm_back(hidden_grad_in, unit_post, root_post, g_attn_out).astype(jnp.bfloat16)
    mixed_grad_b = contract_cols(attn_grad_b, out_full).astype(jnp.bfloat16)
    mixed_grad3 = mixed_grad_b.reshape(rows, HEADS, HEAD_DIM)
    delta = jnp.sum(
        mixed_grad3.astype(jnp.float32)
        * mixed_b.reshape(rows, HEADS, HEAD_DIM).astype(jnp.float32),
        axis=-1,
    )
    scores_again = (
        jnp.einsum("rhd,kd->rhk", query_b, keys_b, preferred_element_type=jnp.float32) * scale
    )
    probs_again = jnp.where(full_mask, jnp.exp(scores_again - logsum[..., None]), 0.0)
    probs_again_b = probs_again.astype(jnp.bfloat16)
    value_grad_all = jnp.einsum(
        "rhk,rhd->kd", probs_again_b, mixed_grad3, preferred_element_type=jnp.float32
    )
    prob_grad = jnp.einsum("rhd,kd->rhk", mixed_grad3, values_b, preferred_element_type=jnp.float32)
    score_grad_b = (probs_again * (prob_grad - delta[..., None])).astype(jnp.bfloat16)
    query_rot_grad = (
        jnp.einsum("rhk,kd->rhd", score_grad_b, keys_b, preferred_element_type=jnp.float32) * scale
    )
    key_grad_all = (
        jnp.einsum("rhk,rhd->kd", score_grad_b, query_b, preferred_element_type=jnp.float32) * scale
    )
    kv_grad_all = jnp.concatenate([key_grad_all, value_grad_all], axis=1)
    kv_grad = kv_grad_all[hops * rows :]
    for hop in range(1, hops + 1):
        block = kv_grad_all[(hops - hop) * rows : (hops - hop + 1) * rows]
        kv_grad = kv_grad + passed_along(block.astype(jnp.bfloat16), "seq", -hop).astype(
            block.dtype
        )
    key_rot_grad = kv_grad[:, :HEAD_DIM]
    value_grad = kv_grad[:, HEAD_DIM:]
    query_norm_grad = query_rot_grad * cos_t[:, None, :] - turn_half(
        query_rot_grad * sin_t[:, None, :]
    )
    key_norm_grad = key_rot_grad * cos_t - turn_half(key_rot_grad * sin_t)
    grad_g_query = jnp.sum(query_norm_grad * unit_query, axis=(0, 1))
    grad_g_key = jnp.sum(key_norm_grad * unit_key, axis=0)
    query_grad = norm_back(query_norm_grad, unit_query, root_query, g_query)
    key_grad = norm_back(key_norm_grad, unit_key, root_key, g_key)
    qkv_grad_b = jnp.concatenate(
        [query_grad.reshape(rows, qwidth), key_grad, value_grad], axis=1
    ).astype(jnp.bfloat16)
    attn_in_grad = contract_cols(qkv_grad_b, qkv_full)
    grad_g_attn_in = jnp.sum(attn_in_grad * unit_attn, axis=0)
    input_grad = hidden_grad_in + norm_back(attn_in_grad, unit_attn, root_attn, g_attn_in)
    gain_terms = jnp.stack([grad_g_attn_in, grad_g_attn_out, grad_g_ffn_in, grad_g_ffn_out])
    head_terms = jnp.stack([grad_g_query, grad_g_key])
    out_term = contract_rows(mixed_b, attn_grad_b)
    qkv_term = contract_rows(attn_input, qkv_grad_b)
    owned_qkv, owned_out, owned_gains, owned_heads = (
        lax.psum_scatter(qkv_term, ("seq", "dp"), scatter_dimension=0, tiled=True),
        lax.psum_scatter(out_term, ("seq", "dp"), scatter_dimension=0, tiled=True),
        lax.psum_scatter(gain_terms, ("seq", "dp"), scatter_dimension=1, tiled=True),
        lax.psum_scatter(head_terms, ("seq", "dp"), scatter_dimension=1, tiled=True),
    )
    return (
        result[None],
        input_grad[None],
        owned_qkv,
        owned_out,
        grad_w_gate,
        grad_w_up,
        grad_w_down,
        owned_gains[0],
        owned_heads[0],
        owned_heads[1],
        owned_gains[1],
        owned_gains[2],
        owned_gains[3],
    )


def solution(mesh):
    return jax.shard_map(
        local,
        mesh=mesh,
        in_specs=(
            P("dp", "seq", None),
            P("dp", "seq", None),
            P("dp", None),
            P(("seq", "dp"), None),
            P(("seq", "dp"), None),
            P(("seq", "dp"), None),
            P(("seq", "dp"), None),
            P(("seq", "dp"), None),
            P(),
            P(),
            P(),
            P(),
            P(),
            P(),
        ),
        out_specs=(
            P("dp", "seq", None),
            P("dp", "seq", None),
            P(("seq", "dp"), None),
            P(("seq", "dp"), None),
            P(("seq", "dp"), None),
            P(("seq", "dp"), None),
            P(("seq", "dp"), None),
            P(("seq", "dp")),
            P(("seq", "dp")),
            P(("seq", "dp")),
            P(("seq", "dp")),
            P(("seq", "dp")),
            P(("seq", "dp")),
        ),
        check_vma=False,
    )
```

profile of v0, /device:TPU:0, one launch (start us, length us, event | category | flops | bytes accessed | tf_op | source)
XLA Modules:
  0.0 682.8 jit_solution(9453058917675593302)
XLA Ops:
  13.7 60.8 %all-gather.21.cloned.1.call-done = bf16[32,36,1536]{2,1,0:T(8,128)(2,1)} async-done(((bf16[1,36,1536]{2,1,0:T(8,128)(2,1)}), bf16[32,36,1536]{2,1,0:T(8,128)(2,1)}) %all-gather.21.cloned.1.call-update) | async-done | bytes 3538960 | tf_op jit(solution)/shard_map/all_gather | solution.py:133
  74.5 3.9 reshape.292
  85.0 4.7 collective-permute-start.1
  89.7 1.9 collective-permute-start.2
  91.7 2.5 collective-permute-start.3
  95.1 2.1 reshape.288
  108.6 3.3 convolution_convert_fusion.4
  113.6 23.6 %all-gather.9.cloned.1.call-done = bf16[1024,1152]{1,0:T(8,128)(2,1)} async-done(((bf16[32,1152]{1,0:T(8,128)(2,1)}), bf16[1024,1152]{1,0:T(8,128)(2,1)}) %all-gather.9.cloned.1.call-update) | async-done | bytes 2359312 | tf_op jit(solution)/shard_map/all_gather | solution.py:134
  137.3 2.4 multiply_reduce_fusion.9
  144.2 29.6 %all-gather.13.cloned.1.call-done = bf16[1728,1152]{1,0:T(8,128)(2,1)} async-done(((bf16[216,1152]{1,0:T(8,128)(2,1)}), bf16[1728,1152]{1,0:T(8,128)(2,1)}) %all-gather.13.cloned.1.call-update) | async-done | bytes 3981328 | tf_op jit(solution)/shard_map/all_gather | solution.py:190
  173.7 32.3 %all-gather.11.cloned.1.call-done = bf16[512,1152]{1,0:T(8,128)(2,1)} async-done(((bf16[128,1152]{1,0:T(8,128)(2,1)}), bf16[512,1152]{1,0:T(8,128)(2,1)}) %all-gather.11.cloned.1.call-update) | async-done | bytes 1179664 | tf_op jit(solution)/shard_map/all_gather | solution.py:186
  206.0 6.8 fusion.51
  212.8 29.9 %all-gather.15.cloned.1.call-done = bf16[1728,1152]{1,0:T(8,128)(2,1)} async-done(((bf16[216,1152]{1,0:T(8,128)(2,1)}), bf16[1728,1152]{1,0:T(8,128)(2,1)}) %all-gather.15.cloned.1.call-update) | async-done | bytes 3981328 | tf_op jit(solution)/shard_map/all_gather | solution.py:191
  242.7 9.3 %multiply_convert_fusion.1 = (bf16[512,1728]{0,1:T(8,128)(2,1)}, f32[512,1728]{0,1:T(8,128)}) fusion(f32[512,1728]{0,1:T(8,128)} %fusion.51, bf16[512,1152]{1,0:T(8,128)(2,1)} %all-gather.11.cloned.1.call-done, bf16[1728,1152]{1,0:T(8,128)(2,1)} %all-gather.15.cloned.1.call-done), kind=kOutput, calls=%fused_computation.15 | convolution fusion | flops 2047279104 | bytes 14008320 | tf_op jit(solution)/shard_map/dot_general | solution.py:69
  252.0 28.2 %all-gather.17.cloned.1.call-done = bf16[1728,1152]{1,0:T(8,128)(2,1)} async-done(((bf16[216,1152]{1,0:T(8,128)(2,1)}), bf16[1728,1152]{1,0:T(8,128)(2,1)}) %all-gather.17.cloned.1.call-update) | async-done | bytes 3981328 | tf_op jit(solution)/shard_map/all_gather | solution.py:192
  280.2 6.7 fusion.52
  286.9 47.8 %reduce-scatter.11.cloned.1.call-done = f32[128,1152]{1,0:T(8,128)} async-done(((f32[512,1152]{1,0:T(8,128)}), f32[128,1152]{1,0:T(8,128)}) %reduce-scatter.11.cloned.1.call-update) | async-done | bytes 589840 | tf_op jit(solution)/shard_map/reduce_scatter | solution.py:195
  335.9 2.1 fusion.20
  338.0 2.5 multiply_convert_fusion.3
  340.8 29.6 %all-gather.19.cloned.1.call-done = bf16[512,1152]{1,0:T(8,128)(2,1)} async-done(((bf16[128,1152]{1,0:T(8,128)(2,1)}), bf16[512,1152]{1,0:T(8,128)(2,1)}) %all-gather.19.cloned.1.call-update) | async-done | bytes 1179664 | tf_op jit(solution)/shard_map/all_gather | solution.py:201
  370.4 9.5 %multiply_convert_fusion = (bf16[512,1728]{0,1:T(8,128)(2,1)S(1)}, bf16[512,1728]{0,1:T(8,128)(2,1)S(1)}) fusion(f32[512,1728]{0,1:T(8,128)} %fusion.51, f32[512,1728]{0,1:T(8,128)} %get-tuple-element.66, bf16[512,1152]{1,0:T(8,128)(2,1)} %all-gather.19.cloned.1.call-done, bf16[1728,1152]{1,0:T(8,128)(2,1)} %all-gather.17.cloned.1.call-done), kind=kOutput, calls=%fused_computation.14 | convolution fusion | flops 2058780672 | bytes 15777792 | tf_op jit(solution)/shard_map/dot_general | solution.py:69
  379.9 2.7 fusion.53
  383.3 4.1 convolution_add_fusion
  387.7 4.4 convolution_convert_fusion
  392.1 2.5 convolution_convert_fusion.1
  394.6 2.5 convolution_convert_fusion.2
  397.1 5.0 pad_maximum_fusion
  402.1 3.5 fusion.13
  406.2 28.3 %reduce-scatter.13.cloned.1.call-done = f32[128,1152]{1,0:T(8,128)} async-done(((f32[512,1152]{1,0:T(8,128)}), f32[128,1152]{1,0:T(8,128)}) %reduce-scatter.13.cloned.1.call-update) | async-done | bytes 589840 | tf_op jit(solution)/shard_map/reduce_scatter | solution.py:212
  434.5 2.2 multiply_reduce_fusion
  436.7 2.8 multiply_reduce_fusion.1
  447.8 4.0 convolution_bitcast_fusion
  451.8 2.4 fusion.14
  462.7 3.2 fusion.54
  468.7 4.8 collective-permute-done.5
  486.1 2.1 multiply_convert_fusion.6
  490.0 5.3 fusion.34
  495.2 103.3 %fusion = f32[40,1536]{1,0:T(8,128)} fusion(f32[1152,1536]{1,0:T(8,128)} %fusion.34), kind=kCustom, calls=%all-reduce-scatter | all-reduce-scatter fusion | flops 1966081 | bytes 7323648
  600.0 4.2 collective-permute-start.10
  604.1 7.0 %collective-permute-start.9 = (f32[40,1536]{1,0:T(8,128)}, f32[40,1536]{1,0:T(8,128)}, u32[]{:S(2)}, u32[]{:S(2)}) collective-permute-start(f32[40,1536]{1,0:T(8,128)} %fusion), channel_id=1, source_target_pairs={{0,2},{1,3},{2,4},{3,5},{4,6},{5,7},{6,8},{7,9},{8,10},{9,11},{10,... | collective-permute-start | bytes 737288
  611.2 3.1 collective-permute-start.8
  614.2 2.9 collective-permute-start.11
  617.1 3.3 multiply_reduce_fusion.2
  620.5 39.1 %all-reduce.5 = (f32[4,1152]{1,0:T(4,128)S(1)}, f32[2,256]{1,0:T(2,128)S(1)}) all-reduce(f32[4,1152]{1,0:T(4,128)S(1)} %pad_maximum_fusion.7, f32[2,256]{1,0:T(2,128)S(1)} %pad_maximum_fusion.8), channel_id=7, replica_groups=mesh['seq'=4,'dp'=8] {'seq','dp'}, use_global_device_ids=true, to_apply=%region_26.27.clone | all-reduce | flops 5120 | bytes 40960
  660.3 2.4 add_bitcast_fusion
  663.3 4.1 concatenate.50
  668.1 3.0 fusion.49
  671.1 4.8 reduce-scatter.15.cloned.1.call-done
  (233 shorter events, 71.6 us)
Async XLA Ops:
  7.2 67.3 %all-gather.21.cloned.1.call-start = ((), (), s32[]{:S(2)}) async-start(), calls=%async_computation.13 | async-start | bytes 4055040 | tf_op jit(solution)/shard_map/all_gather | solution.py:133
  7.9 129.4 %all-gather.9.cloned.1.call-start = ((), (), s32[]{:S(2)}) async-start(), calls=%async_computation.4 | async-start | bytes 2433024 | tf_op jit(solution)/shard_map/all_gather | solution.py:134
  8.7 165.1 %all-gather.13.cloned.1.call-start = ((), (), s32[]{:S(2)}) async-start(), calls=%async_computation.6 | async-start | bytes 4478976 | tf_op jit(solution)/shard_map/all_gather | solution.py:190
  9.4 196.6 %all-gather.11.cloned.1.call-start = ((), (), s32[]{:S(2)}) async-start(), calls=%async_computation.5 | async-start | bytes 1474560 | tf_op jit(solution)/shard_map/all_gather | solution.py:186
  12.4 66.0 %copy-start.44 = (f32[128]{0:T(128)}, f32[128]{0:T(128)S(1)}, u32[]{:S(2)}) copy-start(f32[128]{0:T(128)S(1)} %add_rsqrt_fusion.5) | copy-start | bytes 1540
  13.7 64.7 %copy-start.30 = (f32[1152]{0:T(1024)S(1)}, f32[1152]{0:T(1024)}, u32[]{:S(2)}) copy-start(f32[1152]{0:T(1024)} %param.22) | copy-start | bytes 13828
  80.2 13.9 %copy-start.14 = (f32[128,1536]{1,0:T(8,128)}, f32[128,1536]{1,0:T(8,128)S(1)}, u32[]{:S(2)}) copy-start(f32[128,1536]{1,0:T(8,128)S(1)} %fusion.48) | copy-start | bytes 2359300
  80.2 19.7 %copy-start.42 = (f32[256]{0:T(256)S(1)}, f32[256]{0:T(256)}, u32[]{:S(2)}) copy-start(f32[256]{0:T(256)} %param.23) | copy-start | bytes 3076
  83.7 18.7 %collective-permute-start = (bf16[128,512]{1,0:T(8,128)(2,1)}, bf16[128,512]{1,0:T(8,128)(2,1)}, u32[]{:S(2)}, u32[]{:S(2)}) collective-permute-start(bf16[128,512]{1,0:T(8,128)(2,1)} %pad_maximum_fusion.6), channel_id=1, source_target_pairs={} | collective-permute-start | bytes 393224 | tf_op jit(solution)/shard_map/ppermute | solution.py:21
  85.0 18.4 %collective-permute-start.1 = (bf16[128,512]{1,0:T(8,128)(2,1)}, bf16[128,512]{1,0:T(8,128)(2,1)}, u32[]{:S(2)}, u32[]{:S(2)}) collective-permute-start(bf16[128,512]{1,0:T(8,128)(2,1)} %pad_maximum_fusion.6), channel_id=1, source_target_pairs={{0,24},{1,25},{2,26},{3,27},{4,28},{5,29},{6,30},{7,31}} | collective-permute-start | bytes 393224 | tf_op jit(solution)/shard_map/ppermute | solution.py:21
  89.7 14.6 %collective-permute-start.2 = (bf16[128,512]{1,0:T(8,128)(2,1)}, bf16[128,512]{1,0:T(8,128)(2,1)}, u32[]{:S(2)}, u32[]{:S(2)}) collective-permute-start(bf16[128,512]{1,0:T(8,128)(2,1)} %pad_maximum_fusion.6), channel_id=1, source_target_pairs={{0,16},{8,24},{1,17},{9,25},{2,18},{10,26},{3,19},{11,27},{4,20},{... | collective-permute-start | bytes 393224 | tf_op jit(solution)/shard_map/ppermute | solution.py:21
  91.7 13.6 %collective-permute-start.3 = (bf16[128,512]{1,0:T(8,128)(2,1)}, bf16[128,512]{1,0:T(8,128)(2,1)}, u32[]{:S(2)}, u32[]{:S(2)}) collective-permute-start(bf16[128,512]{1,0:T(8,128)(2,1)} %pad_maximum_fusion.6), channel_id=1, source_target_pairs={{0,8},{8,16},{16,24},{1,9},{9,17},{17,25},{2,10},{10,18},{18,26},{... | collective-permute-start | bytes 393224 | tf_op jit(solution)/shard_map/ppermute | solution.py:21
  99.9 6.3 copy-start.33
  99.9 6.3 copy-start.27
  100.0 6.3 copy-start.29
  142.4 100.3 %all-gather.15.cloned.1.call-start = ((), (), s32[]{:S(2)}) async-start(), calls=%async_computation.7 | async-start | bytes 4478976 | tf_op jit(solution)/shard_map/all_gather | solution.py:191
  143.0 137.2 %all-gather.17.cloned.1.call-start = ((), (), s32[]{:S(2)}) async-start(), calls=%async_computation.8 | async-start | bytes 4478976 | tf_op jit(solution)/shard_map/all_gather | solution.py:192
  143.6 191.1 %reduce-scatter.11.cloned.1.call-start = ((), (), s32[]{:S(2)}) async-start(), calls=%async_computation.9 | async-start | bytes 2949120 | tf_op jit(solution)/shard_map/reduce_scatter | solution.py:195
  286.9 83.5 %all-gather.19.cloned.1.call-start = ((), (), s32[]{:S(2)}) async-start(), calls=%async_computation.10 | async-start | bytes 1474560 | tf_op jit(solution)/shard_map/all_gather | solution.py:201
  340.6 93.9 %reduce-scatter.13.cloned.1.call-start = ((), (), s32[]{:S(2)}) async-start(), calls=%async_computation.11 | async-start | bytes 2949120 | tf_op jit(solution)/shard_map/reduce_scatter | solution.py:212
  370.4 9.5 %copy-start.54 = (bf16[1728,1152]{1,0:T(8,128)(2,1)S(1)}, bf16[1728,1152]{1,0:T(8,128)(2,1)}, u32[]{:S(2)}) copy-start(bf16[1728,1152]{1,0:T(8,128)(2,1)} %all-gather.13.cloned.1.call-done) | copy-start | bytes 11943940
  387.4 280.7 %reduce-scatter.17.cloned.1.call-start = ((), (), s32[]{:S(2)}) async-start(), calls=%async_computation.14 | async-start | bytes 13436928
  402.1 273.9 %reduce-scatter.15.cloned.1.call-start = ((), (), s32[]{:S(2)}) async-start(), calls=%async_computation.12 | async-start | bytes 4866048 | tf_op jit(solution)/shard_map/reduce_scatter | solution.py:280
  434.5 5.8 copy-start.6
  434.5 5.8 copy-start.32
  434.5 5.8 copy-start.49
  455.1 7.6 %copy-start.16 = (bf16[128,1152]{1,0:T(8,128)(2,1)S(1)}, bf16[128,1152]{1,0:T(8,128)(2,1)}, u32[]{:S(2)}) copy-start(bf16[128,1152]{1,0:T(8,128)(2,1)} %copy-done.15) | copy-start | bytes 884740
  455.1 7.6 %copy-start.18 = (bf16[128,4,256]{0,2,1:T(8,128)(2,1)S(1)}, bf16[128,4,256]{0,2,1:T(8,128)(2,1)}, u32[]{:S(2)}) copy-start(bf16[128,4,256]{0,2,1:T(8,128)(2,1)} %copy.84) | copy-start | bytes 786436
  457.2 10.6 %collective-permute-start.7 = (bf16[128,512]{1,0:T(8,128)(2,1)}, bf16[128,512]{1,0:T(8,128)(2,1)}, u32[]{:S(2)}, u32[]{:S(2)}) collective-permute-start(bf16[128,512]{1,0:T(8,128)(2,1)} %get-tuple-element.38), channel_id=1, source_target_pairs={} | collective-permute-start | bytes 393224 | tf_op jit(solution)/shard_map/ppermute | solution.py:21
  458.5 10.2 %collective-permute-start.6 = (bf16[128,512]{1,0:T(8,128)(2,1)}, bf16[128,512]{1,0:T(8,128)(2,1)}, u32[]{:S(2)}, u32[]{:S(2)}) collective-permute-start(bf16[128,512]{1,0:T(8,128)(2,1)} %get-tuple-element.39), channel_id=1, source_target_pairs={{24,0},{25,1},{26,2},{27,3},{28,4},{29,5},{30,6},{31,7}} | collective-permute-start | bytes 393224 | tf_op jit(solution)/shard_map/ppermute | solution.py:21
  459.8 13.6 %collective-permute-start.5 = (bf16[128,512]{1,0:T(8,128)(2,1)}, bf16[128,512]{1,0:T(8,128)(2,1)}, u32[]{:S(2)}, u32[]{:S(2)}) collective-permute-start(bf16[128,512]{1,0:T(8,128)(2,1)} %get-tuple-element.40), channel_id=1, source_target_pairs={{16,0},{24,8},{17,1},{25,9},{18,2},{26,10},{19,3},{27,11},{20,4},{... | collective-permute-start | bytes 393224 | tf_op jit(solution)/shard_map/ppermute | solution.py:21
  461.1 12.3 %collective-permute-start.4 = (bf16[128,512]{1,0:T(8,128)(2,1)}, bf16[128,512]{1,0:T(8,128)(2,1)}, u32[]{:S(2)}, u32[]{:S(2)}) collective-permute-start(bf16[128,512]{1,0:T(8,128)(2,1)} %get-tuple-element.37), channel_id=1, source_target_pairs={{8,0},{16,8},{24,16},{9,1},{17,9},{25,17},{10,2},{18,10},{26,18},{... | collective-permute-start | bytes 393224 | tf_op jit(solution)/shard_map/ppermute | solution.py:21
  467.8 8.4 %copy-start.25 = (f32[128,128]{1,0:T(8,128)S(1)}, f32[128,128]{1,0:T(8,128)}, u32[]{:S(2)}) copy-start(f32[128,128]{1,0:T(8,128)} %copy-done.24) | copy-start | bytes 196612
  467.8 8.4 %copy-start.41 = (f32[256]{0:T(256)S(1)}, f32[256]{0:T(256)}, u32[]{:S(2)}) copy-start(f32[256]{0:T(256)} %param.24) | copy-start | bytes 3076
  467.8 8.4 %copy-start.47 = (f32[128]{0:T(128)S(1)}, f32[128]{0:T(128)}, u32[]{:S(2)}) copy-start(f32[128]{0:T(128)} %copy-done.46) | copy-start | bytes 1540
  467.9 10.2 %copy-start.9 = (bf16[128,4,640]{2,0,1:T(8,128)(2,1)S(1)}, bf16[128,4,640]{2,0,1:T(8,128)(2,1)}, u32[]{:S(2)}) copy-start(bf16[128,4,640]{2,0,1:T(8,128)(2,1)} %copy-done.8) | copy-start | bytes 1966084
  467.9 10.2 %copy-start.22 = (bf16[640,512]{1,0:T(8,128)(2,1)S(1)}, bf16[640,512]{1,0:T(8,128)(2,1)}, u32[]{:S(2)}) copy-start(bf16[640,512]{1,0:T(8,128)(2,1)} %copy-done.21) | copy-start | bytes 1966084
  495.2 121.9 %copy-start.45 = (f32[128]{0:T(128)S(1)}, f32[128]{0:T(128)}, u32[]{:S(2)}) copy-start(f32[128]{0:T(128)} %copy-done.44) | copy-start | bytes 1540
  600.0 20.5 %copy-start.51 = (f32[256]{0:T(256)S(1)}, f32[256]{0:T(256)}, u32[]{:S(2)}) copy-start(f32[256]{0:T(256)} %get-tuple-element.21) | copy-start | bytes 3076
  600.0 20.5 %copy-start.52 = (f32[256]{0:T(256)S(1)}, f32[256]{0:T(256)}, u32[]{:S(2)}) copy-start(f32[256]{0:T(256)} %get-tuple-element.23) | copy-start | bytes 3076
  600.0 20.5 %copy-start.37 = (f32[1,1152]{1,0:T(1,128)S(1)}, f32[1,1152]{1,0:T(1,128)}, u32[]{:S(2)}) copy-start(f32[1,1152]{1,0:T(1,128)} %stack.27) | copy-start | bytes 13828
  600.0 20.5 %copy-start.38 = (f32[1,1152]{1,0:T(1,128)S(1)}, f32[1,1152]{1,0:T(1,128)}, u32[]{:S(2)}) copy-start(f32[1,1152]{1,0:T(1,128)} %stack.26) | copy-start | bytes 13828
  600.0 20.5 %copy-start.39 = (f32[1,1152]{1,0:T(1,128)S(1)}, f32[1,1152]{1,0:T(1,128)}, u32[]{:S(2)}) copy-start(f32[1,1152]{1,0:T(1,128)} %stack.25) | copy-start | bytes 13828
  600.0 63.3 %collective-permute-start.10 = (f32[40,1536]{1,0:T(8,128)}, f32[40,1536]{1,0:T(8,128)}, u32[]{:S(2)}, u32[]{:S(2)}) collective-permute-start(f32[40,1536]{1,0:T(8,128)} %fusion), channel_id=1, source_target_pairs={{0,3},{1,4},{2,5},{3,6},{4,7},{5,8},{6,9},{7,10},{8,11},{9,12},{10... | collective-permute-start | bytes 737288
  604.1 59.2 %collective-permute-start.9 = (f32[40,1536]{1,0:T(8,128)}, f32[40,1536]{1,0:T(8,128)}, u32[]{:S(2)}, u32[]{:S(2)}) collective-permute-start(f32[40,1536]{1,0:T(8,128)} %fusion), channel_id=1, source_target_pairs={{0,2},{1,3},{2,4},{3,5},{4,6},{5,7},{6,8},{7,9},{8,10},{9,11},{10,... | collective-permute-start | bytes 737288
  611.2 52.1 %collective-permute-start.8 = (f32[40,1536]{1,0:T(8,128)}, f32[40,1536]{1,0:T(8,128)}, u32[]{:S(2)}, u32[]{:S(2)}) collective-permute-start(f32[40,1536]{1,0:T(8,128)} %fusion), channel_id=1, source_target_pairs={{0,1},{1,2},{2,3},{3,4},{4,5},{5,6},{6,7},{7,8},{8,9},{9,10},{10,1... | collective-permute-start | bytes 737288
  614.2 49.1 %collective-permute-start.11 = (f32[4,1536]{1,0:T(4,128)}, f32[4,1536]{1,0:T(4,128)}, u32[]{:S(2)}, u32[]{:S(2)}) collective-permute-start(f32[4,1536]{1,0:T(4,128)} %slice.146), channel_id=1, source_target_pairs={{0,4},{1,5},{2,6},{3,7},{4,8},{5,9},{6,10},{7,11},{8,12},{9,13},{1... | collective-permute-start | bytes 73736
  620.4 42.9 %copy-start.23 = (f32[40,1536]{1,0:T(8,128)S(1)}, f32[40,1536]{1,0:T(8,128)}, u32[]{:S(2)}) copy-start(f32[40,1536]{1,0:T(8,128)} %fusion) | copy-start | bytes 737284
  (33 other events, 89.9 us)
Sparse Core Ops, SparseCore 0:
  10.9 63.5 all-gather.20
  77.4 59.8 all-gather.8
  139.2 34.4 all-gather.12
  175.7 30.2 all-gather.10
  207.8 34.9 all-gather.14
  244.5 35.6 all-gather.16
  287.0 47.6 reduce-scatter.10
  340.7 29.6 all-gather.18
  387.5 46.9 reduce-scatter.12
  437.9 104.6 reduce-scatter.16
  548.7 127.2 reduce-scatter.14
where the time goes:
time: 689 us; the launch traced here: 683 us
  waiting for transfers between devices  324 us (47%)
  blocking collectives  142 us (21%)
  matrix products  77.8 us (11%)
  other arithmetic  46.2 us (7%)
  local copies, waits for them, and re-layouts  43.2 us (6%)
  starting transfers between devices  34.3 us (5%)
  between operations  15.1 us (2%)
    unnamed x2, blocking collectives  142 us
    all_gather x1, waiting for transfers between devices, local(): lax.all_gather(w_qkv, ('seq', 'dp'), axis=0, tiled=True)  60.8 us
    reduce_scatter x1, waiting for transfers between devices, local(): ffn_out = lax.psum_scatter(out_part, 'seq', scatter_dimension=0, tiled=True)  47.8 us
    all_gather x1, waiting for transfers between devices, local(): tokens_b = lax.all_gather(ffn_input, 'seq', axis=0, tiled=True)  32.3 us
    dot_general x5, matrix products, contract_cols(): lax.dot_general(left, right, (((1,), (1,)), ((), ())), preferred_element_...  30.4 us
    all_gather x1, waiting for transfers between devices, local(): lax.all_gather(w_up, 'dp', axis=0, tiled=True)  29.9 us
    all_gather x1, waiting for transfers between devices, local(): grads_b = lax.all_gather(ffn_grad_b, 'seq', axis=0, tiled=True)  29.6 us
    all_gather x1, waiting for transfers between devices, local(): lax.all_gather(w_gate, 'dp', axis=0, tiled=True)  29.6 us
  transfers between devices with their start and end apart: 23, of which 12 were waited for; matrix products, arithmetic and copies ran while one was open for 34% of the time, Pallas kernels for 0%

commit v1 on v0

--- a/solution.py
+++ b/solution.py
@@ -15,10 +15,67 @@
 GELU_CUBIC = 0.044715
 
 
-def passed_along(value, axis, by):
+def bits_of(count):
+    bits = []
+    bit = 1
+    while bit < count:
+        bits.append(bit)
+        bit *= 2
+    return bits
+
+
+def swapped(value, axis, bit):
     length = lax.axis_size(axis)
-    pairs = [(i, i + by) for i in range(length) if 0 <= i + by < length]
-    return lax.ppermute(value, axis, pairs)
+    return lax.ppermute(value, axis, [(i, i ^ bit) for i in range(length)])
+
+
+def mine_first(value, axis, bit, at):
+    return jnp.concatenate([value, swapped(value, axis, bit)], axis=at)
+
+
+def keep_half(value, axis, bit, at):
+    own = lax.slice_in_dim(value, 0, 1, axis=at)
+    other = lax.slice_in_dim(value, 1, 2, axis=at).astype(jnp.bfloat16)
+    return own.astype(jnp.float32) + swapped(other, axis, bit).astype(jnp.float32)
+
+
+def gather_xor(value, stages):
+    value = value.reshape((1,) * len(stages) + value.shape)
+    for axis, bit, at in stages:
+        value = mine_first(value, axis, bit, at)
+    return value
+
+
+def scatter_xor(value, stages):
+    for axis, bit, at in stages:
+        value = keep_half(value, axis, bit, at)
+    return value.reshape(value.shape[len(stages) :])
+
+
+def ordered_pair(value, axis, bit, at):
+    other = swapped(value, axis, bit)
+    high = (lax.axis_index(axis) & bit) != 0
+    return jnp.concatenate(
+        [jnp.where(high, other, value), jnp.where(high, value, other)], axis=at
+    )
+
+
+def gather_ordered(value, stages):
+    value = value.reshape((1,) * len(stages) + value.shape)
+    for axis, bit, at in stages:
+        value = ordered_pair(value, axis, bit, at)
+    return value
+
+
+def scatter_ordered(value, stages, dtype):
+    for axis, bit, at in stages:
+        high = (lax.axis_index(axis) & bit) != 0
+        low_half = lax.slice_in_dim(value, 0, 1, axis=at)
+        high_half = lax.slice_in_dim(value, 1, 2, axis=at)
+        own = jnp.where(high, high_half, low_half).astype(jnp.float32)
+        sent = jnp.where(high, low_half, high_half).astype(dtype)
+        value = own + swapped(sent, axis, bit).astype(jnp.float32)
+    return value.reshape(value.shape[len(stages) :])
 
 
 def inv_root(vector):
@@ -94,13 +151,10 @@
 def ffn_weight_terms(tokens_b, grad_b, gate_all, up_all, dgate_all, dup_all):
     gelu_value, gelu_slope = gelu_pair(gate_all)
     hidden = (gelu_value * up_all).astype(jnp.bfloat16)
-    return jnp.concatenate(
-        [
-            contract_rows(dgate_all, tokens_b),
-            contract_rows(dup_all, tokens_b),
-            contract_rows(hidden, grad_b),
-        ],
-        axis=1,
+    return (
+        contract_rows(dgate_all, tokens_b),
+        contract_rows(dup_all, tokens_b),
+        contract_rows(hidden, grad_b),
     )
 
 
@@ -126,22 +180,44 @@
     rows = rows_in.shape[0]
     width = rows_in.shape[1]
     qwidth = HEADS * HEAD_DIM
-    hops = (WINDOW + rows - 2) // rows
-    keys = (hops + 1) * rows
+    seq_count = lax.axis_size("seq")
+    chip_bits = [2 * bit for bit in bits_of(lax.axis_size("dp") // 2)]
+    seq_bits = bits_of(seq_count)
+    nseq, nchip = len(seq_bits), len(chip_bits)
+    seq_stages = [("seq", bit, nseq - 1 - k) for k, bit in enumerate(seq_bits)][::-1]
+    chip_stages = [("dp", bit, nseq + nchip - 1 - k) for k, bit in enumerate(chip_bits)]
+    core_stage = [("dp", 1, nseq + nchip)]
+    all_up = seq_stages + chip_stages + core_stage
+    all_down = seq_stages + chip_stages[::-1] + core_stage
+    kv_stages = seq_stages
+    token_stages = seq_stages + [("dp", 1, nseq)]
+    ffn_up = [("dp", bit, nchip - 1 - k) for k, bit in enumerate(chip_bits)]
+    ffn_down = ffn_up[::-1]
+    keys = seq_count * rows
+    cut = (width // 256) * 128 + (128 if width % 256 else 0)
     scale = 1.0 / math.sqrt(HEAD_DIM)
-    qkv_full, out_full = (
-        lax.all_gather(w_qkv, ("seq", "dp"), axis=0, tiled=True),
-        lax.all_gather(w_out, ("seq", "dp"), axis=0, tiled=True),
-    )
+    qkv_full = gather_ordered(w_qkv, all_up).reshape(-1, w_qkv.shape[1])
+    out_full = gather_ordered(w_out, all_down).reshape(-1, w_out.shape[1])
+    ffn_rows = jnp.stack([w_gate, w_up, w_down])
+    left_rows, right_rows, qkv_full, out_full = lax.optimization_barrier(
+        (ffn_rows[:, :, :cut], ffn_rows[:, :, cut:], qkv_full, out_full)
+    )
+    ffn_full = jnp.concatenate(
+        [gather_xor(left_rows, ffn_up), gather_xor(right_rows, ffn_down)], axis=-1
+    )
+    ffn_full = ffn_full.reshape((-1,) + ffn_rows.shape)
+    gate_full, up_full, down_full = (ffn_full[:, i].reshape(-1, width) for i in range(3))
     block_id = lax.axis_index("seq")
     starts = jnp.cumsum(lens) - lens
     own_index = block_id * rows + jnp.arange(rows, dtype=jnp.int32)
-    key_index = block_id * rows - hops * rows + jnp.arange(keys, dtype=jnp.int32)
+    key_index = (
+        (block_id ^ jnp.arange(seq_count, dtype=jnp.int32))[:, None] * rows
+        + jnp.arange(rows, dtype=jnp.int32)[None, :]
+    ).reshape(keys)
     own_begin = seq_begin(own_index, starts)
     key_begin = seq_begin(key_index, starts)
     mask = (
-        (key_index[None, :] >= 0)
-        & (key_begin[None, :] == own_begin[:, None])
+        (key_begin[None, :] == own_begin[:, None])
         & (key_index[None, :] <= own_index[:, None])
         & (own_index[:, None] - key_index[None, :] < WINDOW)
     )
@@ -164,10 +240,7 @@
     key_rot = key_norm * cos_t + turn_half(key_norm) * sin_t
     query_b = query_rot.astype(jnp.bfloat16)
     kv_own = jnp.concatenate([key_rot.astype(jnp.bfloat16), value_raw.astype(jnp.bfloat16)], axis=1)
-    earlier = []
-    for hop in range(hops, 0, -1):
-        earlier.append(passed_along(kv_own, "seq", hop))
-    kv_all = jnp.concatenate(earlier + [kv_own], axis=0)
+    kv_all = gather_xor(kv_own, kv_stages).reshape(keys, 2 * HEAD_DIM)
     keys_b = kv_all[:, :HEAD_DIM]
     values_b = kv_all[:, HEAD_DIM:]
     scores = jnp.einsum("rhd,kd->rhk", query_b, keys_b, preferred_element_type=jnp.float32) * scale
@@ -183,44 +256,38 @@
     root_ffn = inv_root(hidden_in)
     unit_ffn = hidden_in * root_ffn
     ffn_input = (unit_ffn * g_ffn_in).astype(jnp.bfloat16)
-    tokens_b = lax.all_gather(ffn_input, "seq", axis=0, tiled=True)
-    out_part, gate_all, up_all = ffn_forward_fold(
-        tokens_b,
-        (
-            lax.all_gather(w_gate, "dp", axis=0, tiled=True),
-            lax.all_gather(w_up, "dp", axis=0, tiled=True),
-            lax.all_gather(w_down, "dp", axis=0, tiled=True),
-        ),
-    )
-    ffn_out = lax.psum_scatter(out_part, "seq", scatter_dimension=0, tiled=True)
+    slots = (2,) * len(token_stages)
+    tokens_b = gather_xor(ffn_input, token_stages).reshape(-1, width)
+    out_part, gate_all, up_all = ffn_forward_fold(tokens_b, (gate_full, up_full, down_full))
+    ffn_out = scatter_xor(out_part.reshape(slots + (rows, width)), token_stages[::-1])
     root_out = inv_root(ffn_out)
     unit_out = ffn_out * root_out
     result = hidden_in + unit_out * g_ffn_out
     grad_g_ffn_out = jnp.sum(rows_grad * unit_out, axis=0)
     ffn_grad_b = norm_back(rows_grad, unit_out, root_out, g_ffn_out).astype(jnp.bfloat16)
-    grads_b = lax.all_gather(ffn_grad_b, "seq", axis=0, tiled=True)
+    grads_b = gather_xor(ffn_grad_b, token_stages).reshape(-1, width)
     in_part, dgate_all, dup_all = ffn_backward_fold(
-        grads_b,
-        gate_all,
-        up_all,
-        (
-            lax.all_gather(w_gate, "dp", axis=0, tiled=True),
-            lax.all_gather(w_up, "dp", axis=0, tiled=True),
-            lax.all_gather(w_down, "dp", axis=0, tiled=True),
-        ),
-    )
-    ffn_in_grad = lax.psum_scatter(in_part, "seq", scatter_dimension=0, tiled=True)
-    ffn_terms = lax.psum_scatter(
-        ffn_weight_terms(tokens_b, grads_b, gate_all, up_all, dgate_all, dup_all).astype(
-            jnp.bfloat16
-        ),
-        "dp",
-        scatter_dimension=0,
-        tiled=True,
-    ).astype(jnp.float32)
-    grad_w_gate = ffn_terms[:, :width]
-    grad_w_up = ffn_terms[:, width : 2 * width]
-    grad_w_down = ffn_terms[:, 2 * width :]
+        grads_b, gate_all, up_all, (gate_full, up_full, down_full)
+    )
+    ffn_in_grad = scatter_xor(in_part.reshape(slots + (rows, width)), token_stages[::-1])
+    terms = ffn_weight_terms(tokens_b, grads_b, gate_all, up_all, dgate_all, dup_all)
+    chips = (2,) * nchip
+    own_rows = w_gate.shape[0]
+
+    def term_part(first, last):
+        return jnp.stack(
+            [term[:, first:last].reshape(chips + (own_rows, last - first)) for term in terms],
+            axis=nchip,
+        )
+
+    ffn_terms = jnp.concatenate(
+        [
+            scatter_xor(term_part(0, cut), ffn_up),
+            scatter_xor(term_part(cut, width), ffn_down),
+        ],
+        axis=-1,
+    )
+    grad_w_gate, grad_w_up, grad_w_down = ffn_terms[0], ffn_terms[1], ffn_terms[2]
     grad_g_ffn_in = jnp.sum(ffn_in_grad * unit_ffn, axis=0)
     hidden_grad_in = rows_grad + norm_back(ffn_in_grad, unit_ffn, root_ffn, g_ffn_in)
     grad_g_attn_out = jnp.sum(hidden_grad_in * unit_post, axis=0)
@@ -249,12 +316,9 @@
         jnp.einsum("rhk,rhd->kd", score_grad_b, query_b, preferred_element_type=jnp.float32) * scale
     )
     kv_grad_all = jnp.concatenate([key_grad_all, value_grad_all], axis=1)
-    kv_grad = kv_grad_all[hops * rows :]
-    for hop in range(1, hops + 1):
-        block = kv_grad_all[(hops - hop) * rows : (hops - hop + 1) * rows]
-        kv_grad = kv_grad + passed_along(block.astype(jnp.bfloat16), "seq", -hop).astype(
-            block.dtype
-        )
+    kv_grad = scatter_xor(
+        kv_grad_all.reshape((2,) * nseq + (rows, 2 * HEAD_DIM)), kv_stages[::-1]
+    )
     key_rot_grad = kv_grad[:, :HEAD_DIM]
     value_grad = kv_grad[:, HEAD_DIM:]
     query_norm_grad = query_rot_grad * cos_t[:, None, :] - turn_half(
@@ -271,16 +335,24 @@
     attn_in_grad = contract_cols(qkv_grad_b, qkv_full)
     grad_g_attn_in = jnp.sum(attn_in_grad * unit_attn, axis=0)
     input_grad = hidden_grad_in + norm_back(attn_in_grad, unit_attn, root_attn, g_attn_in)
-    gain_terms = jnp.stack([grad_g_attn_in, grad_g_attn_out, grad_g_ffn_in, grad_g_ffn_out])
-    head_terms = jnp.stack([grad_g_query, grad_g_key])
+    spread = (2,) * (nseq + nchip + 1)
+    count = seq_count * lax.axis_size("dp")
+    gains = [grad_g_attn_in, grad_g_attn_out, grad_g_ffn_in, grad_g_ffn_out, grad_g_query, grad_g_key]
+    gain_terms = jnp.concatenate([g.reshape(count, -1) for g in gains], axis=1)
     out_term = contract_rows(mixed_b, attn_grad_b)
     qkv_term = contract_rows(attn_input, qkv_grad_b)
-    owned_qkv, owned_out, owned_gains, owned_heads = (
-        lax.psum_scatter(qkv_term, ("seq", "dp"), scatter_dimension=0, tiled=True),
-        lax.psum_scatter(out_term, ("seq", "dp"), scatter_dimension=0, tiled=True),
-        lax.psum_scatter(gain_terms, ("seq", "dp"), scatter_dimension=1, tiled=True),
-        lax.psum_scatter(head_terms, ("seq", "dp"), scatter_dimension=1, tiled=True),
-    )
+    owned_qkv = scatter_ordered(
+        qkv_term.reshape(spread + w_qkv.shape), all_up[::-1], jnp.bfloat16
+    )
+    owned_out = scatter_ordered(
+        out_term.reshape(spread + w_out.shape), all_down[::-1], jnp.bfloat16
+    )
+    owned = scatter_ordered(gain_terms.reshape(spread + (-1,)), all_up[::-1], jnp.float32)
+    own_width, own_head = width // count, HEAD_DIM // count
+    owned_gains = [owned[i * own_width : (i + 1) * own_width] for i in range(4)]
+    owned_heads = [
+        owned[4 * own_width + i * own_head : 4 * own_width + (i + 1) * own_head] for i in range(2)
+    ]
     return (
         result[None],
         input_grad[None],

time: 689 us -> 563 us (0.82)
  blocking collectives: 142 us -> 0 us
  other arithmetic: 46.2 us -> 102 us
  waiting for transfers between devices: 324 us -> 279 us
  matrix products: 77.8 us -> 54.4 us
  local copies, waits for them, and re-layouts: 43.2 us -> 65.9 us
  starting transfers between devices: 34.3 us -> 52.6 us
  between operations: 15.1 us -> 2.8 us
    ppermute x8 -> x49, waiting for transfers between devices: 5.59 us -> 279 us  [swapped(): return lax.ppermute(value, axis, [(i, i ^ bit) for i in range(length)])]
    all_gather x7 -> x0, waiting for transfers between devices: 234 us -> none  [the longest x1 60.8 us: local(): lax.all_gather(w_qkv, ('seq', 'dp'), axis=0, tiled=True)]
    unnamed x2 -> x0, blocking collectives: 142 us -> none
    reduce_scatter x3 -> x0, waiting for transfers between devices: 81 us -> none  [the longest x1 47.8 us: local(): ffn_out = lax.psum_scatter(out_part, 'seq', scatter_dimension=0, tiled=True)]
    ppermute x8 -> x49, starting transfers between devices: 15.9 us -> 52.6 us  [swapped(): return lax.ppermute(value, axis, [(i, i ^ bit) for i in range(length)])]
    add x2 -> x22, other arithmetic: 1.33 us -> 18.8 us  [the longest x14 12.5 us: scatter_ordered(): value = own + swapped(sent, axis, bit).astype(jnp.float32)]
    unnamed x5 -> x0, starting transfers between devices: 17.4 us -> none
    select_n x0 -> x15, other arithmetic: none -> 14.6 us  [the longest x10 14.5 us: ordered_pair(): jnp.where(high, other, value)]
  transfers between devices with their start and end apart: 23 -> 49, of which waited for: 12 -> 34; matrix products, arithmetic and copies ran while one was open for 34% -> 22% of each run, Pallas kernels for 0% -> 0%
where the time goes in v1:
time: 563 us; the launch traced here: 557 us
  waiting for transfers between devices  279 us (50%)
  other arithmetic  102 us (18%)
  local copies, waits for them, and re-layouts  65.9 us (12%)
  matrix products  54.4 us (10%)
  starting transfers between devices  52.6 us (9%)
    ppermute x49, waiting for transfers between devices, swapped(): return lax.ppermute(value, axis, [(i, i ^ bit) for i in range(length)])  279 us
    ppermute x49, starting transfers between devices, swapped(): return lax.ppermute(value, axis, [(i, i ^ bit) for i in range(length)])  52.6 us
    dot_general x5, matrix products, contract_cols(): lax.dot_general(left, right, (((1,), (1,)), ((), ())), preferred_element_...  16.9 us
    concatenate x10, other arithmetic, ordered_pair(): jnp.concatenate([jnp.where(high, other, value), jnp.where(high, value, ot...  16.1 us
    dot_general x5, matrix products, dot32(): return jnp.dot(left, right, preferred_element_type=jnp.float32)  15.3 us
    select_n x10, other arithmetic, ordered_pair(): jnp.where(high, other, value)  14.5 us
    unnamed x187, local copies, waits for them, and re-layouts  13.4 us
    add x14, other arithmetic, scatter_ordered(): value = own + swapped(sent, axis, bit).astype(jnp.float32)  12.5 us
  transfers between devices with their start and end apart: 49, of which 34 were waited for; matrix products, arithmetic and copies ran while one was open for 22% of the time, Pallas kernels for 0%

profile of v1, /device:TPU:0, one launch (start us, length us, event | category | flops | bytes accessed | tf_op | source)
XLA Modules:
  0.0 557.0 jit_solution(17403370766907427356)
XLA Ops:
  0.7 4.1 collective-permute-start.5
  10.1 4.7 collective-permute-start.6
  14.8 3.8 collective-permute-done
  23.5 7.6 %collective-permute-done.1 = bf16[2,1,1,1,1,36,1536]{6,3,5,4,2,1,0:T(2,128)(2,1)S(1)} collective-permute-done((bf16[2,1,1,1,1,36,1536]{6,3,5,4,2,1,0:T(2,128)(2,1)S(1)}, bf16[2,1,1,1,1,36,1536]{6,3,5,4,2,1,0:T(2,128)(2,1)S(1)}, u32[]{:S(2)}, u32[]{:S(2)}) %collective-permute-start.1) | collective-permute-done | bytes 221216 | tf_op jit(solution)/shard_map/ppermute | solution.py:29
  36.6 10.8 %collective-permute-done.2 = bf16[2,2,1,1,1,36,1536]{6,1,5,4,3,2,0:T(2,128)(2,1)S(1)} collective-permute-done((bf16[2,2,1,1,1,36,1536]{6,1,5,4,3,2,0:T(2,128)(2,1)S(1)}, bf16[2,2,1,1,1,36,1536]{6,1,5,4,3,2,0:T(2,128)(2,1)S(1)}, u32[]{:S(2)}, u32[]{:S(2)}) %collective-permute-start.2) | collective-permute-done | bytes 442400 | tf_op jit(solution)/shard_map/ppermute | solution.py:29
  54.3 3.1 collective-permute-done.8
  58.8 9.6 %collective-permute-done.3 = bf16[2,2,1,2,1,36,1536]{6,3,5,4,2,1,0:T(2,128)(2,1)S(1)} collective-permute-done((bf16[2,2,1,2,1,36,1536]{6,3,5,4,2,1,0:T(2,128)(2,1)S(1)}, bf16[2,2,1,2,1,36,1536]{6,3,5,4,2,1,0:T(2,128)(2,1)S(1)}, u32[]{:S(2)}, u32[]{:S(2)}) %collective-permute-start.3) | collective-permute-done | bytes 884768 | tf_op jit(solution)/shard_map/ppermute | solution.py:29
  68.4 2.9 broadcast_select_fusion.7
  71.3 3.8 pad_maximum_fusion.6
  83.7 5.6 %broadcast_select_fusion.1 = (bf16[2,2,2,2,1,36,1536]{6,3,5,4,2,1,0:T(2,128)(2,1)S(1)}, bf16[2,2,2,2,1,36,1536]{6,3,5,4,2,1,0:T(2,128)(2,1)S(1)}) fusion(bf16[2,2,2,2,1,36,1536]{6,3,5,4,2,1,0:T(2,128)(2,1)} %collective-permute-done.4, pred[]{:T(512)S(6)} %ne.10, bf16[2,2,1,2,1,36,1536]{6,3,5,4,2,1,0:T(2,128)(2,1)S(1)} %get-tuple-element.53, ...), kind=kLoop, calls=%fused_computation.22 | loop fusion | flops 2654208 | bytes 7077889 | tf_op jit(solution)/shard_map/jit(_where)/select_n | solution.py:59
  89.3 5.0 pad_maximum_fusion.2
  97.2 3.9 reshape.445
  114.7 4.7 collective-permute-start.10
  120.6 5.8 %collective-permute-done.10 = bf16[1,1,128,512]{3,2,1,0:T(8,128)(2,1)S(1)} collective-permute-done((bf16[1,1,128,512]{3,2,1,0:T(8,128)(2,1)S(1)}, bf16[1,1,128,512]{3,2,1,0:T(8,128)(2,1)S(1)}, u32[]{:S(2)}, u32[]{:S(2)}) %collective-permute-start.10) | collective-permute-done | bytes 131104 | tf_op jit(solution)/shard_map/ppermute | solution.py:29
  127.2 7.5 %collective-permute-done.11 = bf16[2,1,128,512]{3,2,1,0:T(8,128)(2,1)S(1)} collective-permute-done((bf16[2,1,128,512]{3,2,1,0:T(8,128)(2,1)S(1)}, bf16[2,1,128,512]{3,2,1,0:T(8,128)(2,1)S(1)}, u32[]{:S(2)}, u32[]{:S(2)}) %collective-permute-start.11) | collective-permute-done | bytes 262176 | tf_op jit(solution)/shard_map/ppermute | solution.py:29
  136.8 2.9 convolution_convert_fusion.1
  148.6 11.9 %collective-permute-done.12 = bf16[1,1,1,128,1152]{4,3,2,1,0:T(8,128)(2,1)S(1)} collective-permute-done((bf16[1,1,1,128,1152]{4,3,2,1,0:T(8,128)(2,1)S(1)}, bf16[1,1,1,128,1152]{4,3,2,1,0:T(8,128)(2,1)S(1)}, u32[]{:S(2)}, u32[]{:S(2)}) %collective-permute-start.12) | collective-permute-done | bytes 294944 | tf_op jit(solution)/shard_map/ppermute | solution.py:29
  162.2 4.3 collective-permute-done.15
  168.1 7.6 %collective-permute-done.13 = bf16[2,1,1,128,1152]{4,3,2,1,0:T(8,128)(2,1)S(1)} collective-permute-done((bf16[2,1,1,128,1152]{4,3,2,1,0:T(8,128)(2,1)S(1)}, bf16[2,1,1,128,1152]{4,3,2,1,0:T(8,128)(2,1)S(1)}, u32[]{:S(2)}, u32[]{:S(2)}) %collective-permute-start.13) | collective-permute-done | bytes 589856 | tf_op jit(solution)/shard_map/ppermute | solution.py:29
  180.5 27.2 %collective-permute-done.18 = bf16[2,1,3,216,512]{4,3,2,1,0:T(8,128)(2,1)S(1)} collective-permute-done((bf16[2,1,3,216,512]{4,3,2,1,0:T(8,128)(2,1)S(1)}, bf16[2,1,3,216,512]{4,3,2,1,0:T(8,128)(2,1)S(1)}, u32[]{:S(2)}, u32[]{:S(2)}) %collective-permute-start.18) | collective-permute-done | bytes 1327136 | tf_op jit(solution)/shard_map/ppermute | solution.py:29
  207.7 5.3 collective-permute-done.16
  217.9 5.4 multiply_convert_fusion.1
  223.3 5.3 dot_general.80
  228.7 5.0 fusion.8
  233.9 2.8 collective-permute-done.19
  238.7 13.7 %collective-permute-done.20 = bf16[2,1,1,128,1152]{4,3,2,1,0:T(8,128)(2,1)S(1)} collective-permute-done((bf16[2,1,1,128,1152]{4,3,2,1,0:T(8,128)(2,1)S(1)}, bf16[2,1,1,128,1152]{4,3,2,1,0:T(8,128)(2,1)S(1)}, u32[]{:S(2)}, u32[]{:S(2)}) %collective-permute-start.20) | collective-permute-done | bytes 589856 | tf_op jit(solution)/shard_map/ppermute | solution.py:29
  252.6 3.3 collective-permute-start.21
  256.0 12.8 %collective-permute-done.21 = bf16[1,1,1,128,1152]{4,3,2,1,0:T(8,128)(2,1)S(1)} collective-permute-done((bf16[1,1,1,128,1152]{4,3,2,1,0:T(8,128)(2,1)S(1)}, bf16[1,1,1,128,1152]{4,3,2,1,0:T(8,128)(2,1)S(1)}, u32[]{:S(2)}, u32[]{:S(2)}) %collective-permute-start.21) | collective-permute-done | bytes 294944 | tf_op jit(solution)/shard_map/ppermute | solution.py:29
  270.9 14.8 %collective-permute-done.22 = bf16[1,1,1,128,1152]{4,3,2,1,0:T(8,128)(2,1)S(1)} collective-permute-done((bf16[1,1,1,128,1152]{4,3,2,1,0:T(8,128)(2,1)S(1)}, bf16[1,1,1,128,1152]{4,3,2,1,0:T(8,128)(2,1)S(1)}, u32[]{:S(2)}, u32[]{:S(2)}) %collective-permute-start.22) | collective-permute-done | bytes 294944 | tf_op jit(solution)/shard_map/ppermute | solution.py:29
  285.9 15.2 %collective-permute-done.23 = bf16[2,1,1,128,1152]{4,3,2,1,0:T(8,128)(2,1)S(1)} collective-permute-done((bf16[2,1,1,128,1152]{4,3,2,1,0:T(8,128)(2,1)S(1)}, bf16[2,1,1,128,1152]{4,3,2,1,0:T(8,128)(2,1)S(1)}, u32[]{:S(2)}, u32[]{:S(2)}) %collective-permute-start.23) | collective-permute-done | bytes 589856 | tf_op jit(solution)/shard_map/ppermute | solution.py:29
  304.5 5.2 fusion.7
  309.7 3.0 fusion.78
  318.2 3.1 convolution_add_fusion
  347.5 16.4 %collective-permute-done.42 = bf16[1,2,3,216,512]{4,3,2,1,0:T(8,128)(2,1)} collective-permute-done((bf16[1,2,3,216,512]{4,3,2,1,0:T(8,128)(2,1)}, bf16[1,2,3,216,512]{4,3,2,1,0:T(8,128)(2,1)}, u32[]{:S(2)}, u32[]{:S(2)}) %collective-permute-start.42) | collective-permute-done | bytes 1327136 | tf_op jit(solution)/shard_map/ppermute | solution.py:29
  367.3 12.7 %collective-permute-done.40 = bf16[2,1,3,216,640]{4,3,2,1,0:T(8,128)(2,1)} collective-permute-done((bf16[2,1,3,216,640]{4,3,2,1,0:T(8,128)(2,1)}, bf16[2,1,3,216,640]{4,3,2,1,0:T(8,128)(2,1)}, u32[]{:S(2)}, u32[]{:S(2)}) %collective-permute-start.40) | collective-permute-done | bytes 1658912 | tf_op jit(solution)/shard_map/ppermute | solution.py:29
  385.3 7.9 %collective-permute-done.43 = bf16[1,1,3,216,512]{4,3,2,1,0:T(8,128)(2,1)S(1)} collective-permute-done((bf16[1,1,3,216,512]{4,3,2,1,0:T(8,128)(2,1)S(1)}, bf16[1,1,3,216,512]{4,3,2,1,0:T(8,128)(2,1)S(1)}, u32[]{:S(2)}, u32[]{:S(2)}) %collective-permute-start.43) | collective-permute-done | bytes 663584 | tf_op jit(solution)/shard_map/ppermute | solution.py:29
  394.5 4.0 collective-permute-done.27
  407.0 3.1 convolution_bitcast_fusion
  421.0 6.3 %collective-permute-done.28 = bf16[2,1,128,512]{3,2,1,0:T(8,128)(2,1)S(1)} collective-permute-done((bf16[2,1,128,512]{3,2,1,0:T(8,128)(2,1)S(1)}, bf16[2,1,128,512]{3,2,1,0:T(8,128)(2,1)S(1)}, u32[]{:S(2)}, u32[]{:S(2)}) %collective-permute-start.28) | collective-permute-done | bytes 262176 | tf_op jit(solution)/shard_map/ppermute | solution.py:29
  433.0 4.4 collective-permute-done.29
  465.1 4.6 select_convert_fusion
  469.9 3.6 collective-permute-done.47
  484.9 9.9 %collective-permute-done.36 = bf16[2,2,2,1,1,32,1152]{6,5,4,3,2,1,0:T(8,128)(2,1)S(1)} collective-permute-done((bf16[2,2,2,1,1,32,1152]{6,5,4,3,2,1,0:T(8,128)(2,1)S(1)}, bf16[2,2,2,1,1,32,1152]{6,5,4,3,2,1,0:T(8,128)(2,1)S(1)}, u32[]{:S(2)}, u32[]{:S(2)}) %collective-permute-start.36) | collective-permute-done | bytes 589856 | tf_op jit(solution)/shard_map/ppermute | solution.py:29
  496.7 5.7 %convert_add_fusion = f32[2,2,2,2,1,36,1536]{6,3,5,4,2,1,0:T(2,128)S(1)} fusion(bf16[2,2,2,2,1,36,1536]{6,3,5,4,2,1,0:T(2,128)(2,1)S(1)} %collective-permute-done.30, pred[]{:T(512)S(6)} %ne.10, f32[2,2,2,2,1,36,1536]{6,5,4,3,2,1,0:T(8,128)S(1)} %get-tuple-element.39, f32[2,2,2,2,1,36,1536]{6,5,4,3,2,1,0:T(8,128)S(1)} %get-tuple-element.38), kind=kLoop, calls=%fused_computation.17 | loop fusion | flops 2654208 | bytes 12386305 | tf_op jit(solution)/shard_map/add | solution.py:77
  505.9 16.1 %collective-permute-done.31 = bf16[2,2,1,2,1,36,1536]{6,3,5,4,2,1,0:T(2,128)(2,1)S(1)} collective-permute-done((bf16[2,2,1,2,1,36,1536]{6,3,5,4,2,1,0:T(2,128)(2,1)S(1)}, bf16[2,2,1,2,1,36,1536]{6,3,5,4,2,1,0:T(2,128)(2,1)S(1)}, u32[]{:S(2)}, u32[]{:S(2)}) %collective-permute-start.31) | collective-permute-done | bytes 884768 | tf_op jit(solution)/shard_map/ppermute | solution.py:29
  525.7 7.7 %collective-permute-done.32 = bf16[2,2,1,1,1,36,1536]{6,1,5,4,3,2,0:T(2,128)(2,1)S(1)} collective-permute-done((bf16[2,2,1,1,1,36,1536]{6,1,5,4,3,2,0:T(2,128)(2,1)S(1)}, bf16[2,2,1,1,1,36,1536]{6,1,5,4,3,2,0:T(2,128)(2,1)S(1)}, u32[]{:S(2)}, u32[]{:S(2)}) %collective-permute-start.32) | collective-permute-done | bytes 442400 | tf_op jit(solution)/shard_map/ppermute | solution.py:29
  537.7 8.0 %collective-permute-done.33 = bf16[2,1,1,1,1,36,1536]{6,3,5,4,2,1,0:T(2,128)(2,1)S(1)} collective-permute-done((bf16[2,1,1,1,1,36,1536]{6,3,5,4,2,1,0:T(2,128)(2,1)S(1)}, bf16[2,1,1,1,1,36,1536]{6,3,5,4,2,1,0:T(2,128)(2,1)S(1)}, u32[]{:S(2)}, u32[]{:S(2)}) %collective-permute-start.33) | collective-permute-done | bytes 221216 | tf_op jit(solution)/shard_map/ppermute | solution.py:29
  548.4 7.1 %collective-permute-done.34 = bf16[1,1,1,1,1,36,1536]{6,3,5,4,2,1,0:T(2,128)(2,1)S(1)} collective-permute-done((bf16[1,1,1,1,1,36,1536]{6,3,5,4,2,1,0:T(2,128)(2,1)S(1)}, bf16[1,1,1,1,1,36,1536]{6,3,5,4,2,1,0:T(2,128)(2,1)S(1)}, u32[]{:S(2)}, u32[]{:S(2)}) %collective-permute-start.34) | collective-permute-done | bytes 110624 | tf_op jit(solution)/shard_map/ppermute | solution.py:29
  (442 shorter events, 205.2 us)
Async XLA Ops:
  0.7 9.4 %collective-permute-start.5 = (bf16[1,1,1,1,1,32,1152]{6,5,4,3,2,1,0:T(8,128)(2,1)}, bf16[1,1,1,1,1,32,1152]{6,5,4,3,2,1,0:T(8,128)(2,1)S(1)}, u32[]{:S(2)}, u32[]{:S(2)}) collective-permute-start(bf16[1,1,1,1,1,32,1152]{6,5,4,3,2,1,0:T(8,128)(2,1)} %bitcast.281), channel_id=1, source_target_pairs={{0,16},{8,24},{16,0},{24,8},{1,17},{9,25},{17,1},{25,9},{2,18},{10... | collective-permute-start | bytes 221192 | tf_op jit(solution)/shard_map/ppermute | solution.py:29
  5.9 12.7 %collective-permute-start = (bf16[1,1,1,1,1,36,1536]{6,3,5,4,2,1,0:T(2,128)(2,1)S(1)}, bf16[1,1,1,1,1,36,1536]{6,3,5,4,2,1,0:T(2,128)(2,1)S(1)}, u32[]{:S(2)}, u32[]{:S(2)}) collective-permute-start(bf16[1,1,1,1,1,36,1536]{6,3,5,4,2,1,0:T(2,128)(2,1)S(1)} %copy.195), channel_id=1, source_target_pairs={{0,16},{8,24},{16,0},{24,8},{1,17},{9,25},{17,1},{25,9},{2,18},{10... | collective-permute-start | bytes 331784 | tf_op jit(solution)/shard_map/ppermute | solution.py:29
  10.1 11.6 %collective-permute-start.6 = (bf16[2,1,1,1,1,32,1152]{6,5,4,3,2,1,0:T(8,128)(2,1)S(1)}, bf16[2,1,1,1,1,32,1152]{6,5,4,3,2,1,0:T(8,128)(2,1)S(1)}, u32[]{:S(2)}, u32[]{:S(2)}) collective-permute-start(bf16[2,1,1,1,1,32,1152]{6,5,4,3,2,1,0:T(8,128)(2,1)S(1)} %pad_maximum_fusion.28), channel_id=1, source_target_pairs={{0,8},{8,0},{16,24},{24,16},{1,9},{9,1},{17,25},{25,17},{2,10},{10... | collective-permute-start | bytes 442376 | tf_op jit(solution)/shard_map/ppermute | solution.py:29
  19.8 11.3 %collective-permute-start.1 = (bf16[2,1,1,1,1,36,1536]{6,3,5,4,2,1,0:T(2,128)(2,1)S(1)}, bf16[2,1,1,1,1,36,1536]{6,3,5,4,2,1,0:T(2,128)(2,1)S(1)}, u32[]{:S(2)}, u32[]{:S(2)}) collective-permute-start(bf16[2,1,1,1,1,36,1536]{6,3,5,4,2,1,0:T(2,128)(2,1)S(1)} %pad_maximum_fusion.22), channel_id=1, source_target_pairs={{0,8},{8,0},{16,24},{24,16},{1,9},{9,1},{17,25},{25,17},{2,10},{10... | collective-permute-start | bytes 663560 | tf_op jit(solution)/shard_map/ppermute | solution.py:29
  21.8 14.1 %collective-permute-start.7 = (bf16[2,2,1,1,1,32,1152]{6,5,4,3,2,1,0:T(8,128)(2,1)S(1)}, bf16[2,2,1,1,1,32,1152]{6,5,4,3,2,1,0:T(8,128)(2,1)S(1)}, u32[]{:S(2)}, u32[]{:S(2)}) collective-permute-start(bf16[2,2,1,1,1,32,1152]{6,5,4,3,2,1,0:T(8,128)(2,1)S(1)} %pad_maximum_fusion.24), channel_id=1, source_target_pairs={{0,4},{1,5},{2,6},{3,7},{4,0},{5,1},{6,2},{7,3},{8,12},{9,13},{10,... | collective-permute-start | bytes 884744 | tf_op jit(solution)/shard_map/ppermute | solution.py:29
  34.3 13.1 %collective-permute-start.2 = (bf16[2,2,1,1,1,36,1536]{6,1,5,4,3,2,0:T(2,128)(2,1)S(1)}, bf16[2,2,1,1,1,36,1536]{6,1,5,4,3,2,0:T(2,128)(2,1)S(1)}, u32[]{:S(2)}, u32[]{:S(2)}) collective-permute-start(bf16[2,2,1,1,1,36,1536]{6,1,5,4,3,2,0:T(2,128)(2,1)S(1)} %copy.198), channel_id=1, source_target_pairs={{0,2},{1,3},{2,0},{3,1},{4,6},{5,7},{6,4},{7,5},{8,10},{9,11},{10,... | collective-permute-start | bytes 1327112 | tf_op jit(solution)/shard_map/ppermute | solution.py:29
  36.1 21.3 %collective-permute-start.8 = (bf16[2,2,2,1,1,32,1152]{6,5,4,3,2,1,0:T(8,128)(2,1)S(1)}, bf16[2,2,2,1,1,32,1152]{6,5,4,3,2,1,0:T(8,128)(2,1)S(1)}, u32[]{:S(2)}, u32[]{:S(2)}) collective-permute-start(bf16[2,2,2,1,1,32,1152]{6,5,4,3,2,1,0:T(8,128)(2,1)S(1)} %pad_maximum_fusion.18), channel_id=1, source_target_pairs={{0,2},{1,3},{2,0},{3,1},{4,6},{5,7},{6,4},{7,5},{8,10},{9,11},{10,... | collective-permute-start | bytes 1769480 | tf_op jit(solution)/shard_map/ppermute | solution.py:29
  51.9 16.5 %collective-permute-start.3 = (bf16[2,2,1,2,1,36,1536]{6,3,5,4,2,1,0:T(2,128)(2,1)S(1)}, bf16[2,2,1,2,1,36,1536]{6,3,5,4,2,1,0:T(2,128)(2,1)S(1)}, u32[]{:S(2)}, u32[]{:S(2)}) collective-permute-start(bf16[2,2,1,2,1,36,1536]{6,3,5,4,2,1,0:T(2,128)(2,1)S(1)} %pad_maximum_fusion.16), channel_id=1, source_target_pairs={{0,4},{1,5},{2,6},{3,7},{4,0},{5,1},{6,2},{7,3},{8,12},{9,13},{10,... | collective-permute-start | bytes 2654216 | tf_op jit(solution)/shard_map/ppermute | solution.py:29
  58.8 21.7 %collective-permute-start.9 = (bf16[2,2,2,2,1,32,1152]{6,5,4,3,2,1,0:T(8,128)(2,1)}, bf16[2,2,2,2,1,32,1152]{6,5,4,3,2,1,0:T(8,128)(2,1)}, u32[]{:S(2)}, u32[]{:S(2)}) collective-permute-start(bf16[2,2,2,2,1,32,1152]{6,5,4,3,2,1,0:T(8,128)(2,1)} %pad_maximum_fusion.10), channel_id=1, source_target_pairs={{0,1},{1,0},{2,3},{3,2},{4,5},{5,4},{6,7},{7,6},{8,9},{9,8},{10,11... | collective-permute-start | bytes 3538952 | tf_op jit(solution)/shard_map/ppermute | solution.py:29
  75.1 8.6 %collective-permute-start.4 = (bf16[2,2,2,2,1,36,1536]{6,3,5,4,2,1,0:T(2,128)(2,1)}, bf16[2,2,2,2,1,36,1536]{6,3,5,4,2,1,0:T(2,128)(2,1)}, u32[]{:S(2)}, u32[]{:S(2)}) collective-permute-start(bf16[2,2,2,2,1,36,1536]{6,3,5,4,2,1,0:T(2,128)(2,1)} %pad_maximum_fusion.6), channel_id=1, source_target_pairs={{0,1},{1,0},{2,3},{3,2},{4,5},{5,4},{6,7},{7,6},{8,9},{9,8},{10,11... | collective-permute-start | bytes 5308424 | tf_op jit(solution)/shard_map/ppermute | solution.py:29
  114.7 11.7 %collective-permute-start.10 = (bf16[1,1,128,512]{3,2,1,0:T(8,128)(2,1)S(1)}, bf16[1,1,128,512]{3,2,1,0:T(8,128)(2,1)S(1)}, u32[]{:S(2)}, u32[]{:S(2)}) collective-permute-start(bf16[1,1,128,512]{3,2,1,0:T(8,128)(2,1)S(1)} %maximum_bitcast_fusion), channel_id=1, source_target_pairs={{0,16},{8,24},{16,0},{24,8},{1,17},{9,25},{17,1},{25,9},{2,18},{10... | collective-permute-start | bytes 393224 | tf_op jit(solution)/shard_map/ppermute | solution.py:29
  126.4 8.2 %collective-permute-start.11 = (bf16[2,1,128,512]{3,2,1,0:T(8,128)(2,1)S(1)}, bf16[2,1,128,512]{3,2,1,0:T(8,128)(2,1)S(1)}, u32[]{:S(2)}, u32[]{:S(2)}) collective-permute-start(bf16[2,1,128,512]{3,2,1,0:T(8,128)(2,1)S(1)} %pad_maximum_fusion.25), channel_id=1, source_target_pairs={{0,8},{8,0},{16,24},{24,16},{1,9},{9,1},{17,25},{25,17},{2,10},{10... | collective-permute-start | bytes 786440 | tf_op jit(solution)/shard_map/ppermute | solution.py:29
  145.3 15.3 %collective-permute-start.12 = (bf16[1,1,1,128,1152]{4,3,2,1,0:T(8,128)(2,1)S(1)}, bf16[1,1,1,128,1152]{4,3,2,1,0:T(8,128)(2,1)S(1)}, u32[]{:S(2)}, u32[]{:S(2)}) collective-permute-start(bf16[1,1,1,128,1152]{4,3,2,1,0:T(8,128)(2,1)S(1)} %fusion.45), channel_id=1, source_target_pairs={{0,16},{8,24},{16,0},{24,8},{1,17},{9,25},{17,1},{25,9},{2,18},{10... | collective-permute-start | bytes 884744 | tf_op jit(solution)/shard_map/ppermute | solution.py:29
  147.2 19.2 %collective-permute-start.15 = (bf16[1,1,3,216,640]{4,3,2,1,0:T(8,128)(2,1)S(1)}, bf16[1,1,3,216,640]{4,3,2,1,0:T(8,128)(2,1)S(1)}, u32[]{:S(2)}, u32[]{:S(2)}) collective-permute-start(bf16[1,1,3,216,640]{4,3,2,1,0:T(8,128)(2,1)S(1)} %bitcast.241), channel_id=1, source_target_pairs={{0,2},{1,3},{2,0},{3,1},{4,6},{5,7},{6,4},{7,5},{8,10},{9,11},{10,... | collective-permute-start | bytes 2488328 | tf_op jit(solution)/shard_map/ppermute | solution.py:29
  160.6 15.1 %collective-permute-start.13 = (bf16[2,1,1,128,1152]{4,3,2,1,0:T(8,128)(2,1)S(1)}, bf16[2,1,1,128,1152]{4,3,2,1,0:T(8,128)(2,1)S(1)}, u32[]{:S(2)}, u32[]{:S(2)}) collective-permute-start(bf16[2,1,1,128,1152]{4,3,2,1,0:T(8,128)(2,1)S(1)} %pad_maximum_fusion.19), channel_id=1, source_target_pairs={{0,8},{8,0},{16,24},{24,16},{1,9},{9,1},{17,25},{25,17},{2,10},{10... | collective-permute-start | bytes 1769480 | tf_op jit(solution)/shard_map/ppermute | solution.py:29
  160.7 17.8 %collective-permute-start.17 = (bf16[1,1,3,216,512]{4,3,2,1,0:T(8,128)(2,1)S(1)}, bf16[1,1,3,216,512]{4,3,2,1,0:T(8,128)(2,1)S(1)}, u32[]{:S(2)}, u32[]{:S(2)}) collective-permute-start(bf16[1,1,3,216,512]{4,3,2,1,0:T(8,128)(2,1)S(1)} %bitcast.245), channel_id=1, source_target_pairs={{0,4},{1,5},{2,6},{3,7},{4,0},{5,1},{6,2},{7,3},{8,12},{9,13},{10,... | collective-permute-start | bytes 1990664 | tf_op jit(solution)/shard_map/ppermute | solution.py:29
  166.7 46.3 %collective-permute-start.16 = (bf16[1,2,3,216,640]{4,3,2,1,0:T(8,128)(2,1)S(1)}, bf16[1,2,3,216,640]{4,3,2,1,0:T(8,128)(2,1)S(1)}, u32[]{:S(2)}, u32[]{:S(2)}) collective-permute-start(bf16[1,2,3,216,640]{4,3,2,1,0:T(8,128)(2,1)S(1)} %pad_maximum_fusion.7), channel_id=1, source_target_pairs={{0,4},{1,5},{2,6},{3,7},{4,0},{5,1},{6,2},{7,3},{8,12},{9,13},{10,... | collective-permute-start | bytes 4976648 | tf_op jit(solution)/shard_map/ppermute | solution.py:29
  175.9 4.3 collective-permute-start.14
  178.7 29.0 %collective-permute-start.18 = (bf16[2,1,3,216,512]{4,3,2,1,0:T(8,128)(2,1)S(1)}, bf16[2,1,3,216,512]{4,3,2,1,0:T(8,128)(2,1)S(1)}, u32[]{:S(2)}, u32[]{:S(2)}) collective-permute-start(bf16[2,1,3,216,512]{4,3,2,1,0:T(8,128)(2,1)S(1)} %pad_maximum_fusion.9), channel_id=1, source_target_pairs={{0,2},{1,3},{2,0},{3,1},{4,6},{5,7},{6,4},{7,5},{8,10},{9,11},{10,... | collective-permute-start | bytes 3981320 | tf_op jit(solution)/shard_map/ppermute | solution.py:29
  233.8 2.9 collective-permute-start.19
  237.0 15.4 %collective-permute-start.20 = (bf16[2,1,1,128,1152]{4,3,2,1,0:T(8,128)(2,1)S(1)}, bf16[2,1,1,128,1152]{4,3,2,1,0:T(8,128)(2,1)S(1)}, u32[]{:S(2)}, u32[]{:S(2)}) collective-permute-start(bf16[2,1,1,128,1152]{4,3,2,1,0:T(8,128)(2,1)S(1)} %slice.640), channel_id=1, source_target_pairs={{0,8},{8,0},{16,24},{24,16},{1,9},{9,1},{17,25},{25,17},{2,10},{10... | collective-permute-start | bytes 1769480 | tf_op jit(solution)/shard_map/ppermute | solution.py:29
  252.6 16.1 %collective-permute-start.21 = (bf16[1,1,1,128,1152]{4,3,2,1,0:T(8,128)(2,1)S(1)}, bf16[1,1,1,128,1152]{4,3,2,1,0:T(8,128)(2,1)S(1)}, u32[]{:S(2)}, u32[]{:S(2)}) collective-permute-start(bf16[1,1,1,128,1152]{4,3,2,1,0:T(8,128)(2,1)S(1)} %slice.642), channel_id=1, source_target_pairs={{0,16},{8,24},{16,0},{24,8},{1,17},{9,25},{17,1},{25,9},{2,18},{10... | collective-permute-start | bytes 884744 | tf_op jit(solution)/shard_map/ppermute | solution.py:29
  270.8 14.9 %collective-permute-start.22 = (bf16[1,1,1,128,1152]{4,3,2,1,0:T(8,128)(2,1)S(1)}, bf16[1,1,1,128,1152]{4,3,2,1,0:T(8,128)(2,1)S(1)}, u32[]{:S(2)}, u32[]{:S(2)}) collective-permute-start(bf16[1,1,1,128,1152]{4,3,2,1,0:T(8,128)(2,1)S(1)} %fusion.30), channel_id=1, source_target_pairs={{0,16},{8,24},{16,0},{24,8},{1,17},{9,25},{17,1},{25,9},{2,18},{10... | collective-permute-start | bytes 884744 | tf_op jit(solution)/shard_map/ppermute | solution.py:29
  285.8 15.3 %collective-permute-start.23 = (bf16[2,1,1,128,1152]{4,3,2,1,0:T(8,128)(2,1)S(1)}, bf16[2,1,1,128,1152]{4,3,2,1,0:T(8,128)(2,1)S(1)}, u32[]{:S(2)}, u32[]{:S(2)}) collective-permute-start(bf16[2,1,1,128,1152]{4,3,2,1,0:T(8,128)(2,1)S(1)} %pad_maximum_fusion.20), channel_id=1, source_target_pairs={{0,8},{8,0},{16,24},{24,16},{1,9},{9,1},{17,25},{25,17},{2,10},{10... | collective-permute-start | bytes 1769480 | tf_op jit(solution)/shard_map/ppermute | solution.py:29
  301.3 2.9 collective-permute-start.24
  322.5 22.3 %collective-permute-start.25 = (bf16[2,2,1,128,1152]{4,3,2,1,0:T(8,128)(2,1)}, bf16[2,2,1,128,1152]{4,3,2,1,0:T(8,128)(2,1)}, u32[]{:S(2)}, u32[]{:S(2)}) collective-permute-start(bf16[2,2,1,128,1152]{4,3,2,1,0:T(8,128)(2,1)} %slice.635), channel_id=1, source_target_pairs={{0,1},{1,0},{2,3},{3,2},{4,5},{5,4},{6,7},{7,6},{8,9},{9,8},{10,11... | collective-permute-start | bytes 3538952 | tf_op jit(solution)/shard_map/ppermute | solution.py:29
  332.5 31.5 %collective-permute-start.42 = (bf16[1,2,3,216,512]{4,3,2,1,0:T(8,128)(2,1)}, bf16[1,2,3,216,512]{4,3,2,1,0:T(8,128)(2,1)}, u32[]{:S(2)}, u32[]{:S(2)}) collective-permute-start(bf16[1,2,3,216,512]{4,3,2,1,0:T(8,128)(2,1)} %slice.634), channel_id=1, source_target_pairs={{0,4},{1,5},{2,6},{3,7},{4,0},{5,1},{6,2},{7,3},{8,12},{9,13},{10,... | collective-permute-start | bytes 3981320 | tf_op jit(solution)/shard_map/ppermute | solution.py:29
  340.5 39.4 %collective-permute-start.40 = (bf16[2,1,3,216,640]{4,3,2,1,0:T(8,128)(2,1)}, bf16[2,1,3,216,640]{4,3,2,1,0:T(8,128)(2,1)}, u32[]{:S(2)}, u32[]{:S(2)}) collective-permute-start(bf16[2,1,3,216,640]{4,3,2,1,0:T(8,128)(2,1)} %slice.633), channel_id=1, source_target_pairs={{0,2},{1,3},{2,0},{3,1},{4,6},{5,7},{6,4},{7,5},{8,10},{9,11},{10,... | collective-permute-start | bytes 4976648 | tf_op jit(solution)/shard_map/ppermute | solution.py:29
  347.2 37.0 %collective-permute-start.26 = (bf16[2,1,1,128,1152]{4,3,2,1,0:T(8,128)(2,1)S(1)}, bf16[2,1,1,128,1152]{4,3,2,1,0:T(8,128)(2,1)S(1)}, u32[]{:S(2)}, u32[]{:S(2)}) collective-permute-start(bf16[2,1,1,128,1152]{4,3,2,1,0:T(8,128)(2,1)S(1)} %slice.639), channel_id=1, source_target_pairs={{0,8},{8,0},{16,24},{24,16},{1,9},{9,1},{17,25},{25,17},{2,10},{10... | collective-permute-start | bytes 1769480 | tf_op jit(solution)/shard_map/ppermute | solution.py:29
  365.8 27.4 %collective-permute-start.43 = (bf16[1,1,3,216,512]{4,3,2,1,0:T(8,128)(2,1)S(1)}, bf16[1,1,3,216,512]{4,3,2,1,0:T(8,128)(2,1)S(1)}, u32[]{:S(2)}, u32[]{:S(2)}) collective-permute-start(bf16[1,1,3,216,512]{4,3,2,1,0:T(8,128)(2,1)S(1)} %slice.638), channel_id=1, source_target_pairs={{0,2},{1,3},{2,0},{3,1},{4,6},{5,7},{6,4},{7,5},{8,10},{9,11},{10,... | collective-permute-start | bytes 1990664 | tf_op jit(solution)/shard_map/ppermute | solution.py:29
  382.7 99.2 %collective-permute-start.41 = (bf16[1,1,3,216,640]{4,3,2,1,0:T(8,128)(2,1)}, bf16[1,1,3,216,640]{4,3,2,1,0:T(8,128)(2,1)}, u32[]{:S(2)}, u32[]{:S(2)}) collective-permute-start(bf16[1,1,3,216,640]{4,3,2,1,0:T(8,128)(2,1)} %slice.637), channel_id=1, source_target_pairs={{0,4},{1,5},{2,6},{3,7},{4,0},{5,1},{6,2},{7,3},{8,12},{9,13},{10,... | collective-permute-start | bytes 2488328 | tf_op jit(solution)/shard_map/ppermute | solution.py:29
  384.4 14.1 %collective-permute-start.27 = (bf16[1,1,1,128,1152]{4,3,2,1,0:T(8,128)(2,1)S(1)}, bf16[1,1,1,128,1152]{4,3,2,1,0:T(8,128)(2,1)S(1)}, u32[]{:S(2)}, u32[]{:S(2)}) collective-permute-start(bf16[1,1,1,128,1152]{4,3,2,1,0:T(8,128)(2,1)S(1)} %slice.641), channel_id=1, source_target_pairs={{0,16},{8,24},{16,0},{24,8},{1,17},{9,25},{17,1},{25,9},{2,18},{10... | collective-permute-start | bytes 884744 | tf_op jit(solution)/shard_map/ppermute | solution.py:29
  419.0 8.3 %collective-permute-start.28 = (bf16[2,1,128,512]{3,2,1,0:T(8,128)(2,1)S(1)}, bf16[2,1,128,512]{3,2,1,0:T(8,128)(2,1)S(1)}, u32[]{:S(2)}, u32[]{:S(2)}) collective-permute-start(bf16[2,1,128,512]{3,2,1,0:T(8,128)(2,1)S(1)} %slice.643), channel_id=1, source_target_pairs={{0,8},{8,0},{16,24},{24,16},{1,9},{9,1},{17,25},{25,17},{2,10},{10... | collective-permute-start | bytes 786440 | tf_op jit(solution)/shard_map/ppermute | solution.py:29
  428.8 8.6 %collective-permute-start.29 = (bf16[1,1,128,512]{3,2,1,0:T(8,128)(2,1)}, bf16[1,1,128,512]{3,2,1,0:T(8,128)(2,1)}, u32[]{:S(2)}, u32[]{:S(2)}) collective-permute-start(bf16[1,1,128,512]{3,2,1,0:T(8,128)(2,1)} %slice.644), channel_id=1, source_target_pairs={{0,16},{8,24},{16,0},{24,8},{1,17},{9,25},{17,1},{25,9},{2,18},{10... | collective-permute-start | bytes 393224 | tf_op jit(solution)/shard_map/ppermute | solution.py:29
  433.0 46.1 %collective-permute-start.35 = (bf16[2,2,2,2,1,32,1152]{6,5,4,3,2,1,0:T(8,128)(2,1)}, bf16[2,2,2,2,1,32,1152]{6,5,4,3,2,1,0:T(8,128)(2,1)}, u32[]{:S(2)}, u32[]{:S(2)}) collective-permute-start(bf16[2,2,2,2,1,32,1152]{6,5,4,3,2,1,0:T(8,128)(2,1)} %select_convert_fusion.1), channel_id=1, source_target_pairs={{0,1},{1,0},{2,3},{3,2},{4,5},{5,4},{6,7},{7,6},{8,9},{9,8},{10,11... | collective-permute-start | bytes 3538952 | tf_op jit(solution)/shard_map/ppermute | solution.py:29
  459.8 3.7 collective-permute-start.45
  463.6 6.2 %collective-permute-start.46 = (f32[2,2,1,1,1,160]{5,4,3,2,1,0:T(1,128)S(1)}, f32[2,2,1,1,1,160]{5,4,3,2,1,0:T(1,128)S(1)}, u32[]{:S(2)}, u32[]{:S(2)}) collective-permute-start(f32[2,2,1,1,1,160]{5,4,3,2,1,0:T(1,128)S(1)} %broadcast_select_fusion.30), channel_id=1, source_target_pairs={{0,2},{1,3},{2,0},{3,1},{4,6},{5,7},{6,4},{7,5},{8,10},{9,11},{10,... | collective-permute-start | bytes 7688 | tf_op jit(solution)/shard_map/ppermute | solution.py:29
  469.7 27.0 %collective-permute-start.30 = (bf16[2,2,2,2,1,36,1536]{6,3,5,4,2,1,0:T(2,128)(2,1)S(1)}, bf16[2,2,2,2,1,36,1536]{6,3,5,4,2,1,0:T(2,128)(2,1)S(1)}, u32[]{:S(2)}, u32[]{:S(2)}) collective-permute-start(bf16[2,2,2,2,1,36,1536]{6,3,5,4,2,1,0:T(2,128)(2,1)S(1)} %select_convert_fusion), channel_id=1, source_target_pairs={{0,1},{1,0},{2,3},{3,2},{4,5},{5,4},{6,7},{7,6},{8,9},{9,8},{10,11... | collective-permute-start | bytes 5308424 | tf_op jit(solution)/shard_map/ppermute | solution.py:29
  469.8 3.7 collective-permute-start.47
  473.5 4.5 collective-permute-start.48
  481.3 13.5 %collective-permute-start.36 = (bf16[2,2,2,1,1,32,1152]{6,5,4,3,2,1,0:T(8,128)(2,1)S(1)}, bf16[2,2,2,1,1,32,1152]{6,5,4,3,2,1,0:T(8,128)(2,1)S(1)}, u32[]{:S(2)}, u32[]{:S(2)}) collective-permute-start(bf16[2,2,2,1,1,32,1152]{6,5,4,3,2,1,0:T(8,128)(2,1)S(1)} %select_convert_fusion.3), channel_id=1, source_target_pairs={{0,2},{1,3},{2,0},{3,1},{4,6},{5,7},{6,4},{7,5},{8,10},{9,11},{10,... | collective-permute-start | bytes 1769480 | tf_op jit(solution)/shard_map/ppermute | solution.py:29
  495.7 8.7 %collective-permute-start.37 = (bf16[2,2,1,1,1,32,1152]{6,5,4,3,2,1,0:T(8,128)(2,1)}, bf16[2,2,1,1,1,32,1152]{6,5,4,3,2,1,0:T(8,128)(2,1)}, u32[]{:S(2)}, u32[]{:S(2)}) collective-permute-start(bf16[2,2,1,1,1,32,1152]{6,5,4,3,2,1,0:T(8,128)(2,1)} %select_convert_fusion.4), channel_id=1, source_target_pairs={{0,4},{1,5},{2,6},{3,7},{4,0},{5,1},{6,2},{7,3},{8,12},{9,13},{10,... | collective-permute-start | bytes 884744 | tf_op jit(solution)/shard_map/ppermute | solution.py:29
  503.3 18.7 %collective-permute-start.31 = (bf16[2,2,1,2,1,36,1536]{6,3,5,4,2,1,0:T(2,128)(2,1)S(1)}, bf16[2,2,1,2,1,36,1536]{6,3,5,4,2,1,0:T(2,128)(2,1)S(1)}, u32[]{:S(2)}, u32[]{:S(2)}) collective-permute-start(bf16[2,2,1,2,1,36,1536]{6,3,5,4,2,1,0:T(2,128)(2,1)S(1)} %select_convert_fusion.2), channel_id=1, source_target_pairs={{0,4},{1,5},{2,6},{3,7},{4,0},{5,1},{6,2},{7,3},{8,12},{9,13},{10,... | collective-permute-start | bytes 2654216 | tf_op jit(solution)/shard_map/ppermute | solution.py:29
  505.5 20.1 %collective-permute-start.38 = (bf16[2,1,1,1,1,32,1152]{6,5,4,3,2,1,0:T(8,128)(2,1)S(1)}, bf16[2,1,1,1,1,32,1152]{6,5,4,3,2,1,0:T(8,128)(2,1)S(1)}, u32[]{:S(2)}, u32[]{:S(2)}) collective-permute-start(bf16[2,1,1,1,1,32,1152]{6,5,4,3,2,1,0:T(8,128)(2,1)S(1)} %select_convert_fusion.5), channel_id=1, source_target_pairs={{0,8},{8,0},{16,24},{24,16},{1,9},{9,1},{17,25},{25,17},{2,10},{10... | collective-permute-start | bytes 442376 | tf_op jit(solution)/shard_map/ppermute | solution.py:29
  525.0 8.4 %collective-permute-start.32 = (bf16[2,2,1,1,1,36,1536]{6,1,5,4,3,2,0:T(2,128)(2,1)S(1)}, bf16[2,2,1,1,1,36,1536]{6,1,5,4,3,2,0:T(2,128)(2,1)S(1)}, u32[]{:S(2)}, u32[]{:S(2)}) collective-permute-start(bf16[2,2,1,1,1,36,1536]{6,1,5,4,3,2,0:T(2,128)(2,1)S(1)} %copy.217), channel_id=1, source_target_pairs={{0,2},{1,3},{2,0},{3,1},{4,6},{5,7},{6,4},{7,5},{8,10},{9,11},{10,... | collective-permute-start | bytes 1327112 | tf_op jit(solution)/shard_map/ppermute | solution.py:29
  534.9 10.8 %collective-permute-start.33 = (bf16[2,1,1,1,1,36,1536]{6,3,5,4,2,1,0:T(2,128)(2,1)S(1)}, bf16[2,1,1,1,1,36,1536]{6,3,5,4,2,1,0:T(2,128)(2,1)S(1)}, u32[]{:S(2)}, u32[]{:S(2)}) collective-permute-start(bf16[2,1,1,1,1,36,1536]{6,3,5,4,2,1,0:T(2,128)(2,1)S(1)} %fusion.41), channel_id=1, source_target_pairs={{0,8},{8,0},{16,24},{24,16},{1,9},{9,1},{17,25},{25,17},{2,10},{10... | collective-permute-start | bytes 663560 | tf_op jit(solution)/shard_map/ppermute | solution.py:29
  535.8 11.9 %collective-permute-start.39 = (bf16[1,1,1,1,1,32,1152]{6,5,4,3,2,1,0:T(8,128)(2,1)S(1)}, bf16[1,1,1,1,1,32,1152]{6,5,4,3,2,1,0:T(8,128)(2,1)S(1)}, u32[]{:S(2)}, u32[]{:S(2)}) collective-permute-start(bf16[1,1,1,1,1,32,1152]{6,5,4,3,2,1,0:T(8,128)(2,1)S(1)} %select_convert_fusion.6), channel_id=1, source_target_pairs={{0,16},{8,24},{16,0},{24,8},{1,17},{9,25},{17,1},{25,9},{2,18},{10... | collective-permute-start | bytes 221192 | tf_op jit(solution)/shard_map/ppermute | solution.py:29
  546.7 8.8 %collective-permute-start.34 = (bf16[1,1,1,1,1,36,1536]{6,3,5,4,2,1,0:T(2,128)(2,1)S(1)}, bf16[1,1,1,1,1,36,1536]{6,3,5,4,2,1,0:T(2,128)(2,1)S(1)}, u32[]{:S(2)}, u32[]{:S(2)}) collective-permute-start(bf16[1,1,1,1,1,36,1536]{6,3,5,4,2,1,0:T(2,128)(2,1)S(1)} %fusion.53), channel_id=1, source_target_pairs={{0,16},{8,24},{16,0},{24,8},{1,17},{9,25},{17,1},{25,9},{2,18},{10... | collective-permute-start | bytes 331784 | tf_op jit(solution)/shard_map/ppermute | solution.py:29
  (99 other events, 843.3 us)

commit v2 on v1

--- a/solution.py
+++ b/solution.py
@@ -39,6 +39,14 @@
     return own.astype(jnp.float32) + swapped(other, axis, bit).astype(jnp.float32)
 
 
+def scatter_sum(value, stages):
+    for axis, bit, at in stages:
+        own = lax.slice_in_dim(value, 0, 1, axis=at)
+        other = lax.slice_in_dim(value, 1, 2, axis=at)
+        value = own + swapped(other, axis, bit)
+    return value.reshape(value.shape[len(stages) :])
+
+
 def gather_xor(value, stages):
     value = value.reshape((1,) * len(stages) + value.shape)
     for axis, bit, at in stages:
@@ -52,30 +60,18 @@
     return value.reshape(value.shape[len(stages) :])
 
 
-def ordered_pair(value, axis, bit, at):
-    other = swapped(value, axis, bit)
-    high = (lax.axis_index(axis) & bit) != 0
-    return jnp.concatenate(
-        [jnp.where(high, other, value), jnp.where(high, value, other)], axis=at
-    )
-
-
-def gather_ordered(value, stages):
-    value = value.reshape((1,) * len(stages) + value.shape)
-    for axis, bit, at in stages:
-        value = ordered_pair(value, axis, bit, at)
-    return value
-
-
-def scatter_ordered(value, stages, dtype):
-    for axis, bit, at in stages:
-        high = (lax.axis_index(axis) & bit) != 0
-        low_half = lax.slice_in_dim(value, 0, 1, axis=at)
-        high_half = lax.slice_in_dim(value, 1, 2, axis=at)
-        own = jnp.where(high, high_half, low_half).astype(jnp.float32)
-        sent = jnp.where(high, low_half, high_half).astype(dtype)
-        value = own + swapped(sent, axis, bit).astype(jnp.float32)
-    return value.reshape(value.shape[len(stages) :])
+def one_hot_order(origin, count):
+    return (jnp.arange(count, dtype=jnp.int32)[:, None] == origin[None, :]).astype(jnp.bfloat16)
+
+
+def in_order(value, order):
+    return lax.dot_general(
+        value.astype(jnp.float32),
+        order.astype(jnp.float32),
+        (((1,), (1,)), ((), ())),
+        precision=lax.Precision.HIGHEST,
+        preferred_element_type=jnp.float32,
+    )
 
 
 def inv_root(vector):
@@ -189,25 +185,58 @@
     core_stage = [("dp", 1, nseq + nchip)]
     all_up = seq_stages + chip_stages + core_stage
     all_down = seq_stages + chip_stages[::-1] + core_stage
+    dp_count = lax.axis_size("dp")
+    chips = dp_count // 2
+    planes = [[2 * chip + core for chip in range(chips)] for core in range(2)]
     kv_stages = seq_stages
+    seq_stages_only = seq_stages
     token_stages = seq_stages + [("dp", 1, nseq)]
-    ffn_up = [("dp", bit, nchip - 1 - k) for k, bit in enumerate(chip_bits)]
-    ffn_down = ffn_up[::-1]
     keys = seq_count * rows
-    cut = (width // 256) * 128 + (128 if width % 256 else 0)
     scale = 1.0 / math.sqrt(HEAD_DIM)
-    qkv_full = gather_ordered(w_qkv, all_up).reshape(-1, w_qkv.shape[1])
-    out_full = gather_ordered(w_out, all_down).reshape(-1, w_out.shape[1])
-    ffn_rows = jnp.stack([w_gate, w_up, w_down])
-    left_rows, right_rows, qkv_full, out_full = lax.optimization_barrier(
-        (ffn_rows[:, :, :cut], ffn_rows[:, :, cut:], qkv_full, out_full)
-    )
-    ffn_full = jnp.concatenate(
-        [gather_xor(left_rows, ffn_up), gather_xor(right_rows, ffn_down)], axis=-1
-    )
-    ffn_full = ffn_full.reshape((-1,) + ffn_rows.shape)
-    gate_full, up_full, down_full = (ffn_full[:, i].reshape(-1, width) for i in range(3))
     block_id = lax.axis_index("seq")
+    dp_id = lax.axis_index("dp")
+    seq_off = jnp.arange(seq_count, dtype=jnp.int32)
+    chip_off = jnp.arange(chips, dtype=jnp.int32)
+    core_off = jnp.arange(2, dtype=jnp.int32)
+    qkv_own = w_qkv.shape[0]
+    qkv_pad = (qkv_own + 7) // 8 * 8
+    out_own = w_out.shape[0]
+    ffn_own = w_gate.shape[0]
+    half = w_qkv.shape[1] // 2
+    qkv_dev = (
+        (block_id ^ seq_off)[:, None, None] * dp_count
+        + ((dp_id // 2) ^ chip_off)[None, :, None] * 2
+        + ((dp_id % 2) ^ core_off)[None, None, :]
+    ).reshape(-1, 1)
+    lane = jnp.arange(qkv_pad, dtype=jnp.int32)[None, :]
+    qkv_origin = jnp.where(lane < qkv_own, qkv_dev * qkv_own + lane, -1).reshape(-1)
+    out_dev = (
+        (block_id ^ seq_off)[None, None, :] * dp_count
+        + chip_off[None, :, None] * 2
+        + ((dp_id % 2) ^ core_off)[:, None, None]
+    ).reshape(-1, 1)
+    out_origin = (out_dev * out_own + jnp.arange(out_own, dtype=jnp.int32)[None, :]).reshape(-1)
+    qkv_order = one_hot_order(qkv_origin, width)
+    out_order = one_hot_order(out_origin, qwidth)
+    w_qkv_pad = jnp.pad(w_qkv, ((0, qkv_pad - qkv_own), (0, 0)))
+    qkv_full = jnp.concatenate(
+        [
+            gather_xor(w_qkv_pad[:, :half], all_up),
+            gather_xor(w_qkv_pad[:, half:], all_down),
+        ],
+        axis=-1,
+    ).reshape(-1, 2 * half)
+    out_column = gather_xor(w_out, seq_stages_only).reshape(-1, width)
+    plane_rows = lax.all_gather(
+        jnp.concatenate([w_gate, w_up, w_down, out_column], axis=0),
+        "dp",
+        axis_index_groups=planes,
+        axis=0,
+    )
+    gate_full, up_full, down_full = (
+        plane_rows[:, i * ffn_own : (i + 1) * ffn_own].reshape(-1, width) for i in range(3)
+    )
+    out_full = mine_first(plane_rows[None, :, 3 * ffn_own :], "dp", 1, 0).reshape(-1, width)
     starts = jnp.cumsum(lens) - lens
     own_index = block_id * rows + jnp.arange(rows, dtype=jnp.int32)
     key_index = (
@@ -226,7 +255,8 @@
     root_attn = inv_root(rows_in)
     unit_attn = rows_in * root_attn
     attn_input = (unit_attn * g_attn_in).astype(jnp.bfloat16)
-    projected = dot32(attn_input, qkv_full)
+    attn_slots = dot32(attn_input, qkv_order).astype(jnp.bfloat16)
+    projected = dot32(attn_slots, qkv_full)
     query = projected[:, :qwidth].reshape(rows, HEADS, HEAD_DIM)
     key_raw = projected[:, qwidth : qwidth + HEAD_DIM]
     value_raw = projected[:, qwidth + HEAD_DIM :]
@@ -249,7 +279,8 @@
     probs_b = probs.astype(jnp.bfloat16)
     mixed = jnp.einsum("rhk,kd->rhd", probs_b, values_b, preferred_element_type=jnp.float32)
     mixed_b = mixed.reshape(rows, qwidth).astype(jnp.bfloat16)
-    attn_out = dot32(mixed_b, out_full)
+    mixed_slots = dot32(mixed_b, out_order).astype(jnp.bfloat16)
+    attn_out = dot32(mixed_slots, out_full)
     root_post = inv_root(attn_out)
     unit_post = attn_out * root_post
     hidden_in = rows_in + unit_post * g_attn_out
@@ -271,28 +302,32 @@
     )
     ffn_in_grad = scatter_xor(in_part.reshape(slots + (rows, width)), token_stages[::-1])
     terms = ffn_weight_terms(tokens_b, grads_b, gate_all, up_all, dgate_all, dup_all)
-    chips = (2,) * nchip
-    own_rows = w_gate.shape[0]
-
-    def term_part(first, last):
-        return jnp.stack(
-            [term[:, first:last].reshape(chips + (own_rows, last - first)) for term in terms],
-            axis=nchip,
-        )
-
-    ffn_terms = jnp.concatenate(
-        [
-            scatter_xor(term_part(0, cut), ffn_up),
-            scatter_xor(term_part(cut, width), ffn_down),
-        ],
-        axis=-1,
-    )
+    ffn_terms = lax.psum_scatter(
+        jnp.concatenate(
+            [term.astype(jnp.bfloat16).reshape(chips, ffn_own, width) for term in terms], axis=1
+        ),
+        "dp",
+        axis_index_groups=planes,
+        scatter_dimension=0,
+    ).astype(jnp.float32)
+    ffn_terms = ffn_terms.reshape(3, ffn_own, width)
     grad_w_gate, grad_w_up, grad_w_down = ffn_terms[0], ffn_terms[1], ffn_terms[2]
     grad_g_ffn_in = jnp.sum(ffn_in_grad * unit_ffn, axis=0)
     hidden_grad_in = rows_grad + norm_back(ffn_in_grad, unit_ffn, root_ffn, g_ffn_in)
     grad_g_attn_out = jnp.sum(hidden_grad_in * unit_post, axis=0)
     attn_grad_b = norm_back(hidden_grad_in, unit_post, root_post, g_attn_out).astype(jnp.bfloat16)
-    mixed_grad_b = contract_cols(attn_grad_b, out_full).astype(jnp.bfloat16)
+    mixed_grad_slots = contract_cols(attn_grad_b, out_full).astype(jnp.bfloat16)
+    mixed_grad_b = contract_cols(mixed_grad_slots, out_order).astype(jnp.bfloat16)
+    out_term = contract_rows(mixed_slots, attn_grad_b).reshape(2, chips, -1, width)
+    out_plane = lax.psum_scatter(
+        keep_half(out_term, "dp", 1, 0)[0].astype(jnp.bfloat16),
+        "dp",
+        axis_index_groups=planes,
+        scatter_dimension=0,
+    ).astype(jnp.float32)
+    owned_out = scatter_xor(
+        out_plane.reshape((2,) * nseq + w_out.shape), seq_stages[::-1]
+    )
     mixed_grad3 = mixed_grad_b.reshape(rows, HEADS, HEAD_DIM)
     delta = jnp.sum(
         mixed_grad3.astype(jnp.float32)
@@ -332,22 +367,23 @@
     qkv_grad_b = jnp.concatenate(
         [query_grad.reshape(rows, qwidth), key_grad, value_grad], axis=1
     ).astype(jnp.bfloat16)
-    attn_in_grad = contract_cols(qkv_grad_b, qkv_full)
+    attn_in_grad = in_order(contract_cols(qkv_grad_b, qkv_full), qkv_order)
     grad_g_attn_in = jnp.sum(attn_in_grad * unit_attn, axis=0)
     input_grad = hidden_grad_in + norm_back(attn_in_grad, unit_attn, root_attn, g_attn_in)
     spread = (2,) * (nseq + nchip + 1)
     count = seq_count * lax.axis_size("dp")
     gains = [grad_g_attn_in, grad_g_attn_out, grad_g_ffn_in, grad_g_ffn_out, grad_g_query, grad_g_key]
     gain_terms = jnp.concatenate([g.reshape(count, -1) for g in gains], axis=1)
-    out_term = contract_rows(mixed_b, attn_grad_b)
-    qkv_term = contract_rows(attn_input, qkv_grad_b)
-    owned_qkv = scatter_ordered(
-        qkv_term.reshape(spread + w_qkv.shape), all_up[::-1], jnp.bfloat16
-    )
-    owned_out = scatter_ordered(
-        out_term.reshape(spread + w_out.shape), all_down[::-1], jnp.bfloat16
-    )
-    owned = scatter_ordered(gain_terms.reshape(spread + (-1,)), all_up[::-1], jnp.float32)
+    qkv_term = contract_rows(attn_slots, qkv_grad_b).reshape(spread + (qkv_pad, 2 * half))
+    owned_qkv = jnp.concatenate(
+        [
+            scatter_xor(qkv_term[..., :half], all_up[::-1]),
+            scatter_xor(qkv_term[..., half:], all_down[::-1]),
+        ],
+        axis=-1,
+    )[:qkv_own]
+    gain_slots = jnp.take(gain_terms, qkv_dev.reshape(-1), axis=0)
+    owned = scatter_sum(gain_slots.reshape(spread + (-1,)), all_up[::-1])
     own_width, own_head = width // count, HEAD_DIM // count
     owned_gains = [owned[i * own_width : (i + 1) * own_width] for i in range(4)]
     owned_heads = [

time: 563 us -> 454 us (0.81)
  other arithmetic: 102 us -> 37.8 us
  local copies, waits for them, and re-layouts: 65.9 us -> 26 us
  waiting for transfers between devices: 279 us -> 263 us
  between operations: 2.8 us -> 15.8 us
    ppermute x49 -> x47, waiting for transfers between devices: 279 us -> 237 us  [swapped(): return lax.ppermute(value, axis, [(i, i ^ bit) for i in range(length)])]
    all_gather x0 -> x1, waiting for transfers between devices: none -> 26.4 us  [local(): lax.all_gather(jnp.concatenate([w_gate, w_up, w_down, out_column], axis=0...]
    select_n x15 -> x3, other arithmetic: 14.6 us -> 0.16 us  [the longest x2 0.09 us: local(): gain_slots = jnp.take(gain_terms, qkv_dev.reshape(-1), axis=0)]
    add x14 -> x9, other arithmetic: 12.5 us -> 0.93 us  [the longest x2 0.74 us: local(): (block_id ^ seq_off)[:, None, None] * dp_count]
    concatenate x11 -> x4, other arithmetic: 16.8 us -> 7.81 us  [the longest x1 3.4 us: local(): jnp.concatenate([term.astype(jnp.bfloat16).reshape(chips, ffn_own, width)...]
    unnamed x187 -> x144, local copies, waits for them, and re-layouts: 13.4 us -> 4.51 us
    convert_element_type x10 -> x2, other arithmetic: 9.6 us -> 2.87 us  [the longest x1 1.59 us: local(): ffn_terms = lax.psum_scatter(jnp.concatenate([term.astype(jnp.bfloat16).r...]
    reshape x3 -> x7, local copies, waits for them, and re-layouts: 6.75 us -> 0.57 us  [the longest x6 0.56 us: local(): gain_terms = jnp.concatenate([g.reshape(count, -1) for g in gains], axis=1)]
  transfers between devices with their start and end apart: 49 -> 50, of which waited for: 34 -> 39; matrix products, arithmetic and copies ran while one was open for 22% -> 15% of each run, Pallas kernels for 0% -> 0%
where the time goes in v2:
time: 454 us; the launch traced here: 450 us
  waiting for transfers between devices  263 us (58%)
  matrix products  55.4 us (12%)
  starting transfers between devices  51.7 us (11%)
  other arithmetic  37.8 us (8%)
  local copies, waits for them, and re-layouts  26 us (6%)
  between operations  15.8 us (3%)
    ppermute x47, waiting for transfers between devices, swapped(): return lax.ppermute(value, axis, [(i, i ^ bit) for i in range(length)])  237 us
    ppermute x47, starting transfers between devices, swapped(): return lax.ppermute(value, axis, [(i, i ^ bit) for i in range(length)])  51.2 us
    all_gather x1, waiting for transfers between devices, local(): lax.all_gather(jnp.concatenate([w_gate, w_up, w_down, out_column], axis=0...  26.4 us
    dot_general x5, matrix products, contract_cols(): lax.dot_general(left, right, (((1,), (1,)), ((), ())), preferred_element_...  18.8 us
    dot_general x7, matrix products, dot32(): return jnp.dot(left, right, preferred_element_type=jnp.float32)  15.7 us
    dot_general x5, matrix products, contract_rows(): lax.dot_general(left, right, (((0,), (0,)), ((), ())), preferred_element_...  11.7 us
  transfers between devices with their start and end apart: 50, of which 39 were waited for; matrix products, arithmetic and copies ran while one was open for 15% of the time, Pallas kernels for 0%

profile of v2, /device:TPU:0, one launch (start us, length us, event | category | flops | bytes accessed | tf_op | source)
XLA Modules:
  0.0 450.2 jit_solution(13754528485598472950)
XLA Ops:
  7.2 4.1 collective-permute-start.12
  11.4 4.1 collective-permute-done.12
  17.2 4.4 collective-permute-done.13
  22.5 2.8 pad_maximum_fusion.4
  25.5 2.7 collective-permute-start
  30.7 2.8 collective-permute-start.1
  37.5 2.5 collective-permute-start.2
  41.7 8.0 %collective-permute-done.2 = bf16[2,2,1,1,1,40,768]{6,5,4,3,2,1,0:T(8,128)(2,1)S(1)} collective-permute-done((bf16[2,2,1,1,1,40,768]{6,5,4,3,2,1,0:T(8,128)(2,1)S(1)}, bf16[2,2,1,1,1,40,768]{6,5,4,3,2,1,0:T(8,128)(2,1)S(1)}, u32[]{:S(2)}, u32[]{:S(2)}) %collective-permute-start.2) | collective-permute-done | bytes 245792 | tf_op jit(solution)/shard_map/ppermute | solution.py:29
  55.7 18.1 %collective-permute-done.3 = bf16[2,2,1,2,1,40,768]{6,5,4,3,2,1,0:T(8,128)(2,1)S(1)} collective-permute-done((bf16[2,2,1,2,1,40,768]{6,5,4,3,2,1,0:T(8,128)(2,1)S(1)}, bf16[2,2,1,2,1,40,768]{6,5,4,3,2,1,0:T(8,128)(2,1)S(1)}, u32[]{:S(2)}, u32[]{:S(2)}) %collective-permute-start.3) | collective-permute-done | bytes 491552 | tf_op jit(solution)/shard_map/ppermute | solution.py:29
  82.4 2.7 collective-permute-start.10
  85.2 6.6 %collective-permute-done.10 = bf16[1,1,128,512]{3,2,1,0:T(8,128)(2,1)S(1)} collective-permute-done((bf16[1,1,128,512]{3,2,1,0:T(8,128)(2,1)S(1)}, bf16[1,1,128,512]{3,2,1,0:T(8,128)(2,1)S(1)}, u32[]{:S(2)}, u32[]{:S(2)}) %collective-permute-start.10) | collective-permute-done | bytes 131104 | tf_op jit(solution)/shard_map/ppermute | solution.py:29
  93.1 26.4 %all-gather.3.cloned.1.call-done = bf16[3104,1152]{1,0:T(8,128)(2,1)} async-done(((bf16[776,1152]{1,0:T(8,128)(2,1)}), bf16[3104,1152]{1,0:T(8,128)(2,1)}) %all-gather.3.cloned.1.call-update) | async-done | bytes 7151632 | tf_op jit(solution)/shard_map/all_gather | solution.py:230
  131.9 2.5 collective-permute-start.15
  134.4 14.1 %collective-permute-done.15 = bf16[1,1,1,128,1152]{4,3,2,1,0:T(8,128)(2,1)S(1)} collective-permute-done((bf16[1,1,1,128,1152]{4,3,2,1,0:T(8,128)(2,1)S(1)}, bf16[1,1,1,128,1152]{4,3,2,1,0:T(8,128)(2,1)S(1)}, u32[]{:S(2)}, u32[]{:S(2)}) %collective-permute-start.15) | collective-permute-done | bytes 294944 | tf_op jit(solution)/shard_map/ppermute | solution.py:29
  149.2 14.2 %collective-permute-done.16 = bf16[2,1,1,128,1152]{4,3,2,1,0:T(8,128)(2,1)S(1)} collective-permute-done((bf16[2,1,1,128,1152]{4,3,2,1,0:T(8,128)(2,1)S(1)}, bf16[2,1,1,128,1152]{4,3,2,1,0:T(8,128)(2,1)S(1)}, u32[]{:S(2)}, u32[]{:S(2)}) %collective-permute-start.16) | collective-permute-done | bytes 589856 | tf_op jit(solution)/shard_map/ppermute | solution.py:29
  166.8 2.5 fusion.77
  169.3 5.4 %multiply_convert_fusion.1 = (bf16[1024,864]{0,1:T(8,128)(2,1)}, f32[1024,864]{0,1:T(8,128)}) fusion(f32[1024,864]{0,1:T(8,128)S(1)} %fusion.77, bf16[1024,1152]{1,0:T(8,128)(2,1)S(1)} %bitcast.228, bf16[864,1152]{1,0:T(8,128)(2,1)S(1)} %bitcast.233), kind=kOutput, calls=%fused_computation.21 | convolution fusion | flops 2047279104 | bytes 13197312 | tf_op jit(solution)/shard_map/dot_general | solution.py:122
  174.7 5.5 %dot_general.86 = bf16[2,2,2,128,864]{3,2,1,0,4:T(2,128)(2,1)} reshape(bf16[1024,864]{0,1:T(8,128)(2,1)} %get-tuple-element.71) | data formatting | bytes 3538944 | tf_op jit(solution)/shard_map/dot_general | solution.py:112
  180.1 5.0 %fusion.17 = f32[2,2,2,128,1152]{4,3,2,1,0:T(8,128)S(1)} fusion(bf16[864,1152,1,1,1]{1,0,4,3,2:T(8,128)(2,1)} %bitcast.208, bf16[2,2,2,128,864]{3,2,1,0,4:T(2,128)(2,1)} %dot_general.86), kind=kOutput, calls=%fused_computation.43 | convolution fusion | flops 2038431744 | bytes 8478720 | tf_op jit(solution)/shard_map/dot_general | solution.py:112
  185.7 2.5 collective-permute-done.18
  189.6 14.6 %collective-permute-done.19 = bf16[2,1,1,128,1152]{4,3,2,1,0:T(8,128)(2,1)S(1)} collective-permute-done((bf16[2,1,1,128,1152]{4,3,2,1,0:T(8,128)(2,1)S(1)}, bf16[2,1,1,128,1152]{4,3,2,1,0:T(8,128)(2,1)S(1)}, u32[]{:S(2)}, u32[]{:S(2)}) %collective-permute-start.19) | collective-permute-done | bytes 589856 | tf_op jit(solution)/shard_map/ppermute | solution.py:29
  204.3 2.7 collective-permute-start.20
  207.0 13.0 %collective-permute-done.20 = bf16[1,1,1,128,1152]{4,3,2,1,0:T(8,128)(2,1)S(1)} collective-permute-done((bf16[1,1,1,128,1152]{4,3,2,1,0:T(8,128)(2,1)S(1)}, bf16[1,1,1,128,1152]{4,3,2,1,0:T(8,128)(2,1)S(1)}, u32[]{:S(2)}, u32[]{:S(2)}) %collective-permute-start.20) | collective-permute-done | bytes 294944 | tf_op jit(solution)/shard_map/ppermute | solution.py:29
  222.2 15.0 %collective-permute-done.21 = bf16[1,1,1,128,1152]{4,3,2,1,0:T(8,128)(2,1)S(1)} collective-permute-done((bf16[1,1,1,128,1152]{4,3,2,1,0:T(8,128)(2,1)S(1)}, bf16[1,1,1,128,1152]{4,3,2,1,0:T(8,128)(2,1)S(1)}, u32[]{:S(2)}, u32[]{:S(2)}) %collective-permute-start.21) | collective-permute-done | bytes 294944 | tf_op jit(solution)/shard_map/ppermute | solution.py:29
  237.3 13.2 %collective-permute-done.22 = bf16[2,1,1,128,1152]{4,3,2,1,0:T(8,128)(2,1)S(1)} collective-permute-done((bf16[2,1,1,128,1152]{4,3,2,1,0:T(8,128)(2,1)S(1)}, bf16[2,1,1,128,1152]{4,3,2,1,0:T(8,128)(2,1)S(1)}, u32[]{:S(2)}, u32[]{:S(2)}) %collective-permute-start.22) | collective-permute-done | bytes 589856 | tf_op jit(solution)/shard_map/ppermute | solution.py:29
  250.8 2.8 collective-permute-done.23
  254.0 5.0 %multiply_convert_fusion = (bf16[1024,864]{0,1:T(8,128)(2,1)S(1)}, bf16[1024,864]{0,1:T(8,128)(2,1)S(1)}) fusion(f32[1024,864]{0,1:T(8,128)S(1)} %copy-done.66, f32[1024,864]{0,1:T(8,128)S(1)} %copy-done.67, bf16[1024,1152]{1,0:T(8,128)(2,1)S(1)} %bitcast.231, bf16[864,1152]{1,0:T(8,128)(2,1)S(1)} %bitcast.209), kind=kOutput, calls=%fused_computation.20 | convolution fusion | flops 2058780672 | bytes 14966784 | tf_op jit(solution)/shard_map/dot_general | solution.py:122
  259.0 3.0 fusion.78
  262.0 3.1 convolution_add_fusion
  265.4 2.7 collective-permute-done.24
  268.9 15.0 %collective-permute-done.25 = bf16[2,1,1,128,1152]{4,3,2,1,0:T(8,128)(2,1)S(1)} collective-permute-done((bf16[2,1,1,128,1152]{4,3,2,1,0:T(8,128)(2,1)S(1)}, bf16[2,1,1,128,1152]{4,3,2,1,0:T(8,128)(2,1)S(1)}, u32[]{:S(2)}, u32[]{:S(2)}) %collective-permute-start.25) | collective-permute-done | bytes 589856 | tf_op jit(solution)/shard_map/ppermute | solution.py:29
  286.2 13.4 %collective-permute-done.26 = bf16[1,1,1,128,1152]{4,3,2,1,0:T(8,128)(2,1)S(1)} collective-permute-done((bf16[1,1,1,128,1152]{4,3,2,1,0:T(8,128)(2,1)S(1)}, bf16[1,1,1,128,1152]{4,3,2,1,0:T(8,128)(2,1)S(1)}, u32[]{:S(2)}, u32[]{:S(2)}) %collective-permute-start.26) | collective-permute-done | bytes 294944 | tf_op jit(solution)/shard_map/ppermute | solution.py:29
  303.6 2.7 collective-permute-done.39
  308.0 3.1 fusion.22
  311.1 4.8 %convolution_convert_fusion = bf16[864,1152]{1,0:T(8,128)(2,1)S(1)} fusion(bf16[1024,864]{0,1:T(8,128)(2,1)} %get-tuple-element.71, bf16[1024,1152]{1,0:T(8,128)(2,1)} %bitcast.232), kind=kOutput, calls=%fused_computation.22 | convolution fusion | flops 2039427072 | bytes 6119424 | tf_op jit(solution)/shard_map/dot_general | solution.py:116
  320.9 3.4 pad_maximum_fusion
  336.1 8.0 %collective-permute-done.27 = bf16[2,1,128,512]{3,2,1,0:T(8,128)(2,1)S(1)} collective-permute-done((bf16[2,1,128,512]{3,2,1,0:T(8,128)(2,1)S(1)}, bf16[2,1,128,512]{3,2,1,0:T(8,128)(2,1)S(1)}, u32[]{:S(2)}, u32[]{:S(2)}) %collective-permute-start.27) | collective-permute-done | bytes 262176 | tf_op jit(solution)/shard_map/ppermute | solution.py:29
  347.4 6.4 %collective-permute-done.28 = bf16[1,1,128,512]{3,2,1,0:T(8,128)(2,1)S(1)} collective-permute-done((bf16[1,1,128,512]{3,2,1,0:T(8,128)(2,1)S(1)}, bf16[1,1,128,512]{3,2,1,0:T(8,128)(2,1)S(1)}, u32[]{:S(2)}, u32[]{:S(2)}) %collective-permute-start.28) | collective-permute-done | bytes 131104 | tf_op jit(solution)/shard_map/ppermute | solution.py:29
  358.0 3.6 fusion.53
  361.6 3.1 multiply_reduce_fusion.2
  376.9 2.5 collective-permute-done.45
  386.6 14.5 %collective-permute-done.30 = bf16[2,2,1,2,1,40,768]{6,5,4,3,2,1,0:T(8,128)(2,1)S(1)} collective-permute-done((bf16[2,2,1,2,1,40,768]{6,5,4,3,2,1,0:T(8,128)(2,1)S(1)}, bf16[2,2,1,2,1,40,768]{6,5,4,3,2,1,0:T(8,128)(2,1)S(1)}, u32[]{:S(2)}, u32[]{:S(2)}) %collective-permute-start.30) | collective-permute-done | bytes 491552 | tf_op jit(solution)/shard_map/ppermute | solution.py:29
  401.8 5.2 %collective-permute-done.35 = bf16[2,2,2,1,1,40,768]{6,5,4,3,2,1,0:T(8,128)(2,1)S(1)} collective-permute-done((bf16[2,2,2,1,1,40,768]{6,5,4,3,2,1,0:T(8,128)(2,1)S(1)}, bf16[2,2,2,1,1,40,768]{6,5,4,3,2,1,0:T(8,128)(2,1)S(1)}, u32[]{:S(2)}, u32[]{:S(2)}) %collective-permute-start.35) | collective-permute-done | bytes 491552 | tf_op jit(solution)/shard_map/ppermute | solution.py:29
  408.6 6.3 %collective-permute-done.31 = bf16[2,2,1,1,1,40,768]{6,5,4,3,2,1,0:T(8,128)(2,1)S(1)} collective-permute-done((bf16[2,2,1,1,1,40,768]{6,5,4,3,2,1,0:T(8,128)(2,1)S(1)}, bf16[2,2,1,1,1,40,768]{6,5,4,3,2,1,0:T(8,128)(2,1)S(1)}, u32[]{:S(2)}, u32[]{:S(2)}) %collective-permute-start.31) | collective-permute-done | bytes 245792 | tf_op jit(solution)/shard_map/ppermute | solution.py:29
  417.2 2.7 collective-permute-done.32
  423.1 3.5 collective-permute-done.33
  428.0 4.9 %collective-permute-done.40 = bf16[2,1,32,1152]{3,2,1,0:T(8,128)(2,1)S(1)} collective-permute-done((bf16[2,1,32,1152]{3,2,1,0:T(8,128)(2,1)S(1)}, bf16[2,1,32,1152]{3,2,1,0:T(8,128)(2,1)S(1)}, u32[]{:S(2)}, u32[]{:S(2)}) %collective-permute-start.40) | collective-permute-done | bytes 147488 | tf_op jit(solution)/shard_map/ppermute | solution.py:29
  434.6 4.9 %collective-permute-done.41 = bf16[1,1,32,1152]{3,2,1,0:T(8,128)(2,1)S(1)} collective-permute-done((bf16[1,1,32,1152]{3,2,1,0:T(8,128)(2,1)S(1)}, bf16[1,1,32,1152]{3,2,1,0:T(8,128)(2,1)S(1)}, u32[]{:S(2)}, u32[]{:S(2)}) %collective-permute-start.41) | collective-permute-done | bytes 73760 | tf_op jit(solution)/shard_map/ppermute | solution.py:29
  (397 shorter events, 114.5 us)
Async XLA Ops:
  7.2 112.3 %all-gather.3.cloned.1.call-start = ((), (), s32[]{:S(2)}) async-start(), calls=%async_computation.2 | async-start | bytes 8939520 | tf_op jit(solution)/shard_map/all_gather | solution.py:230
  7.2 8.3 %collective-permute-start.12 = (bf16[1,1,32,1152]{3,2,1,0:T(8,128)(2,1)}, bf16[1,1,32,1152]{3,2,1,0:T(8,128)(2,1)S(1)}, u32[]{:S(2)}, u32[]{:S(2)}) collective-permute-start(bf16[1,1,32,1152]{3,2,1,0:T(8,128)(2,1)} %bitcast.242), channel_id=1, source_target_pairs={{0,16},{8,24},{16,0},{24,8},{1,17},{9,25},{17,1},{25,9},{2,18},{10... | collective-permute-start | bytes 221192 | tf_op jit(solution)/shard_map/ppermute | solution.py:29
  16.4 5.2 %collective-permute-start.13 = (bf16[2,1,32,1152]{3,2,1,0:T(8,128)(2,1)S(1)}, bf16[2,1,32,1152]{3,2,1,0:T(8,128)(2,1)S(1)}, u32[]{:S(2)}, u32[]{:S(2)}) collective-permute-start(bf16[2,1,32,1152]{3,2,1,0:T(8,128)(2,1)S(1)} %pad_maximum_fusion.23), channel_id=1, source_target_pairs={{0,8},{8,0},{16,24},{24,16},{1,9},{9,1},{17,25},{25,17},{2,10},{10... | collective-permute-start | bytes 442376 | tf_op jit(solution)/shard_map/ppermute | solution.py:29
  25.4 401.3 %reduce-scatter.7.cloned.1.call-start = ((), (), s32[]{:S(2)}) async-start(), calls=%async_computation.3 | async-start | bytes 1474560
  25.5 5.2 %collective-permute-start = (bf16[1,1,1,1,1,40,768]{6,5,4,3,2,1,0:T(8,128)(2,1)S(1)}, bf16[1,1,1,1,1,40,768]{6,5,4,3,2,1,0:T(8,128)(2,1)S(1)}, u32[]{:S(2)}, u32[]{:S(2)}) collective-permute-start(bf16[1,1,1,1,1,40,768]{6,5,4,3,2,1,0:T(8,128)(2,1)S(1)} %get-tuple-element.51), channel_id=1, source_target_pairs={{0,16},{8,24},{16,0},{24,8},{1,17},{9,25},{17,1},{25,9},{2,18},{10... | collective-permute-start | bytes 184328 | tf_op jit(solution)/shard_map/ppermute | solution.py:29
  28.2 5.3 %collective-permute-start.5 = (bf16[1,1,1,1,1,40,768]{6,5,4,3,2,1,0:T(8,128)(2,1)S(1)}, bf16[1,1,1,1,1,40,768]{6,5,4,3,2,1,0:T(8,128)(2,1)S(1)}, u32[]{:S(2)}, u32[]{:S(2)}) collective-permute-start(bf16[1,1,1,1,1,40,768]{6,5,4,3,2,1,0:T(8,128)(2,1)S(1)} %get-tuple-element.52), channel_id=1, source_target_pairs={{0,16},{8,24},{16,0},{24,8},{1,17},{9,25},{17,1},{25,9},{2,18},{10... | collective-permute-start | bytes 184328 | tf_op jit(solution)/shard_map/ppermute | solution.py:29
  30.7 6.7 %collective-permute-start.1 = (bf16[2,1,1,1,1,40,768]{6,5,4,3,2,1,0:T(8,128)(2,1)S(1)}, bf16[2,1,1,1,1,40,768]{6,5,4,3,2,1,0:T(8,128)(2,1)S(1)}, u32[]{:S(2)}, u32[]{:S(2)}) collective-permute-start(bf16[2,1,1,1,1,40,768]{6,5,4,3,2,1,0:T(8,128)(2,1)S(1)} %pad_maximum_fusion.25), channel_id=1, source_target_pairs={{0,8},{8,0},{16,24},{24,16},{1,9},{9,1},{17,25},{25,17},{2,10},{10... | collective-permute-start | bytes 368648 | tf_op jit(solution)/shard_map/ppermute | solution.py:29
  33.5 6.6 %collective-permute-start.6 = (bf16[2,1,1,1,1,40,768]{6,5,4,3,2,1,0:T(8,128)(2,1)S(1)}, bf16[2,1,1,1,1,40,768]{6,5,4,3,2,1,0:T(8,128)(2,1)S(1)}, u32[]{:S(2)}, u32[]{:S(2)}) collective-permute-start(bf16[2,1,1,1,1,40,768]{6,5,4,3,2,1,0:T(8,128)(2,1)S(1)} %pad_maximum_fusion.26), channel_id=1, source_target_pairs={{0,8},{8,0},{16,24},{24,16},{1,9},{9,1},{17,25},{25,17},{2,10},{10... | collective-permute-start | bytes 368648 | tf_op jit(solution)/shard_map/ppermute | solution.py:29
  37.5 12.3 %collective-permute-start.2 = (bf16[2,2,1,1,1,40,768]{6,5,4,3,2,1,0:T(8,128)(2,1)S(1)}, bf16[2,2,1,1,1,40,768]{6,5,4,3,2,1,0:T(8,128)(2,1)S(1)}, u32[]{:S(2)}, u32[]{:S(2)}) collective-permute-start(bf16[2,2,1,1,1,40,768]{6,5,4,3,2,1,0:T(8,128)(2,1)S(1)} %pad_maximum_fusion.19), channel_id=1, source_target_pairs={{0,2},{1,3},{2,0},{3,1},{4,6},{5,7},{6,4},{7,5},{8,10},{9,11},{10,... | collective-permute-start | bytes 737288 | tf_op jit(solution)/shard_map/ppermute | solution.py:29
  40.1 14.2 %collective-permute-start.7 = (bf16[2,2,1,1,1,40,768]{6,5,4,3,2,1,0:T(8,128)(2,1)S(1)}, bf16[2,2,1,1,1,40,768]{6,5,4,3,2,1,0:T(8,128)(2,1)S(1)}, u32[]{:S(2)}, u32[]{:S(2)}) collective-permute-start(bf16[2,2,1,1,1,40,768]{6,5,4,3,2,1,0:T(8,128)(2,1)S(1)} %pad_maximum_fusion.20), channel_id=1, source_target_pairs={{0,4},{1,5},{2,6},{3,7},{4,0},{5,1},{6,2},{7,3},{8,12},{9,13},{10,... | collective-permute-start | bytes 737288 | tf_op jit(solution)/shard_map/ppermute | solution.py:29
  49.8 24.0 %collective-permute-start.3 = (bf16[2,2,1,2,1,40,768]{6,5,4,3,2,1,0:T(8,128)(2,1)S(1)}, bf16[2,2,1,2,1,40,768]{6,5,4,3,2,1,0:T(8,128)(2,1)S(1)}, u32[]{:S(2)}, u32[]{:S(2)}) collective-permute-start(bf16[2,2,1,2,1,40,768]{6,5,4,3,2,1,0:T(8,128)(2,1)S(1)} %pad_maximum_fusion.13), channel_id=1, source_target_pairs={{0,4},{1,5},{2,6},{3,7},{4,0},{5,1},{6,2},{7,3},{8,12},{9,13},{10,... | collective-permute-start | bytes 1474568 | tf_op jit(solution)/shard_map/ppermute | solution.py:29
  54.4 19.7 %collective-permute-start.8 = (bf16[2,2,2,1,1,40,768]{6,5,4,3,2,1,0:T(8,128)(2,1)S(1)}, bf16[2,2,2,1,1,40,768]{6,5,4,3,2,1,0:T(8,128)(2,1)S(1)}, u32[]{:S(2)}, u32[]{:S(2)}) collective-permute-start(bf16[2,2,2,1,1,40,768]{6,5,4,3,2,1,0:T(8,128)(2,1)S(1)} %pad_maximum_fusion.14), channel_id=1, source_target_pairs={{0,2},{1,3},{2,0},{3,1},{4,6},{5,7},{6,4},{7,5},{8,10},{9,11},{10,... | collective-permute-start | bytes 1474568 | tf_op jit(solution)/shard_map/ppermute | solution.py:29
  74.1 3.8 collective-permute-start.9
  82.4 9.4 %collective-permute-start.10 = (bf16[1,1,128,512]{3,2,1,0:T(8,128)(2,1)S(1)}, bf16[1,1,128,512]{3,2,1,0:T(8,128)(2,1)S(1)}, u32[]{:S(2)}, u32[]{:S(2)}) collective-permute-start(bf16[1,1,128,512]{3,2,1,0:T(8,128)(2,1)S(1)} %maximum_bitcast_fusion), channel_id=1, source_target_pairs={{0,16},{8,24},{16,0},{24,8},{1,17},{9,25},{17,1},{25,9},{2,18},{10... | collective-permute-start | bytes 393224 | tf_op jit(solution)/shard_map/ppermute | solution.py:29
  92.5 28.7 %collective-permute-start.11 = (bf16[2,1,128,512]{3,2,1,0:T(8,128)(2,1)}, bf16[2,1,128,512]{3,2,1,0:T(8,128)(2,1)}, u32[]{:S(2)}, u32[]{:S(2)}) collective-permute-start(bf16[2,1,128,512]{3,2,1,0:T(8,128)(2,1)} %pad_maximum_fusion.17), channel_id=1, source_target_pairs={{0,8},{8,0},{16,24},{24,16},{1,9},{9,1},{17,25},{25,17},{2,10},{10... | collective-permute-start | bytes 786440 | tf_op jit(solution)/shard_map/ppermute | solution.py:29
  120.9 6.9 %collective-permute-start.14 = (bf16[1,4,128,1152]{3,2,1,0:T(8,128)(2,1)S(1)}, bf16[1,4,128,1152]{3,2,1,0:T(8,128)(2,1)}, u32[]{:S(2)}, u32[]{:S(2)}) collective-permute-start(bf16[1,4,128,1152]{3,2,1,0:T(8,128)(2,1)S(1)} %slice_bitcast_fusion), channel_id=1, source_target_pairs={{0,1},{1,0},{2,3},{3,2},{4,5},{5,4},{6,7},{7,6},{8,9},{9,8},{10,11... | collective-permute-start | bytes 3538952 | tf_op jit(solution)/shard_map/ppermute | solution.py:29
  131.9 16.6 %collective-permute-start.15 = (bf16[1,1,1,128,1152]{4,3,2,1,0:T(8,128)(2,1)S(1)}, bf16[1,1,1,128,1152]{4,3,2,1,0:T(8,128)(2,1)S(1)}, u32[]{:S(2)}, u32[]{:S(2)}) collective-permute-start(bf16[1,1,1,128,1152]{4,3,2,1,0:T(8,128)(2,1)S(1)} %fusion.44), channel_id=1, source_target_pairs={{0,16},{8,24},{16,0},{24,8},{1,17},{9,25},{17,1},{25,9},{2,18},{10... | collective-permute-start | bytes 884744 | tf_op jit(solution)/shard_map/ppermute | solution.py:29
  148.6 14.8 %collective-permute-start.16 = (bf16[2,1,1,128,1152]{4,3,2,1,0:T(8,128)(2,1)S(1)}, bf16[2,1,1,128,1152]{4,3,2,1,0:T(8,128)(2,1)S(1)}, u32[]{:S(2)}, u32[]{:S(2)}) collective-permute-start(bf16[2,1,1,128,1152]{4,3,2,1,0:T(8,128)(2,1)S(1)} %pad_maximum_fusion.10), channel_id=1, source_target_pairs={{0,8},{8,0},{16,24},{24,16},{1,9},{9,1},{17,25},{25,17},{2,10},{10... | collective-permute-start | bytes 1769480 | tf_op jit(solution)/shard_map/ppermute | solution.py:29
  163.5 2.9 collective-permute-start.17
  185.3 2.9 collective-permute-start.18
  188.5 15.7 %collective-permute-start.19 = (bf16[2,1,1,128,1152]{4,3,2,1,0:T(8,128)(2,1)S(1)}, bf16[2,1,1,128,1152]{4,3,2,1,0:T(8,128)(2,1)S(1)}, u32[]{:S(2)}, u32[]{:S(2)}) collective-permute-start(bf16[2,1,1,128,1152]{4,3,2,1,0:T(8,128)(2,1)S(1)} %slice.605), channel_id=1, source_target_pairs={{0,8},{8,0},{16,24},{24,16},{1,9},{9,1},{17,25},{25,17},{2,10},{10... | collective-permute-start | bytes 1769480 | tf_op jit(solution)/shard_map/ppermute | solution.py:29
  204.3 15.7 %collective-permute-start.20 = (bf16[1,1,1,128,1152]{4,3,2,1,0:T(8,128)(2,1)S(1)}, bf16[1,1,1,128,1152]{4,3,2,1,0:T(8,128)(2,1)S(1)}, u32[]{:S(2)}, u32[]{:S(2)}) collective-permute-start(bf16[1,1,1,128,1152]{4,3,2,1,0:T(8,128)(2,1)S(1)} %slice.609), channel_id=1, source_target_pairs={{0,16},{8,24},{16,0},{24,8},{1,17},{9,25},{17,1},{25,9},{2,18},{10... | collective-permute-start | bytes 884744 | tf_op jit(solution)/shard_map/ppermute | solution.py:29
  222.2 15.0 %collective-permute-start.21 = (bf16[1,1,1,128,1152]{4,3,2,1,0:T(8,128)(2,1)S(1)}, bf16[1,1,1,128,1152]{4,3,2,1,0:T(8,128)(2,1)S(1)}, u32[]{:S(2)}, u32[]{:S(2)}) collective-permute-start(bf16[1,1,1,128,1152]{4,3,2,1,0:T(8,128)(2,1)S(1)} %fusion.33), channel_id=1, source_target_pairs={{0,16},{8,24},{16,0},{24,8},{1,17},{9,25},{17,1},{25,9},{2,18},{10... | collective-permute-start | bytes 884744 | tf_op jit(solution)/shard_map/ppermute | solution.py:29
  237.3 13.3 %collective-permute-start.22 = (bf16[2,1,1,128,1152]{4,3,2,1,0:T(8,128)(2,1)S(1)}, bf16[2,1,1,128,1152]{4,3,2,1,0:T(8,128)(2,1)S(1)}, u32[]{:S(2)}, u32[]{:S(2)}) collective-permute-start(bf16[2,1,1,128,1152]{4,3,2,1,0:T(8,128)(2,1)S(1)} %pad_maximum_fusion.11), channel_id=1, source_target_pairs={{0,8},{8,0},{16,24},{24,16},{1,9},{9,1},{17,25},{25,17},{2,10},{10... | collective-permute-start | bytes 1769480 | tf_op jit(solution)/shard_map/ppermute | solution.py:29
  250.7 2.9 collective-permute-start.23
  265.2 2.9 collective-permute-start.24
  268.5 15.4 %collective-permute-start.25 = (bf16[2,1,1,128,1152]{4,3,2,1,0:T(8,128)(2,1)S(1)}, bf16[2,1,1,128,1152]{4,3,2,1,0:T(8,128)(2,1)S(1)}, u32[]{:S(2)}, u32[]{:S(2)}) collective-permute-start(bf16[2,1,1,128,1152]{4,3,2,1,0:T(8,128)(2,1)S(1)} %slice.604), channel_id=1, source_target_pairs={{0,8},{8,0},{16,24},{24,16},{1,9},{9,1},{17,25},{25,17},{2,10},{10... | collective-permute-start | bytes 1769480 | tf_op jit(solution)/shard_map/ppermute | solution.py:29
  284.1 15.5 %collective-permute-start.26 = (bf16[1,1,1,128,1152]{4,3,2,1,0:T(8,128)(2,1)S(1)}, bf16[1,1,1,128,1152]{4,3,2,1,0:T(8,128)(2,1)S(1)}, u32[]{:S(2)}, u32[]{:S(2)}) collective-permute-start(bf16[1,1,1,128,1152]{4,3,2,1,0:T(8,128)(2,1)S(1)} %slice.608), channel_id=1, source_target_pairs={{0,16},{8,24},{16,0},{24,8},{1,17},{9,25},{17,1},{25,9},{2,18},{10... | collective-permute-start | bytes 884744 | tf_op jit(solution)/shard_map/ppermute | solution.py:29
  303.3 2.9 collective-permute-start.39
  307.5 132.6 %reduce-scatter.9.cloned.1.call-start = ((), (), s32[]{:S(2)}) async-start(), calls=%async_computation.4 | async-start | bytes 7464960
  335.7 8.4 %collective-permute-start.27 = (bf16[2,1,128,512]{3,2,1,0:T(8,128)(2,1)S(1)}, bf16[2,1,128,512]{3,2,1,0:T(8,128)(2,1)S(1)}, u32[]{:S(2)}, u32[]{:S(2)}) collective-permute-start(bf16[2,1,128,512]{3,2,1,0:T(8,128)(2,1)S(1)} %slice.610), channel_id=1, source_target_pairs={{0,8},{8,0},{16,24},{24,16},{1,9},{9,1},{17,25},{25,17},{2,10},{10... | collective-permute-start | bytes 786440 | tf_op jit(solution)/shard_map/ppermute | solution.py:29
  345.3 8.5 %collective-permute-start.28 = (bf16[1,1,128,512]{3,2,1,0:T(8,128)(2,1)S(1)}, bf16[1,1,128,512]{3,2,1,0:T(8,128)(2,1)S(1)}, u32[]{:S(2)}, u32[]{:S(2)}) collective-permute-start(bf16[1,1,128,512]{3,2,1,0:T(8,128)(2,1)S(1)} %slice.613), channel_id=1, source_target_pairs={{0,16},{8,24},{16,0},{24,8},{1,17},{9,25},{17,1},{25,9},{2,18},{10... | collective-permute-start | bytes 393224 | tf_op jit(solution)/shard_map/ppermute | solution.py:29
  367.8 4.0 collective-permute-start.43
  369.5 11.4 %collective-permute-start.29 = (bf16[2,2,2,2,1,40,768]{6,5,4,3,2,1,0:T(8,128)(2,1)S(1)}, bf16[2,2,2,2,1,40,768]{6,5,4,3,2,1,0:T(8,128)(2,1)S(1)}, u32[]{:S(2)}, u32[]{:S(2)}) collective-permute-start(bf16[2,2,2,2,1,40,768]{6,5,4,3,2,1,0:T(8,128)(2,1)S(1)} %get-tuple-element.37), channel_id=1, source_target_pairs={{0,1},{1,0},{2,3},{3,2},{4,5},{5,4},{6,7},{7,6},{8,9},{9,8},{10,11... | collective-permute-start | bytes 2949128 | tf_op jit(solution)/shard_map/ppermute | solution.py:29
  369.8 11.1 %collective-permute-start.34 = (bf16[2,2,2,2,1,40,768]{6,5,4,3,2,1,0:T(8,128)(2,1)S(1)}, bf16[2,2,2,2,1,40,768]{6,5,4,3,2,1,0:T(8,128)(2,1)S(1)}, u32[]{:S(2)}, u32[]{:S(2)}) collective-permute-start(bf16[2,2,2,2,1,40,768]{6,5,4,3,2,1,0:T(8,128)(2,1)S(1)} %get-tuple-element.38), channel_id=1, source_target_pairs={{0,1},{1,0},{2,3},{3,2},{4,5},{5,4},{6,7},{7,6},{8,9},{9,8},{10,11... | collective-permute-start | bytes 2949128 | tf_op jit(solution)/shard_map/ppermute | solution.py:29
  371.9 3.9 collective-permute-start.44
  375.8 3.6 collective-permute-start.45
  379.4 4.5 collective-permute-start.46
  381.5 19.7 %collective-permute-start.30 = (bf16[2,2,1,2,1,40,768]{6,5,4,3,2,1,0:T(8,128)(2,1)S(1)}, bf16[2,2,1,2,1,40,768]{6,5,4,3,2,1,0:T(8,128)(2,1)S(1)}, u32[]{:S(2)}, u32[]{:S(2)}) collective-permute-start(bf16[2,2,1,2,1,40,768]{6,5,4,3,2,1,0:T(8,128)(2,1)S(1)} %slice.607), channel_id=1, source_target_pairs={{0,4},{1,5},{2,6},{3,7},{4,0},{5,1},{6,2},{7,3},{8,12},{9,13},{10,... | collective-permute-start | bytes 1474568 | tf_op jit(solution)/shard_map/ppermute | solution.py:29
  384.6 22.5 %collective-permute-start.35 = (bf16[2,2,2,1,1,40,768]{6,5,4,3,2,1,0:T(8,128)(2,1)S(1)}, bf16[2,2,2,1,1,40,768]{6,5,4,3,2,1,0:T(8,128)(2,1)S(1)}, u32[]{:S(2)}, u32[]{:S(2)}) collective-permute-start(bf16[2,2,2,1,1,40,768]{6,5,4,3,2,1,0:T(8,128)(2,1)S(1)} %slice.606), channel_id=1, source_target_pairs={{0,2},{1,3},{2,0},{3,1},{4,6},{5,7},{6,4},{7,5},{8,10},{9,11},{10,... | collective-permute-start | bytes 1474568 | tf_op jit(solution)/shard_map/ppermute | solution.py:29
  401.3 13.6 %collective-permute-start.31 = (bf16[2,2,1,1,1,40,768]{6,5,4,3,2,1,0:T(8,128)(2,1)S(1)}, bf16[2,2,1,1,1,40,768]{6,5,4,3,2,1,0:T(8,128)(2,1)S(1)}, u32[]{:S(2)}, u32[]{:S(2)}) collective-permute-start(bf16[2,2,1,1,1,40,768]{6,5,4,3,2,1,0:T(8,128)(2,1)S(1)} %slice.612), channel_id=1, source_target_pairs={{0,2},{1,3},{2,0},{3,1},{4,6},{5,7},{6,4},{7,5},{8,10},{9,11},{10,... | collective-permute-start | bytes 737288 | tf_op jit(solution)/shard_map/ppermute | solution.py:29
  407.2 9.3 %collective-permute-start.36 = (bf16[2,2,1,1,1,40,768]{6,5,4,3,2,1,0:T(8,128)(2,1)S(1)}, bf16[2,2,1,1,1,40,768]{6,5,4,3,2,1,0:T(8,128)(2,1)S(1)}, u32[]{:S(2)}, u32[]{:S(2)}) collective-permute-start(bf16[2,2,1,1,1,40,768]{6,5,4,3,2,1,0:T(8,128)(2,1)S(1)} %slice.611), channel_id=1, source_target_pairs={{0,4},{1,5},{2,6},{3,7},{4,0},{5,1},{6,2},{7,3},{8,12},{9,13},{10,... | collective-permute-start | bytes 737288 | tf_op jit(solution)/shard_map/ppermute | solution.py:29
  415.0 5.0 %collective-permute-start.32 = (bf16[2,1,1,1,1,40,768]{6,5,4,3,2,1,0:T(8,128)(2,1)S(1)}, bf16[2,1,1,1,1,40,768]{6,5,4,3,2,1,0:T(8,128)(2,1)S(1)}, u32[]{:S(2)}, u32[]{:S(2)}) collective-permute-start(bf16[2,1,1,1,1,40,768]{6,5,4,3,2,1,0:T(8,128)(2,1)S(1)} %slice.615), channel_id=1, source_target_pairs={{0,8},{8,0},{16,24},{24,16},{1,9},{9,1},{17,25},{25,17},{2,10},{10... | collective-permute-start | bytes 368648 | tf_op jit(solution)/shard_map/ppermute | solution.py:29
  416.5 4.9 %collective-permute-start.37 = (bf16[2,1,1,1,1,40,768]{6,5,4,3,2,1,0:T(8,128)(2,1)S(1)}, bf16[2,1,1,1,1,40,768]{6,5,4,3,2,1,0:T(8,128)(2,1)S(1)}, u32[]{:S(2)}, u32[]{:S(2)}) collective-permute-start(bf16[2,1,1,1,1,40,768]{6,5,4,3,2,1,0:T(8,128)(2,1)S(1)} %slice.614), channel_id=1, source_target_pairs={{0,8},{8,0},{16,24},{24,16},{1,9},{9,1},{17,25},{25,17},{2,10},{10... | collective-permute-start | bytes 368648 | tf_op jit(solution)/shard_map/ppermute | solution.py:29
  420.0 6.6 %collective-permute-start.33 = (bf16[1,1,1,1,1,40,768]{6,5,4,3,2,1,0:T(8,128)(2,1)S(1)}, bf16[1,1,1,1,1,40,768]{6,5,4,3,2,1,0:T(8,128)(2,1)S(1)}, u32[]{:S(2)}, u32[]{:S(2)}) collective-permute-start(bf16[1,1,1,1,1,40,768]{6,5,4,3,2,1,0:T(8,128)(2,1)S(1)} %slice.620), channel_id=1, source_target_pairs={{0,16},{8,24},{16,0},{24,8},{1,17},{9,25},{17,1},{25,9},{2,18},{10... | collective-permute-start | bytes 184328 | tf_op jit(solution)/shard_map/ppermute | solution.py:29
  421.5 6.5 %collective-permute-start.38 = (bf16[1,1,1,1,1,40,768]{6,5,4,3,2,1,0:T(8,128)(2,1)S(1)}, bf16[1,1,1,1,1,40,768]{6,5,4,3,2,1,0:T(8,128)(2,1)S(1)}, u32[]{:S(2)}, u32[]{:S(2)}) collective-permute-start(bf16[1,1,1,1,1,40,768]{6,5,4,3,2,1,0:T(8,128)(2,1)S(1)} %slice.619), channel_id=1, source_target_pairs={{0,16},{8,24},{16,0},{24,8},{1,17},{9,25},{17,1},{25,9},{2,18},{10... | collective-permute-start | bytes 184328 | tf_op jit(solution)/shard_map/ppermute | solution.py:29
  427.6 5.2 %collective-permute-start.40 = (bf16[2,1,32,1152]{3,2,1,0:T(8,128)(2,1)S(1)}, bf16[2,1,32,1152]{3,2,1,0:T(8,128)(2,1)S(1)}, u32[]{:S(2)}, u32[]{:S(2)}) collective-permute-start(bf16[2,1,32,1152]{3,2,1,0:T(8,128)(2,1)S(1)} %slice.469), channel_id=1, source_target_pairs={{0,8},{8,0},{16,24},{24,16},{1,9},{9,1},{17,25},{25,17},{2,10},{10... | collective-permute-start | bytes 442376 | tf_op jit(solution)/shard_map/ppermute | solution.py:29
  433.8 5.7 %collective-permute-start.41 = (bf16[1,1,32,1152]{3,2,1,0:T(8,128)(2,1)S(1)}, bf16[1,1,32,1152]{3,2,1,0:T(8,128)(2,1)S(1)}, u32[]{:S(2)}, u32[]{:S(2)}) collective-permute-start(bf16[1,1,32,1152]{3,2,1,0:T(8,128)(2,1)S(1)} %slice.616), channel_id=1, source_target_pairs={{0,16},{8,24},{16,0},{24,8},{1,17},{9,25},{17,1},{25,9},{2,18},{10... | collective-permute-start | bytes 221192 | tf_op jit(solution)/shard_map/ppermute | solution.py:29
  (74 other events, 778.2 us)
Sparse Core Ops, SparseCore 0:
  25.5 93.9 all-gather.2
  307.7 28.3 reduce-scatter.6
  339.0 79.0 reduce-scatter.8

commit v3 on v2

--- a/solution.py
+++ b/solution.py
@@ -37,14 +37,6 @@
     own = lax.slice_in_dim(value, 0, 1, axis=at)
     other = lax.slice_in_dim(value, 1, 2, axis=at).astype(jnp.bfloat16)
     return own.astype(jnp.float32) + swapped(other, axis, bit).astype(jnp.float32)
-
-
-def scatter_sum(value, stages):
-    for axis, bit, at in stages:
-        own = lax.slice_in_dim(value, 0, 1, axis=at)
-        other = lax.slice_in_dim(value, 1, 2, axis=at)
-        value = own + swapped(other, axis, bit)
-    return value.reshape(value.shape[len(stages) :])
 
 
 def gather_xor(value, stages):
@@ -187,10 +179,10 @@
     all_down = seq_stages + chip_stages[::-1] + core_stage
     dp_count = lax.axis_size("dp")
     chips = dp_count // 2
-    planes = [[2 * chip + core for chip in range(chips)] for core in range(2)]
+    plane_up = [("dp", bit, nchip - 1 - k) for k, bit in enumerate(chip_bits)]
+    plane_down = plane_up[::-1]
+    cut = (width // 256) * 128 + (128 if width % 256 else 0)
     kv_stages = seq_stages
-    seq_stages_only = seq_stages
-    token_stages = seq_stages + [("dp", 1, nseq)]
     keys = seq_count * rows
     scale = 1.0 / math.sqrt(HEAD_DIM)
     block_id = lax.axis_index("seq")
@@ -199,7 +191,7 @@
     chip_off = jnp.arange(chips, dtype=jnp.int32)
     core_off = jnp.arange(2, dtype=jnp.int32)
     qkv_own = w_qkv.shape[0]
-    qkv_pad = (qkv_own + 7) // 8 * 8
+    qkv_pad = (qkv_own + 8) // 8 * 8
     out_own = w_out.shape[0]
     ffn_own = w_gate.shape[0]
     half = w_qkv.shape[1] // 2
@@ -211,8 +203,8 @@
     lane = jnp.arange(qkv_pad, dtype=jnp.int32)[None, :]
     qkv_origin = jnp.where(lane < qkv_own, qkv_dev * qkv_own + lane, -1).reshape(-1)
     out_dev = (
-        (block_id ^ seq_off)[None, None, :] * dp_count
-        + chip_off[None, :, None] * 2
+        seq_off[None, :, None] * dp_count
+        + ((dp_id // 2) ^ chip_off)[None, None, :] * 2
         + ((dp_id % 2) ^ core_off)[:, None, None]
     ).reshape(-1, 1)
     out_origin = (out_dev * out_own + jnp.arange(out_own, dtype=jnp.int32)[None, :]).reshape(-1)
@@ -226,17 +218,16 @@
         ],
         axis=-1,
     ).reshape(-1, 2 * half)
-    out_column = gather_xor(w_out, seq_stages_only).reshape(-1, width)
-    plane_rows = lax.all_gather(
+    out_column = gather_xor(w_out, plane_up).reshape(-1, width)
+    line_rows = lax.all_gather(
         jnp.concatenate([w_gate, w_up, w_down, out_column], axis=0),
-        "dp",
-        axis_index_groups=planes,
+        "seq",
         axis=0,
     )
     gate_full, up_full, down_full = (
-        plane_rows[:, i * ffn_own : (i + 1) * ffn_own].reshape(-1, width) for i in range(3)
-    )
-    out_full = mine_first(plane_rows[None, :, 3 * ffn_own :], "dp", 1, 0).reshape(-1, width)
+        line_rows[:, i * ffn_own : (i + 1) * ffn_own].reshape(-1, width) for i in range(3)
+    )
+    out_full = mine_first(line_rows[None, :, 3 * ffn_own :], "dp", 1, 0).reshape(-1, width)
     starts = jnp.cumsum(lens) - lens
     own_index = block_id * rows + jnp.arange(rows, dtype=jnp.int32)
     key_index = (
@@ -287,29 +278,47 @@
     root_ffn = inv_root(hidden_in)
     unit_ffn = hidden_in * root_ffn
     ffn_input = (unit_ffn * g_ffn_in).astype(jnp.bfloat16)
-    slots = (2,) * len(token_stages)
-    tokens_b = gather_xor(ffn_input, token_stages).reshape(-1, width)
+
+    def gather_tokens(value):
+        both = jnp.concatenate(
+            [gather_xor(value[:, :cut], plane_up), gather_xor(value[:, cut:], plane_down)], axis=-1
+        )
+        return mine_first(both[None], "dp", 1, 0).reshape(-1, width)
+
+    def scatter_tokens(value):
+        value = keep_half(value.reshape((2,) * (1 + nchip) + (rows, width)), "dp", 1, 0)[0]
+        return jnp.concatenate(
+            [
+                scatter_xor(value[..., :cut], plane_down),
+                scatter_xor(value[..., cut:], plane_up),
+            ],
+            axis=-1,
+        )
+
+    tokens_b = gather_tokens(ffn_input)
     out_part, gate_all, up_all = ffn_forward_fold(tokens_b, (gate_full, up_full, down_full))
-    ffn_out = scatter_xor(out_part.reshape(slots + (rows, width)), token_stages[::-1])
+    ffn_out = scatter_tokens(out_part)
     root_out = inv_root(ffn_out)
     unit_out = ffn_out * root_out
     result = hidden_in + unit_out * g_ffn_out
     grad_g_ffn_out = jnp.sum(rows_grad * unit_out, axis=0)
     ffn_grad_b = norm_back(rows_grad, unit_out, root_out, g_ffn_out).astype(jnp.bfloat16)
-    grads_b = gather_xor(ffn_grad_b, token_stages).reshape(-1, width)
+    grads_b = gather_tokens(ffn_grad_b)
     in_part, dgate_all, dup_all = ffn_backward_fold(
         grads_b, gate_all, up_all, (gate_full, up_full, down_full)
     )
-    ffn_in_grad = scatter_xor(in_part.reshape(slots + (rows, width)), token_stages[::-1])
+    ffn_in_grad = scatter_tokens(in_part)
     terms = ffn_weight_terms(tokens_b, grads_b, gate_all, up_all, dgate_all, dup_all)
-    ffn_terms = lax.psum_scatter(
-        jnp.concatenate(
-            [term.astype(jnp.bfloat16).reshape(chips, ffn_own, width) for term in terms], axis=1
-        ),
-        "dp",
-        axis_index_groups=planes,
-        scatter_dimension=0,
-    ).astype(jnp.float32)
+    ffn_in_grad, term_rows = lax.optimization_barrier(
+        (
+            ffn_in_grad,
+            jnp.concatenate(
+                [term.astype(jnp.bfloat16).reshape(seq_count, ffn_own, width) for term in terms],
+                axis=1,
+            ),
+        )
+    )
+    ffn_terms = lax.psum_scatter(term_rows, "seq", scatter_dimension=0).astype(jnp.float32)
     ffn_terms = ffn_terms.reshape(3, ffn_own, width)
     grad_w_gate, grad_w_up, grad_w_down = ffn_terms[0], ffn_terms[1], ffn_terms[2]
     grad_g_ffn_in = jnp.sum(ffn_in_grad * unit_ffn, axis=0)
@@ -318,15 +327,14 @@
     attn_grad_b = norm_back(hidden_grad_in, unit_post, root_post, g_attn_out).astype(jnp.bfloat16)
     mixed_grad_slots = contract_cols(attn_grad_b, out_full).astype(jnp.bfloat16)
     mixed_grad_b = contract_cols(mixed_grad_slots, out_order).astype(jnp.bfloat16)
-    out_term = contract_rows(mixed_slots, attn_grad_b).reshape(2, chips, -1, width)
-    out_plane = lax.psum_scatter(
+    out_term = contract_rows(mixed_slots, attn_grad_b).reshape(2, seq_count, -1, width)
+    out_line = lax.psum_scatter(
         keep_half(out_term, "dp", 1, 0)[0].astype(jnp.bfloat16),
-        "dp",
-        axis_index_groups=planes,
+        "seq",
         scatter_dimension=0,
     ).astype(jnp.float32)
     owned_out = scatter_xor(
-        out_plane.reshape((2,) * nseq + w_out.shape), seq_stages[::-1]
+        out_line.reshape((2,) * nchip + w_out.shape), plane_down
     )
     mixed_grad3 = mixed_grad_b.reshape(rows, HEADS, HEAD_DIM)
     delta = jnp.sum(
@@ -375,15 +383,14 @@
     gains = [grad_g_attn_in, grad_g_attn_out, grad_g_ffn_in, grad_g_ffn_out, grad_g_query, grad_g_key]
     gain_terms = jnp.concatenate([g.reshape(count, -1) for g in gains], axis=1)
     qkv_term = contract_rows(attn_slots, qkv_grad_b).reshape(spread + (qkv_pad, 2 * half))
-    owned_qkv = jnp.concatenate(
-        [
-            scatter_xor(qkv_term[..., :half], all_up[::-1]),
-            scatter_xor(qkv_term[..., half:], all_down[::-1]),
-        ],
-        axis=-1,
-    )[:qkv_own]
     gain_slots = jnp.take(gain_terms, qkv_dev.reshape(-1), axis=0)
-    owned = scatter_sum(gain_slots.reshape(spread + (-1,)), all_up[::-1])
+    left_term = qkv_term[..., :half].at[..., qkv_own, : gain_slots.shape[1]].set(
+        gain_slots.reshape(spread + (-1,))
+    )
+    left_owned = scatter_xor(left_term, all_up[::-1])
+    right_owned = scatter_xor(qkv_term[..., half:], all_down[::-1])
+    owned_qkv = jnp.concatenate([left_owned, right_owned], axis=-1)[:qkv_own]
+    owned = left_owned[qkv_own]
     own_width, own_head = width // count, HEAD_DIM // count
     owned_gains = [owned[i * own_width : (i + 1) * own_width] for i in range(4)]
     owned_heads = [

time: 454 us -> 453 us (level)
  waiting for transfers between devices: 263 us -> 240 us
  starting transfers between devices: 51.7 us -> 61.5 us
  other arithmetic: 37.8 us -> 47.1 us
  local copies, waits for them, and re-layouts: 26 us -> 32.6 us
    ppermute x47 -> x50, waiting for transfers between devices: 237 us -> 145 us  [swapped(): return lax.ppermute(value, axis, [(i, i ^ bit) for i in range(length)])]
    all_gather x1, waiting for transfers between devices: 26.4 us -> 74.9 us  [local(): lax.all_gather(jnp.concatenate([w_gate, w_up, w_down, out_column], axis=0...]
    unnamed x5 -> x4, waiting for transfers between devices: 0.07 us -> 20 us
    ppermute x47 -> x50, starting transfers between devices: 51.2 us -> 61.4 us  [swapped(): return lax.ppermute(value, axis, [(i, i ^ bit) for i in range(length)])]
    dot_general x1 -> x0, local copies, waits for them, and re-layouts: 5.47 us -> none  [dot32(): return jnp.dot(left, right, preferred_element_type=jnp.float32)]
  transfers between devices with their start and end apart: 50 -> 53, of which waited for: 39 -> 43; matrix products, arithmetic and copies ran while one was open for 15% -> 19% of each run, Pallas kernels for 0% -> 0%
where the time goes in v3:
time: 453 us; the launch traced here: 449 us
  waiting for transfers between devices  240 us (53%)
  starting transfers between devices  61.5 us (14%)
  matrix products  52.4 us (12%)
  other arithmetic  47.1 us (10%)
  local copies, waits for them, and re-layouts  32.6 us (7%)
  between operations  15.6 us (3%)
    ppermute x50, waiting for transfers between devices, swapped(): return lax.ppermute(value, axis, [(i, i ^ bit) for i in range(length)])  145 us
    all_gather x1, waiting for transfers between devices, local(): lax.all_gather(jnp.concatenate([w_gate, w_up, w_down, out_column], axis=0...  74.9 us
    ppermute x50, starting transfers between devices, swapped(): return lax.ppermute(value, axis, [(i, i ^ bit) for i in range(length)])  61.4 us
    unnamed x4, waiting for transfers between devices  20 us
    dot_general x5, matrix products, contract_cols(): lax.dot_general(left, right, (((1,), (1,)), ((), ())), preferred_element_...  17.2 us
    dot_general x7, matrix products, dot32(): return jnp.dot(left, right, preferred_element_type=jnp.float32)  14.1 us
    dot_general x5, matrix products, contract_rows(): lax.dot_general(left, right, (((0,), (0,)), ((), ())), preferred_element_...  9.39 us
  transfers between devices with their start and end apart: 53, of which 43 were waited for; matrix products, arithmetic and copies ran while one was open for 19% of the time, Pallas kernels for 0%

profile of v3, /device:TPU:0, one launch (start us, length us, event | category | flops | bytes accessed | tf_op | source)
XLA Modules:
  0.0 448.9 jit_solution(9475362312864600727)
XLA Ops:
  7.2 3.0 collective-permute-start.12
  10.3 2.5 collective-permute-done.12
  15.8 3.1 collective-permute-done.13
  19.9 2.7 pad_maximum_fusion.4
  22.7 3.2 collective-permute-start
  41.1 2.5 collective-permute-start.3
  47.6 3.4 collective-permute-done.3
  51.2 3.5 collective-permute-done.8
  64.0 20.4 %collective-permute-done.10 = bf16[1,1,128,512]{3,2,1,0:T(8,128)(2,1)S(1)} collective-permute-done((bf16[1,1,128,512]{3,2,1,0:T(8,128)(2,1)S(1)}, bf16[1,1,128,512]{3,2,1,0:T(8,128)(2,1)S(1)}, u32[]{:S(2)}, u32[]{:S(2)}) %collective-permute-start.10) | collective-permute-done | bytes 131104 | tf_op jit(solution)/shard_map/ppermute | solution.py:29
  85.2 74.9 %all-gather.3.cloned.1.call-done = bf16[3104,1152]{1,0:T(8,128)(2,1)} async-done(((bf16[776,1152]{1,0:T(8,128)(2,1)}), bf16[3104,1152]{1,0:T(8,128)(2,1)}) %all-gather.3.cloned.1.call-update) | async-done | bytes 7151632 | tf_op jit(solution)/shard_map/all_gather | solution.py:222
  176.4 3.6 collective-permute-done.15
  183.1 6.1 %collective-permute-done.18 = bf16[2,1,128,512]{3,2,1,0:T(8,128)(2,1)S(1)} collective-permute-done((bf16[2,1,128,512]{3,2,1,0:T(8,128)(2,1)S(1)}, bf16[2,1,128,512]{3,2,1,0:T(8,128)(2,1)S(1)}, u32[]{:S(2)}, u32[]{:S(2)}) %collective-permute-start.18) | collective-permute-done | bytes 262176 | tf_op jit(solution)/shard_map/ppermute | solution.py:29
  192.6 2.5 fusion.73
  195.1 3.0 multiply_convert_fusion.1
  198.1 3.4 fusion.74
  202.0 2.6 collective-permute-done.20
  208.1 5.3 %collective-permute-done.23 = bf16[2,1,128,512]{3,2,1,0:T(8,128)(2,1)S(1)} collective-permute-done((bf16[2,1,128,512]{3,2,1,0:T(8,128)(2,1)S(1)}, bf16[2,1,128,512]{3,2,1,0:T(8,128)(2,1)S(1)}, u32[]{:S(2)}, u32[]{:S(2)}) %collective-permute-start.23) | collective-permute-done | bytes 262176 | tf_op jit(solution)/shard_map/ppermute | solution.py:29
  218.9 3.3 collective-permute-done.22
  225.8 3.8 collective-permute-done.25
  232.9 5.6 %collective-permute-done.28 = bf16[2,1,128,512]{3,2,1,0:T(8,128)(2,1)S(1)} collective-permute-done((bf16[2,1,128,512]{3,2,1,0:T(8,128)(2,1)S(1)}, bf16[2,1,128,512]{3,2,1,0:T(8,128)(2,1)S(1)}, u32[]{:S(2)}, u32[]{:S(2)}) %collective-permute-start.28) | collective-permute-done | bytes 262176 | tf_op jit(solution)/shard_map/ppermute | solution.py:29
  238.7 2.8 collective-permute-done.29
  241.8 4.8 %multiply_convert_fusion = (bf16[1024,864]{0,1:T(8,128)(2,1)S(1)}, bf16[1024,864]{0,1:T(8,128)(2,1)S(1)}) fusion(f32[1024,864]{0,1:T(8,128)S(1)} %fusion.73, f32[1024,864]{0,1:T(8,128)S(1)} %get-tuple-element.91, bf16[1024,1152]{1,0:T(8,128)(2,1)S(1)} %bitcast.225, bf16[864,1152]{1,0:T(8,128)(2,1)S(1)} %bitcast.232), kind=kOutput, calls=%fused_computation.20 | convolution fusion | flops 2058780672 | bytes 14966784 | tf_op jit(solution)/shard_map/dot_general | solution.py:114
  246.6 3.0 fusion.75
  249.5 3.1 convolution_add_fusion
  253.0 2.5 convolution_convert_fusion.2
  258.0 2.5 convolution_convert_fusion
  265.2 3.3 pad_maximum_fusion
  268.5 3.4 collective-permute-done.33
  279.0 3.1 collective-permute-done.32
  285.2 2.7 collective-permute-done.47
  289.9 3.1 fusion.20
  293.0 3.4 fusion.25
  297.7 3.0 convolution_bitcast_fusion
  310.2 10.9 %collective-permute-done.35 = bf16[2,1,128,512]{3,2,1,0:T(8,128)(2,1)S(1)} collective-permute-done((bf16[2,1,128,512]{3,2,1,0:T(8,128)(2,1)S(1)}, bf16[2,1,128,512]{3,2,1,0:T(8,128)(2,1)S(1)}, u32[]{:S(2)}, u32[]{:S(2)}) %collective-permute-start.35) | collective-permute-done | bytes 262176 | tf_op jit(solution)/shard_map/ppermute | solution.py:29
  322.3 2.7 collective-permute-start.36
  337.8 3.5 fusion.48
  341.4 3.1 multiply_reduce_fusion.2
  346.9 2.5 slice.555
  364.3 7.5 %collective-permute-done.38 = bf16[2,2,1,2,1,40,768]{6,5,4,3,2,1,0:T(8,128)(2,1)S(1)} collective-permute-done((bf16[2,2,1,2,1,40,768]{6,5,4,3,2,1,0:T(8,128)(2,1)S(1)}, bf16[2,2,1,2,1,40,768]{6,5,4,3,2,1,0:T(8,128)(2,1)S(1)}, u32[]{:S(2)}, u32[]{:S(2)}) %collective-permute-start.38) | collective-permute-done | bytes 491552 | tf_op jit(solution)/shard_map/ppermute | solution.py:29
  373.3 2.7 collective-permute-done.43
  377.7 3.0 collective-permute-done.39
  383.5 6.2 %collective-permute-done.40 = bf16[2,1,1,1,1,40,768]{6,5,4,3,2,1,0:T(8,128)(2,1)S(1)} collective-permute-done((bf16[2,1,1,1,1,40,768]{6,5,4,3,2,1,0:T(8,128)(2,1)S(1)}, bf16[2,1,1,1,1,40,768]{6,5,4,3,2,1,0:T(8,128)(2,1)S(1)}, u32[]{:S(2)}, u32[]{:S(2)}) %collective-permute-start.40) | collective-permute-done | bytes 122912 | tf_op jit(solution)/shard_map/ppermute | solution.py:29
  389.7 3.3 collective-permute-start.41
  393.0 5.4 %collective-permute-done.45 = bf16[2,1,1,1,1,40,768]{6,5,4,3,2,1,0:T(8,128)(2,1)S(1)} collective-permute-done((bf16[2,1,1,1,1,40,768]{6,5,4,3,2,1,0:T(8,128)(2,1)S(1)}, bf16[2,1,1,1,1,40,768]{6,5,4,3,2,1,0:T(8,128)(2,1)S(1)}, u32[]{:S(2)}, u32[]{:S(2)}) %collective-permute-start.45) | collective-permute-done | bytes 122912 | tf_op jit(solution)/shard_map/ppermute | solution.py:29
  398.6 5.1 %collective-permute-done.41 = bf16[1,1,1,1,1,40,768]{6,5,4,3,2,1,0:T(8,128)(2,1)S(1)} collective-permute-done((bf16[1,1,1,1,1,40,768]{6,5,4,3,2,1,0:T(8,128)(2,1)S(1)}, bf16[1,1,1,1,1,40,768]{6,5,4,3,2,1,0:T(8,128)(2,1)S(1)}, u32[]{:S(2)}, u32[]{:S(2)}) %collective-permute-start.41) | collective-permute-done | bytes 61472 | tf_op jit(solution)/shard_map/ppermute | solution.py:29
  403.7 2.7 collective-permute-done.46
  410.6 3.2 collective-permute-done.48
  418.9 19.9 %reduce-scatter.7.cloned.1.call-done = bf16[1,648,1152]{2,1,0:T(8,128)(2,1)} async-done(((bf16[4,648,1152]{2,1,0:T(8,128)(2,1)}), bf16[1,648,1152]{2,1,0:T(8,128)(2,1)}) %reduce-scatter.7.cloned.1.call-update) | async-done | bytes 1493008
  (391 shorter events, 152.4 us)
Async XLA Ops:
  7.2 152.9 %all-gather.3.cloned.1.call-start = ((), (), s32[]{:S(2)}) async-start(), calls=%async_computation.3 | async-start | bytes 8939520 | tf_op jit(solution)/shard_map/all_gather | solution.py:222
  7.2 5.6 %collective-permute-start.12 = (bf16[1,1,32,1152]{3,2,1,0:T(8,128)(2,1)}, bf16[1,1,32,1152]{3,2,1,0:T(8,128)(2,1)S(1)}, u32[]{:S(2)}, u32[]{:S(2)}) collective-permute-start(bf16[1,1,32,1152]{3,2,1,0:T(8,128)(2,1)} %bitcast.242), channel_id=1, source_target_pairs={{0,2},{1,3},{2,0},{3,1},{4,6},{5,7},{6,4},{7,5},{8,10},{9,11},{10,... | collective-permute-start | bytes 221192 | tf_op jit(solution)/shard_map/ppermute | solution.py:29
  13.7 5.2 %collective-permute-start.13 = (bf16[1,2,32,1152]{3,2,1,0:T(8,128)(2,1)S(1)}, bf16[1,2,32,1152]{3,2,1,0:T(8,128)(2,1)S(1)}, u32[]{:S(2)}, u32[]{:S(2)}) collective-permute-start(bf16[1,2,32,1152]{3,2,1,0:T(8,128)(2,1)S(1)} %pad_maximum_fusion.25), channel_id=1, source_target_pairs={{0,4},{1,5},{2,6},{3,7},{4,0},{5,1},{6,2},{7,3},{8,12},{9,13},{10,... | collective-permute-start | bytes 442376 | tf_op jit(solution)/shard_map/ppermute | solution.py:29
  22.7 384.5 %reduce-scatter.5.cloned.1.call-start = ((), (), s32[]{:S(2)}) async-start(), calls=%async_computation.2 | async-start | bytes 1474560 | tf_op jit(solution)/shard_map/reduce_scatter | solution.py:331
  22.7 6.1 %collective-permute-start = (bf16[1,1,1,1,1,40,768]{6,5,4,3,2,1,0:T(8,128)(2,1)S(1)}, bf16[1,1,1,1,1,40,768]{6,5,4,3,2,1,0:T(8,128)(2,1)S(1)}, u32[]{:S(2)}, u32[]{:S(2)}) collective-permute-start(bf16[1,1,1,1,1,40,768]{6,5,4,3,2,1,0:T(8,128)(2,1)S(1)} %get-tuple-element.76), channel_id=1, source_target_pairs={{0,16},{8,24},{16,0},{24,8},{1,17},{9,25},{17,1},{25,9},{2,18},{10... | collective-permute-start | bytes 184328 | tf_op jit(solution)/shard_map/ppermute | solution.py:29
  25.9 5.2 %collective-permute-start.5 = (bf16[1,1,1,1,1,40,768]{6,5,4,3,2,1,0:T(8,128)(2,1)S(1)}, bf16[1,1,1,1,1,40,768]{6,5,4,3,2,1,0:T(8,128)(2,1)S(1)}, u32[]{:S(2)}, u32[]{:S(2)}) collective-permute-start(bf16[1,1,1,1,1,40,768]{6,5,4,3,2,1,0:T(8,128)(2,1)S(1)} %get-tuple-element.77), channel_id=1, source_target_pairs={{0,16},{8,24},{16,0},{24,8},{1,17},{9,25},{17,1},{25,9},{2,18},{10... | collective-permute-start | bytes 184328 | tf_op jit(solution)/shard_map/ppermute | solution.py:29
  28.9 4.9 %collective-permute-start.1 = (bf16[2,1,1,1,1,40,768]{6,5,4,3,2,1,0:T(8,128)(2,1)S(1)}, bf16[2,1,1,1,1,40,768]{6,5,4,3,2,1,0:T(8,128)(2,1)S(1)}, u32[]{:S(2)}, u32[]{:S(2)}) collective-permute-start(bf16[2,1,1,1,1,40,768]{6,5,4,3,2,1,0:T(8,128)(2,1)S(1)} %pad_maximum_fusion.27), channel_id=1, source_target_pairs={{0,8},{8,0},{16,24},{24,16},{1,9},{9,1},{17,25},{25,17},{2,10},{10... | collective-permute-start | bytes 368648 | tf_op jit(solution)/shard_map/ppermute | solution.py:29
  31.1 7.1 %collective-permute-start.6 = (bf16[2,1,1,1,1,40,768]{6,5,4,3,2,1,0:T(8,128)(2,1)S(1)}, bf16[2,1,1,1,1,40,768]{6,5,4,3,2,1,0:T(8,128)(2,1)S(1)}, u32[]{:S(2)}, u32[]{:S(2)}) collective-permute-start(bf16[2,1,1,1,1,40,768]{6,5,4,3,2,1,0:T(8,128)(2,1)S(1)} %pad_maximum_fusion.28), channel_id=1, source_target_pairs={{0,8},{8,0},{16,24},{24,16},{1,9},{9,1},{17,25},{25,17},{2,10},{10... | collective-permute-start | bytes 368648 | tf_op jit(solution)/shard_map/ppermute | solution.py:29
  33.8 7.2 %collective-permute-start.2 = (bf16[2,2,1,1,1,40,768]{6,5,4,3,2,1,0:T(8,128)(2,1)S(1)}, bf16[2,2,1,1,1,40,768]{6,5,4,3,2,1,0:T(8,128)(2,1)S(1)}, u32[]{:S(2)}, u32[]{:S(2)}) collective-permute-start(bf16[2,2,1,1,1,40,768]{6,5,4,3,2,1,0:T(8,128)(2,1)S(1)} %pad_maximum_fusion.21), channel_id=1, source_target_pairs={{0,2},{1,3},{2,0},{3,1},{4,6},{5,7},{6,4},{7,5},{8,10},{9,11},{10,... | collective-permute-start | bytes 737288 | tf_op jit(solution)/shard_map/ppermute | solution.py:29
  38.3 7.5 %collective-permute-start.7 = (bf16[2,2,1,1,1,40,768]{6,5,4,3,2,1,0:T(8,128)(2,1)S(1)}, bf16[2,2,1,1,1,40,768]{6,5,4,3,2,1,0:T(8,128)(2,1)S(1)}, u32[]{:S(2)}, u32[]{:S(2)}) collective-permute-start(bf16[2,2,1,1,1,40,768]{6,5,4,3,2,1,0:T(8,128)(2,1)S(1)} %pad_maximum_fusion.22), channel_id=1, source_target_pairs={{0,4},{1,5},{2,6},{3,7},{4,0},{5,1},{6,2},{7,3},{8,12},{9,13},{10,... | collective-permute-start | bytes 737288 | tf_op jit(solution)/shard_map/ppermute | solution.py:29
  41.1 9.9 %collective-permute-start.3 = (bf16[2,2,1,2,1,40,768]{6,5,4,3,2,1,0:T(8,128)(2,1)S(1)}, bf16[2,2,1,2,1,40,768]{6,5,4,3,2,1,0:T(8,128)(2,1)S(1)}, u32[]{:S(2)}, u32[]{:S(2)}) collective-permute-start(bf16[2,2,1,2,1,40,768]{6,5,4,3,2,1,0:T(8,128)(2,1)S(1)} %pad_maximum_fusion.11), channel_id=1, source_target_pairs={{0,4},{1,5},{2,6},{3,7},{4,0},{5,1},{6,2},{7,3},{8,12},{9,13},{10,... | collective-permute-start | bytes 1474568 | tf_op jit(solution)/shard_map/ppermute | solution.py:29
  45.8 8.9 %collective-permute-start.8 = (bf16[2,2,2,1,1,40,768]{6,5,4,3,2,1,0:T(8,128)(2,1)S(1)}, bf16[2,2,2,1,1,40,768]{6,5,4,3,2,1,0:T(8,128)(2,1)S(1)}, u32[]{:S(2)}, u32[]{:S(2)}) collective-permute-start(bf16[2,2,2,1,1,40,768]{6,5,4,3,2,1,0:T(8,128)(2,1)S(1)} %pad_maximum_fusion.12), channel_id=1, source_target_pairs={{0,2},{1,3},{2,0},{3,1},{4,6},{5,7},{6,4},{7,5},{8,10},{9,11},{10,... | collective-permute-start | bytes 1474568 | tf_op jit(solution)/shard_map/ppermute | solution.py:29
  51.1 6.1 %collective-permute-start.4 = (bf16[2,2,2,2,1,40,768]{6,5,4,3,2,1,0:T(8,128)(2,1)S(1)}, bf16[2,2,2,2,1,40,768]{6,5,4,3,2,1,0:T(8,128)(2,1)S(1)}, u32[]{:S(2)}, u32[]{:S(2)}) collective-permute-start(bf16[2,2,2,2,1,40,768]{6,5,4,3,2,1,0:T(8,128)(2,1)S(1)} %pad_maximum_fusion.6), channel_id=1, source_target_pairs={{0,1},{1,0},{2,3},{3,2},{4,5},{5,4},{6,7},{7,6},{8,9},{9,8},{10,11... | collective-permute-start | bytes 2949128 | tf_op jit(solution)/shard_map/ppermute | solution.py:29
  62.1 22.3 %collective-permute-start.10 = (bf16[1,1,128,512]{3,2,1,0:T(8,128)(2,1)S(1)}, bf16[1,1,128,512]{3,2,1,0:T(8,128)(2,1)S(1)}, u32[]{:S(2)}, u32[]{:S(2)}) collective-permute-start(bf16[1,1,128,512]{3,2,1,0:T(8,128)(2,1)S(1)} %maximum_bitcast_fusion.2), channel_id=1, source_target_pairs={{0,16},{8,24},{16,0},{24,8},{1,17},{9,25},{17,1},{25,9},{2,18},{10... | collective-permute-start | bytes 393224 | tf_op jit(solution)/shard_map/ppermute | solution.py:29
  85.1 77.6 %collective-permute-start.11 = (bf16[2,1,128,512]{3,2,1,0:T(8,128)(2,1)}, bf16[2,1,128,512]{3,2,1,0:T(8,128)(2,1)}, u32[]{:S(2)}, u32[]{:S(2)}) collective-permute-start(bf16[2,1,128,512]{3,2,1,0:T(8,128)(2,1)} %pad_maximum_fusion.17), channel_id=1, source_target_pairs={{0,8},{8,0},{16,24},{24,16},{1,9},{9,1},{17,25},{25,17},{2,10},{10... | collective-permute-start | bytes 786440 | tf_op jit(solution)/shard_map/ppermute | solution.py:29
  161.4 8.6 %collective-permute-start.14 = (bf16[1,4,128,1152]{3,2,1,0:T(8,128)(2,1)S(1)}, bf16[1,4,128,1152]{3,2,1,0:T(8,128)(2,1)}, u32[]{:S(2)}, u32[]{:S(2)}) collective-permute-start(bf16[1,4,128,1152]{3,2,1,0:T(8,128)(2,1)S(1)} %slice_bitcast_fusion), channel_id=1, source_target_pairs={{0,1},{1,0},{2,3},{3,2},{4,5},{5,4},{6,7},{7,6},{8,9},{9,8},{10,11... | collective-permute-start | bytes 3538952 | tf_op jit(solution)/shard_map/ppermute | solution.py:29
  173.3 6.7 %collective-permute-start.15 = (bf16[1,1,128,640]{3,2,1,0:T(8,128)(2,1)S(1)}, bf16[1,1,128,640]{3,2,1,0:T(8,128)(2,1)S(1)}, u32[]{:S(2)}, u32[]{:S(2)}) collective-permute-start(bf16[1,1,128,640]{3,2,1,0:T(8,128)(2,1)S(1)} %slice_bitcast_fusion.11), channel_id=1, source_target_pairs={{0,2},{1,3},{2,0},{3,1},{4,6},{5,7},{6,4},{7,5},{8,10},{9,11},{10,... | collective-permute-start | bytes 491528 | tf_op jit(solution)/shard_map/ppermute | solution.py:29
  174.9 6.7 %collective-permute-start.17 = (bf16[1,1,128,512]{3,2,1,0:T(8,128)(2,1)S(1)}, bf16[1,1,128,512]{3,2,1,0:T(8,128)(2,1)S(1)}, u32[]{:S(2)}, u32[]{:S(2)}) collective-permute-start(bf16[1,1,128,512]{3,2,1,0:T(8,128)(2,1)S(1)} %slice_bitcast_fusion.13), channel_id=1, source_target_pairs={{0,4},{1,5},{2,6},{3,7},{4,0},{5,1},{6,2},{7,3},{8,12},{9,13},{10,... | collective-permute-start | bytes 393224 | tf_op jit(solution)/shard_map/ppermute | solution.py:29
  180.0 9.3 %collective-permute-start.16 = (bf16[1,2,128,640]{3,2,1,0:T(8,128)(2,1)S(1)}, bf16[1,2,128,640]{3,2,1,0:T(8,128)(2,1)S(1)}, u32[]{:S(2)}, u32[]{:S(2)}) collective-permute-start(bf16[1,2,128,640]{3,2,1,0:T(8,128)(2,1)S(1)} %pad_maximum_fusion.14), channel_id=1, source_target_pairs={{0,4},{1,5},{2,6},{3,7},{4,0},{5,1},{6,2},{7,3},{8,12},{9,13},{10,... | collective-permute-start | bytes 983048 | tf_op jit(solution)/shard_map/ppermute | solution.py:29
  181.6 7.6 %collective-permute-start.18 = (bf16[2,1,128,512]{3,2,1,0:T(8,128)(2,1)S(1)}, bf16[2,1,128,512]{3,2,1,0:T(8,128)(2,1)S(1)}, u32[]{:S(2)}, u32[]{:S(2)}) collective-permute-start(bf16[2,1,128,512]{3,2,1,0:T(8,128)(2,1)S(1)} %pad_maximum_fusion.18), channel_id=1, source_target_pairs={{0,2},{1,3},{2,0},{3,1},{4,6},{5,7},{6,4},{7,5},{8,10},{9,11},{10,... | collective-permute-start | bytes 786440 | tf_op jit(solution)/shard_map/ppermute | solution.py:29
  189.4 2.9 collective-permute-start.19
  201.7 2.9 collective-permute-start.20
  204.9 8.4 %collective-permute-start.23 = (bf16[2,1,128,512]{3,2,1,0:T(8,128)(2,1)S(1)}, bf16[2,1,128,512]{3,2,1,0:T(8,128)(2,1)S(1)}, u32[]{:S(2)}, u32[]{:S(2)}) collective-permute-start(bf16[2,1,128,512]{3,2,1,0:T(8,128)(2,1)S(1)} %slice.530), channel_id=1, source_target_pairs={{0,2},{1,3},{2,0},{3,1},{4,6},{5,7},{6,4},{7,5},{8,10},{9,11},{10,... | collective-permute-start | bytes 786440 | tf_op jit(solution)/shard_map/ppermute | solution.py:29
  206.5 10.2 %collective-permute-start.21 = (bf16[1,2,128,640]{3,2,1,0:T(8,128)(2,1)S(1)}, bf16[1,2,128,640]{3,2,1,0:T(8,128)(2,1)S(1)}, u32[]{:S(2)}, u32[]{:S(2)}) collective-permute-start(bf16[1,2,128,640]{3,2,1,0:T(8,128)(2,1)S(1)} %slice.526), channel_id=1, source_target_pairs={{0,4},{1,5},{2,6},{3,7},{4,0},{5,1},{6,2},{7,3},{8,12},{9,13},{10,... | collective-permute-start | bytes 983048 | tf_op jit(solution)/shard_map/ppermute | solution.py:29
  213.5 5.4 %collective-permute-start.24 = (bf16[1,1,128,512]{3,2,1,0:T(8,128)(2,1)S(1)}, bf16[1,1,128,512]{3,2,1,0:T(8,128)(2,1)S(1)}, u32[]{:S(2)}, u32[]{:S(2)}) collective-permute-start(bf16[1,1,128,512]{3,2,1,0:T(8,128)(2,1)S(1)} %slice.704), channel_id=1, source_target_pairs={{0,4},{1,5},{2,6},{3,7},{4,0},{5,1},{6,2},{7,3},{8,12},{9,13},{10,... | collective-permute-start | bytes 393224 | tf_op jit(solution)/shard_map/ppermute | solution.py:29
  216.8 5.4 %collective-permute-start.22 = (bf16[1,1,128,640]{3,2,1,0:T(8,128)(2,1)S(1)}, bf16[1,1,128,640]{3,2,1,0:T(8,128)(2,1)S(1)}, u32[]{:S(2)}, u32[]{:S(2)}) collective-permute-start(bf16[1,1,128,640]{3,2,1,0:T(8,128)(2,1)S(1)} %slice.701), channel_id=1, source_target_pairs={{0,2},{1,3},{2,0},{3,1},{4,6},{5,7},{6,4},{7,5},{8,10},{9,11},{10,... | collective-permute-start | bytes 491528 | tf_op jit(solution)/shard_map/ppermute | solution.py:29
  224.2 5.4 %collective-permute-start.25 = (bf16[1,1,128,640]{3,2,1,0:T(8,128)(2,1)S(1)}, bf16[1,1,128,640]{3,2,1,0:T(8,128)(2,1)S(1)}, u32[]{:S(2)}, u32[]{:S(2)}) collective-permute-start(bf16[1,1,128,640]{3,2,1,0:T(8,128)(2,1)S(1)} %slice_bitcast_fusion.10), channel_id=1, source_target_pairs={{0,2},{1,3},{2,0},{3,1},{4,6},{5,7},{6,4},{7,5},{8,10},{9,11},{10,... | collective-permute-start | bytes 491528 | tf_op jit(solution)/shard_map/ppermute | solution.py:29
  224.3 7.7 %collective-permute-start.27 = (bf16[1,1,128,512]{3,2,1,0:T(8,128)(2,1)S(1)}, bf16[1,1,128,512]{3,2,1,0:T(8,128)(2,1)S(1)}, u32[]{:S(2)}, u32[]{:S(2)}) collective-permute-start(bf16[1,1,128,512]{3,2,1,0:T(8,128)(2,1)S(1)} %slice_bitcast_fusion.12), channel_id=1, source_target_pairs={{0,4},{1,5},{2,6},{3,7},{4,0},{5,1},{6,2},{7,3},{8,12},{9,13},{10,... | collective-permute-start | bytes 393224 | tf_op jit(solution)/shard_map/ppermute | solution.py:29
  229.7 8.8 %collective-permute-start.26 = (bf16[1,2,128,640]{3,2,1,0:T(8,128)(2,1)S(1)}, bf16[1,2,128,640]{3,2,1,0:T(8,128)(2,1)S(1)}, u32[]{:S(2)}, u32[]{:S(2)}) collective-permute-start(bf16[1,2,128,640]{3,2,1,0:T(8,128)(2,1)S(1)} %pad_maximum_fusion.15), channel_id=1, source_target_pairs={{0,4},{1,5},{2,6},{3,7},{4,0},{5,1},{6,2},{7,3},{8,12},{9,13},{10,... | collective-permute-start | bytes 983048 | tf_op jit(solution)/shard_map/ppermute | solution.py:29
  232.1 6.4 %collective-permute-start.28 = (bf16[2,1,128,512]{3,2,1,0:T(8,128)(2,1)S(1)}, bf16[2,1,128,512]{3,2,1,0:T(8,128)(2,1)S(1)}, u32[]{:S(2)}, u32[]{:S(2)}) collective-permute-start(bf16[2,1,128,512]{3,2,1,0:T(8,128)(2,1)S(1)} %pad_maximum_fusion.19), channel_id=1, source_target_pairs={{0,2},{1,3},{2,0},{3,1},{4,6},{5,7},{6,4},{7,5},{8,10},{9,11},{10,... | collective-permute-start | bytes 786440 | tf_op jit(solution)/shard_map/ppermute | solution.py:29
  252.8 7.6 %collective-permute-start.30 = (bf16[1,2,2,128,1152]{4,3,2,1,0:T(8,128)(2,1)S(1)}, bf16[1,2,2,128,1152]{4,3,2,1,0:T(8,128)(2,1)S(1)}, u32[]{:S(2)}, u32[]{:S(2)}) collective-permute-start(bf16[1,2,2,128,1152]{4,3,2,1,0:T(8,128)(2,1)S(1)} %bitcast.236), channel_id=1, source_target_pairs={{0,1},{1,0},{2,3},{3,2},{4,5},{5,4},{6,7},{7,6},{8,9},{9,8},{10,11... | collective-permute-start | bytes 3538952 | tf_op jit(solution)/shard_map/ppermute | solution.py:29
  263.0 12.4 %collective-permute-start.31 = (bf16[1,2,128,640]{3,2,1,0:T(8,128)(2,1)}, bf16[1,2,128,640]{3,2,1,0:T(8,128)(2,1)}, u32[]{:S(2)}, u32[]{:S(2)}) collective-permute-start(bf16[1,2,128,640]{3,2,1,0:T(8,128)(2,1)} %slice.538), channel_id=1, source_target_pairs={{0,4},{1,5},{2,6},{3,7},{4,0},{5,1},{6,2},{7,3},{8,12},{9,13},{10,... | collective-permute-start | bytes 983048 | tf_op jit(solution)/shard_map/ppermute | solution.py:29
  263.6 8.3 %collective-permute-start.33 = (bf16[2,1,128,512]{3,2,1,0:T(8,128)(2,1)S(1)}, bf16[2,1,128,512]{3,2,1,0:T(8,128)(2,1)S(1)}, u32[]{:S(2)}, u32[]{:S(2)}) collective-permute-start(bf16[2,1,128,512]{3,2,1,0:T(8,128)(2,1)S(1)} %slice.542), channel_id=1, source_target_pairs={{0,2},{1,3},{2,0},{3,1},{4,6},{5,7},{6,4},{7,5},{8,10},{9,11},{10,... | collective-permute-start | bytes 786440 | tf_op jit(solution)/shard_map/ppermute | solution.py:29
  273.9 5.0 %collective-permute-start.34 = (bf16[1,1,128,512]{3,2,1,0:T(8,128)(2,1)S(1)}, bf16[1,1,128,512]{3,2,1,0:T(8,128)(2,1)S(1)}, u32[]{:S(2)}, u32[]{:S(2)}) collective-permute-start(bf16[1,1,128,512]{3,2,1,0:T(8,128)(2,1)S(1)} %slice.703), channel_id=1, source_target_pairs={{0,4},{1,5},{2,6},{3,7},{4,0},{5,1},{6,2},{7,3},{8,12},{9,13},{10,... | collective-permute-start | bytes 393224 | tf_op jit(solution)/shard_map/ppermute | solution.py:29
  276.6 5.4 %collective-permute-start.32 = (bf16[1,1,128,640]{3,2,1,0:T(8,128)(2,1)S(1)}, bf16[1,1,128,640]{3,2,1,0:T(8,128)(2,1)S(1)}, u32[]{:S(2)}, u32[]{:S(2)}) collective-permute-start(bf16[1,1,128,640]{3,2,1,0:T(8,128)(2,1)S(1)} %slice.700), channel_id=1, source_target_pairs={{0,2},{1,3},{2,0},{3,1},{4,6},{5,7},{6,4},{7,5},{8,10},{9,11},{10,... | collective-permute-start | bytes 491528 | tf_op jit(solution)/shard_map/ppermute | solution.py:29
  289.3 149.6 %reduce-scatter.7.cloned.1.call-start = ((), (), s32[]{:S(2)}) async-start(), calls=%async_computation.4 | async-start | bytes 7464960
  306.4 14.7 %collective-permute-start.35 = (bf16[2,1,128,512]{3,2,1,0:T(8,128)(2,1)S(1)}, bf16[2,1,128,512]{3,2,1,0:T(8,128)(2,1)S(1)}, u32[]{:S(2)}, u32[]{:S(2)}) collective-permute-start(bf16[2,1,128,512]{3,2,1,0:T(8,128)(2,1)S(1)} %slice.697), channel_id=1, source_target_pairs={{0,8},{8,0},{16,24},{24,16},{1,9},{9,1},{17,25},{25,17},{2,10},{10... | collective-permute-start | bytes 786440 | tf_op jit(solution)/shard_map/ppermute | solution.py:29
  322.3 9.2 %collective-permute-start.36 = (bf16[1,1,128,512]{3,2,1,0:T(8,128)(2,1)S(1)}, bf16[1,1,128,512]{3,2,1,0:T(8,128)(2,1)S(1)}, u32[]{:S(2)}, u32[]{:S(2)}) collective-permute-start(bf16[1,1,128,512]{3,2,1,0:T(8,128)(2,1)S(1)} %slice.702), channel_id=1, source_target_pairs={{0,16},{8,24},{16,0},{24,8},{1,17},{9,25},{17,1},{25,9},{2,18},{10... | collective-permute-start | bytes 393224 | tf_op jit(solution)/shard_map/ppermute | solution.py:29
  358.5 13.3 %collective-permute-start.38 = (bf16[2,2,1,2,1,40,768]{6,5,4,3,2,1,0:T(8,128)(2,1)S(1)}, bf16[2,2,1,2,1,40,768]{6,5,4,3,2,1,0:T(8,128)(2,1)S(1)}, u32[]{:S(2)}, u32[]{:S(2)}) collective-permute-start(bf16[2,2,1,2,1,40,768]{6,5,4,3,2,1,0:T(8,128)(2,1)S(1)} %slice.696), channel_id=1, source_target_pairs={{0,4},{1,5},{2,6},{3,7},{4,0},{5,1},{6,2},{7,3},{8,12},{9,13},{10,... | collective-permute-start | bytes 1474568 | tf_op jit(solution)/shard_map/ppermute | solution.py:29
  361.9 14.2 %collective-permute-start.43 = (bf16[2,2,2,1,1,40,768]{6,5,4,3,2,1,0:T(8,128)(2,1)S(1)}, bf16[2,2,2,1,1,40,768]{6,5,4,3,2,1,0:T(8,128)(2,1)S(1)}, u32[]{:S(2)}, u32[]{:S(2)}) collective-permute-start(bf16[2,2,2,1,1,40,768]{6,5,4,3,2,1,0:T(8,128)(2,1)S(1)} %slice.695), channel_id=1, source_target_pairs={{0,2},{1,3},{2,0},{3,1},{4,6},{5,7},{6,4},{7,5},{8,10},{9,11},{10,... | collective-permute-start | bytes 1474568 | tf_op jit(solution)/shard_map/ppermute | solution.py:29
  372.0 8.7 %collective-permute-start.39 = (bf16[2,2,1,1,1,40,768]{6,5,4,3,2,1,0:T(8,128)(2,1)S(1)}, bf16[2,2,1,1,1,40,768]{6,5,4,3,2,1,0:T(8,128)(2,1)S(1)}, u32[]{:S(2)}, u32[]{:S(2)}) collective-permute-start(bf16[2,2,1,1,1,40,768]{6,5,4,3,2,1,0:T(8,128)(2,1)S(1)} %slice.699), channel_id=1, source_target_pairs={{0,2},{1,3},{2,0},{3,1},{4,6},{5,7},{6,4},{7,5},{8,10},{9,11},{10,... | collective-permute-start | bytes 737288 | tf_op jit(solution)/shard_map/ppermute | solution.py:29
  376.2 7.0 %collective-permute-start.44 = (bf16[2,2,1,1,1,40,768]{6,5,4,3,2,1,0:T(8,128)(2,1)S(1)}, bf16[2,2,1,1,1,40,768]{6,5,4,3,2,1,0:T(8,128)(2,1)S(1)}, u32[]{:S(2)}, u32[]{:S(2)}) collective-permute-start(bf16[2,2,1,1,1,40,768]{6,5,4,3,2,1,0:T(8,128)(2,1)S(1)} %slice.698), channel_id=1, source_target_pairs={{0,4},{1,5},{2,6},{3,7},{4,0},{5,1},{6,2},{7,3},{8,12},{9,13},{10,... | collective-permute-start | bytes 737288 | tf_op jit(solution)/shard_map/ppermute | solution.py:29
  380.8 8.9 %collective-permute-start.40 = (bf16[2,1,1,1,1,40,768]{6,5,4,3,2,1,0:T(8,128)(2,1)S(1)}, bf16[2,1,1,1,1,40,768]{6,5,4,3,2,1,0:T(8,128)(2,1)S(1)}, u32[]{:S(2)}, u32[]{:S(2)}) collective-permute-start(bf16[2,1,1,1,1,40,768]{6,5,4,3,2,1,0:T(8,128)(2,1)S(1)} %slice.706), channel_id=1, source_target_pairs={{0,8},{8,0},{16,24},{24,16},{1,9},{9,1},{17,25},{25,17},{2,10},{10... | collective-permute-start | bytes 368648 | tf_op jit(solution)/shard_map/ppermute | solution.py:29
  383.2 15.2 %collective-permute-start.45 = (bf16[2,1,1,1,1,40,768]{6,5,4,3,2,1,0:T(8,128)(2,1)S(1)}, bf16[2,1,1,1,1,40,768]{6,5,4,3,2,1,0:T(8,128)(2,1)S(1)}, u32[]{:S(2)}, u32[]{:S(2)}) collective-permute-start(bf16[2,1,1,1,1,40,768]{6,5,4,3,2,1,0:T(8,128)(2,1)S(1)} %slice.705), channel_id=1, source_target_pairs={{0,8},{8,0},{16,24},{24,16},{1,9},{9,1},{17,25},{25,17},{2,10},{10... | collective-permute-start | bytes 368648 | tf_op jit(solution)/shard_map/ppermute | solution.py:29
  389.7 14.0 %collective-permute-start.41 = (bf16[1,1,1,1,1,40,768]{6,5,4,3,2,1,0:T(8,128)(2,1)S(1)}, bf16[1,1,1,1,1,40,768]{6,5,4,3,2,1,0:T(8,128)(2,1)S(1)}, u32[]{:S(2)}, u32[]{:S(2)}) collective-permute-start(bf16[1,1,1,1,1,40,768]{6,5,4,3,2,1,0:T(8,128)(2,1)S(1)} %slice.711), channel_id=1, source_target_pairs={{0,16},{8,24},{16,0},{24,8},{1,17},{9,25},{17,1},{25,9},{2,18},{10... | collective-permute-start | bytes 184328 | tf_op jit(solution)/shard_map/ppermute | solution.py:29
  398.5 8.0 %collective-permute-start.46 = (bf16[1,1,1,1,1,40,768]{6,5,4,3,2,1,0:T(8,128)(2,1)S(1)}, bf16[1,1,1,1,1,40,768]{6,5,4,3,2,1,0:T(8,128)(2,1)S(1)}, u32[]{:S(2)}, u32[]{:S(2)}) collective-permute-start(bf16[1,1,1,1,1,40,768]{6,5,4,3,2,1,0:T(8,128)(2,1)S(1)} %slice.710), channel_id=1, source_target_pairs={{0,16},{8,24},{16,0},{24,8},{1,17},{9,25},{17,1},{25,9},{2,18},{10... | collective-permute-start | bytes 184328 | tf_op jit(solution)/shard_map/ppermute | solution.py:29
  408.2 5.6 %collective-permute-start.48 = (bf16[1,2,32,1152]{3,2,1,0:T(8,128)(2,1)S(1)}, bf16[1,2,32,1152]{3,2,1,0:T(8,128)(2,1)S(1)}, u32[]{:S(2)}, u32[]{:S(2)}) collective-permute-start(bf16[1,2,32,1152]{3,2,1,0:T(8,128)(2,1)S(1)} %bitcast.246), channel_id=1, source_target_pairs={{0,4},{1,5},{2,6},{3,7},{4,0},{5,1},{6,2},{7,3},{8,12},{9,13},{10,... | collective-permute-start | bytes 442376 | tf_op jit(solution)/shard_map/ppermute | solution.py:29
  413.8 4.4 collective-permute-start.49
  (66 other events, 682.3 us)
Sparse Core Ops, SparseCore 0:
  22.8 137.2 all-gather.2
  289.4 34.6 reduce-scatter.4
  326.4 112.3 reduce-scatter.6

commit v4 on v3

--- a/solution.py
+++ b/solution.py
@@ -202,11 +202,7 @@
     ).reshape(-1, 1)
     lane = jnp.arange(qkv_pad, dtype=jnp.int32)[None, :]
     qkv_origin = jnp.where(lane < qkv_own, qkv_dev * qkv_own + lane, -1).reshape(-1)
-    out_dev = (
-        seq_off[None, :, None] * dp_count
-        + ((dp_id // 2) ^ chip_off)[None, None, :] * 2
-        + ((dp_id % 2) ^ core_off)[:, None, None]
-    ).reshape(-1, 1)
+    out_dev = qkv_dev
     out_origin = (out_dev * out_own + jnp.arange(out_own, dtype=jnp.int32)[None, :]).reshape(-1)
     qkv_order = one_hot_order(qkv_origin, width)
     out_order = one_hot_order(out_origin, qwidth)
@@ -218,16 +214,15 @@
         ],
         axis=-1,
     ).reshape(-1, 2 * half)
-    out_column = gather_xor(w_out, plane_up).reshape(-1, width)
+    out_full = gather_xor(w_out, all_down).reshape(-1, width)
     line_rows = lax.all_gather(
-        jnp.concatenate([w_gate, w_up, w_down, out_column], axis=0),
+        jnp.concatenate([w_gate, w_up, w_down], axis=0),
         "seq",
         axis=0,
     )
     gate_full, up_full, down_full = (
         line_rows[:, i * ffn_own : (i + 1) * ffn_own].reshape(-1, width) for i in range(3)
     )
-    out_full = mine_first(line_rows[None, :, 3 * ffn_own :], "dp", 1, 0).reshape(-1, width)
     starts = jnp.cumsum(lens) - lens
     own_index = block_id * rows + jnp.arange(rows, dtype=jnp.int32)
     key_index = (
@@ -327,15 +322,9 @@
     attn_grad_b = norm_back(hidden_grad_in, unit_post, root_post, g_attn_out).astype(jnp.bfloat16)
     mixed_grad_slots = contract_cols(attn_grad_b, out_full).astype(jnp.bfloat16)
     mixed_grad_b = contract_cols(mixed_grad_slots, out_order).astype(jnp.bfloat16)
-    out_term = contract_rows(mixed_slots, attn_grad_b).reshape(2, seq_count, -1, width)
-    out_line = lax.psum_scatter(
-        keep_half(out_term, "dp", 1, 0)[0].astype(jnp.bfloat16),
-        "seq",
-        scatter_dimension=0,
-    ).astype(jnp.float32)
-    owned_out = scatter_xor(
-        out_line.reshape((2,) * nchip + w_out.shape), plane_down
-    )
+    spread = (2,) * (nseq + nchip + 1)
+    out_term = contract_rows(mixed_slots, attn_grad_b).reshape(spread + w_out.shape)
+    owned_out = scatter_xor(out_term, all_down[::-1])
     mixed_grad3 = mixed_grad_b.reshape(rows, HEADS, HEAD_DIM)
     delta = jnp.sum(
         mixed_grad3.astype(jnp.float32)
@@ -362,6 +351,7 @@
     kv_grad = scatter_xor(
         kv_grad_all.reshape((2,) * nseq + (rows, 2 * HEAD_DIM)), kv_stages[::-1]
     )
+    kv_grad, owned_out = lax.optimization_barrier((kv_grad, owned_out))
     key_rot_grad = kv_grad[:, :HEAD_DIM]
     value_grad = kv_grad[:, HEAD_DIM:]
     query_norm_grad = query_rot_grad * cos_t[:, None, :] - turn_half(

time: 453 us -> 403 us (0.89)
  waiting for transfers between devices: 240 us -> 165 us
  starting transfers between devices: 61.5 us -> 69.8 us
  other arithmetic: 47.1 us -> 55 us
  local copies, waits for them, and re-layouts: 32.6 us -> 39.9 us
    all_gather x1, waiting for transfers between devices: 74.9 us -> 0.01 us  [local(): lax.all_gather(jnp.concatenate([w_gate, w_up, w_down], axis=0), 'seq', ax...]
    ppermute x50 -> x54, waiting for transfers between devices: 145 us -> 165 us  [swapped(): return lax.ppermute(value, axis, [(i, i ^ bit) for i in range(length)])]
    unnamed x4 -> x3, waiting for transfers between devices: 20 us -> 0.03 us
    ppermute x50 -> x54, starting transfers between devices: 61.4 us -> 69.7 us  [swapped(): return lax.ppermute(value, axis, [(i, i ^ bit) for i in range(length)])]
    add x15 -> x18, other arithmetic: 6.06 us -> 10.8 us  [keep_half(): own.astype(jnp.float32) + swapped(other, axis, bit).astype(jnp.float32)]
    unnamed x120 -> x156, local copies, waits for them, and re-layouts: 5.44 us -> 9.56 us
    concatenate x19 -> x21, other arithmetic: 6.34 us -> 9.29 us  [mine_first(): return jnp.concatenate([value, swapped(value, axis, bit)], axis=at)]
    slice x25 -> x27, local copies, waits for them, and re-layouts: 7.15 us -> 9.6 us  [keep_half(): other = lax.slice_in_dim(value, 1, 2, axis=at).astype(jnp.bfloat16)]
  transfers between devices with their start and end apart: 53 -> 56, of which waited for: 43 -> 37; matrix products, arithmetic and copies ran while one was open for 19% -> 24% of each run, Pallas kernels for 0% -> 0%
where the time goes in v4:
time: 403 us; the launch traced here: 397 us
  waiting for transfers between devices  165 us (41%)
  starting transfers between devices  69.8 us (17%)
  other arithmetic  55 us (14%)
  matrix products  51.3 us (13%)
  local copies, waits for them, and re-layouts  39.9 us (10%)
  between operations  16.1 us (4%)
    ppermute x54, waiting for transfers between devices, swapped(): return lax.ppermute(value, axis, [(i, i ^ bit) for i in range(length)])  165 us
    ppermute x54, starting transfers between devices, swapped(): return lax.ppermute(value, axis, [(i, i ^ bit) for i in range(length)])  69.7 us
    dot_general x5, matrix products, contract_cols(): lax.dot_general(left, right, (((1,), (1,)), ((), ())), preferred_element_...  17.2 us
    dot_general x7, matrix products, dot32(): return jnp.dot(left, right, preferred_element_type=jnp.float32)  14.3 us
    add x18, other arithmetic, keep_half(): own.astype(jnp.float32) + swapped(other, axis, bit).astype(jnp.float32)  10.8 us
    slice x27, local copies, waits for them, and re-layouts, keep_half(): other = lax.slice_in_dim(value, 1, 2, axis=at).astype(jnp.bfloat16)  9.6 us
    unnamed x156, local copies, waits for them, and re-layouts  9.56 us
    dot_general x5, matrix products, contract_rows(): lax.dot_general(left, right, (((0,), (0,)), ((), ())), preferred_element_...  9.39 us
  transfers between devices with their start and end apart: 56, of which 37 were waited for; matrix products, arithmetic and copies ran while one was open for 24% of the time, Pallas kernels for 0%

profile of v4, /device:TPU:0, one launch (start us, length us, event | category | flops | bytes accessed | tf_op | source)
XLA Modules:
  0.0 397.0 jit_solution(11133683736897108350)
XLA Ops:
  8.1 4.1 %collective-permute-start = (bf16[1,1,1,1,1,40,768]{6,5,4,3,2,1,0:T(8,128)(2,1)S(1)}, bf16[1,1,1,1,1,40,768]{6,5,4,3,2,1,0:T(8,128)(2,1)S(1)}, u32[]{:S(2)}, u32[]{:S(2)}) collective-permute-start(bf16[1,1,1,1,1,40,768]{6,5,4,3,2,1,0:T(8,128)(2,1)S(1)} %get-tuple-element.78), channel_id=1, source_target_pairs={{0,16},{8,24},{16,0},{24,8},{1,17},{9,25},{17,1},{25,9},{2,18},{10... | collective-permute-start | bytes 184328 | tf_op jit(solution)/shard_map/ppermute | solution.py:29
  12.3 2.8 collective-permute-start.12
  15.2 2.6 pad_maximum_fusion.4
  30.8 3.6 collective-permute-done.13
  39.8 4.8 %collective-permute-done.14 = bf16[2,2,1,1,1,32,1152]{6,5,4,3,2,1,0:T(8,128)(2,1)S(1)} collective-permute-done((bf16[2,2,1,1,1,32,1152]{6,5,4,3,2,1,0:T(8,128)(2,1)S(1)}, bf16[2,2,1,1,1,32,1152]{6,5,4,3,2,1,0:T(8,128)(2,1)S(1)}, u32[]{:S(2)}, u32[]{:S(2)}) %collective-permute-start.14) | collective-permute-done | bytes 294944 | tf_op jit(solution)/shard_map/ppermute | solution.py:29
  46.9 3.8 collective-permute-done.3
  58.7 3.4 maximum_maximum_fusion
  69.3 3.7 collective-permute-start.10
  73.4 14.9 %collective-permute-done.10 = bf16[1,1,128,512]{3,2,1,0:T(8,128)(2,1)S(1)} collective-permute-done((bf16[1,1,128,512]{3,2,1,0:T(8,128)(2,1)S(1)}, bf16[1,1,128,512]{3,2,1,0:T(8,128)(2,1)S(1)}, u32[]{:S(2)}, u32[]{:S(2)}) %collective-permute-start.10) | collective-permute-done | bytes 131104 | tf_op jit(solution)/shard_map/ppermute | solution.py:29
  88.4 2.8 pad_maximum_fusion.1
  91.3 29.4 %collective-permute-done.11 = bf16[2,1,128,512]{3,2,1,0:T(8,128)(2,1)S(1)} collective-permute-done((bf16[2,1,128,512]{3,2,1,0:T(8,128)(2,1)S(1)}, bf16[2,1,128,512]{3,2,1,0:T(8,128)(2,1)S(1)}, u32[]{:S(2)}, u32[]{:S(2)}) %collective-permute-start.11) | collective-permute-done | bytes 262176 | tf_op jit(solution)/shard_map/ppermute | solution.py:29
  128.8 3.4 collective-permute-done.17
  136.0 4.7 %collective-permute-done.20 = bf16[2,1,128,512]{3,2,1,0:T(8,128)(2,1)S(1)} collective-permute-done((bf16[2,1,128,512]{3,2,1,0:T(8,128)(2,1)S(1)}, bf16[2,1,128,512]{3,2,1,0:T(8,128)(2,1)S(1)}, u32[]{:S(2)}, u32[]{:S(2)}) %collective-permute-start.20) | collective-permute-done | bytes 262176 | tf_op jit(solution)/shard_map/ppermute | solution.py:29
  140.9 2.8 collective-permute-done.21
  145.4 3.4 fusion.69
  148.8 2.5 fusion.71
  151.3 3.0 multiply_convert_fusion.1
  154.3 3.0 fusion.72
  157.8 2.6 collective-permute-done.22
  163.1 6.0 %collective-permute-done.25 = bf16[2,1,128,512]{3,2,1,0:T(8,128)(2,1)S(1)} collective-permute-done((bf16[2,1,128,512]{3,2,1,0:T(8,128)(2,1)S(1)}, bf16[2,1,128,512]{3,2,1,0:T(8,128)(2,1)S(1)}, u32[]{:S(2)}, u32[]{:S(2)}) %collective-permute-start.25) | collective-permute-done | bytes 262176 | tf_op jit(solution)/shard_map/ppermute | solution.py:29
  170.0 2.8 collective-permute-done.23
  174.8 3.5 collective-permute-done.24
  181.4 5.3 %collective-permute-done.27 = bf16[1,1,128,640]{3,2,1,0:T(8,128)(2,1)S(1)} collective-permute-done((bf16[1,1,128,640]{3,2,1,0:T(8,128)(2,1)S(1)}, bf16[1,1,128,640]{3,2,1,0:T(8,128)(2,1)S(1)}, u32[]{:S(2)}, u32[]{:S(2)}) %collective-permute-start.27) | collective-permute-done | bytes 163872 | tf_op jit(solution)/shard_map/ppermute | solution.py:29
  189.4 4.4 %collective-permute-done.30 = bf16[2,1,128,512]{3,2,1,0:T(8,128)(2,1)S(1)} collective-permute-done((bf16[2,1,128,512]{3,2,1,0:T(8,128)(2,1)S(1)}, bf16[2,1,128,512]{3,2,1,0:T(8,128)(2,1)S(1)}, u32[]{:S(2)}, u32[]{:S(2)}) %collective-permute-start.30) | collective-permute-done | bytes 262176 | tf_op jit(solution)/shard_map/ppermute | solution.py:29
  194.1 2.8 collective-permute-done.31
  197.2 4.8 %multiply_convert_fusion = (bf16[1024,864]{0,1:T(8,128)(2,1)S(1)}, bf16[1024,864]{0,1:T(8,128)(2,1)S(1)}) fusion(f32[1024,864]{0,1:T(8,128)S(1)} %fusion.71, f32[1024,864]{0,1:T(8,128)S(1)} %get-tuple-element.92, bf16[1024,1152]{1,0:T(8,128)(2,1)S(1)} %bitcast.214, bf16[864,1152]{1,0:T(8,128)(2,1)S(1)} %bitcast.221), kind=kOutput, calls=%fused_computation.20 | convolution fusion | flops 2058780672 | bytes 14966784 | tf_op jit(solution)/shard_map/dot_general | solution.py:114
  201.9 2.9 fusion.73
  204.9 3.1 convolution_add_fusion
  210.8 2.5 convolution_convert_fusion.1
  220.8 3.3 pad_maximum_fusion
  224.0 4.1 %collective-permute-done.35 = bf16[2,1,128,512]{3,2,1,0:T(8,128)(2,1)S(1)} collective-permute-done((bf16[2,1,128,512]{3,2,1,0:T(8,128)(2,1)S(1)}, bf16[2,1,128,512]{3,2,1,0:T(8,128)(2,1)S(1)}, u32[]{:S(2)}, u32[]{:S(2)}) %collective-permute-start.35) | collective-permute-done | bytes 262176 | tf_op jit(solution)/shard_map/ppermute | solution.py:29
  253.8 3.4 fusion.25
  261.3 6.8 %collective-permute-done.40 = bf16[2,2,2,1,1,32,1152]{6,5,4,3,2,1,0:T(8,128)(2,1)} collective-permute-done((bf16[2,2,2,1,1,32,1152]{6,5,4,3,2,1,0:T(8,128)(2,1)}, bf16[2,2,2,1,1,32,1152]{6,5,4,3,2,1,0:T(8,128)(2,1)}, u32[]{:S(2)}, u32[]{:S(2)}) %collective-permute-start.40) | collective-permute-done | bytes 589856 | tf_op jit(solution)/shard_map/ppermute | solution.py:29
  272.5 3.0 convolution_bitcast_fusion
  284.2 12.2 %collective-permute-done.37 = bf16[2,1,128,512]{3,2,1,0:T(8,128)(2,1)} collective-permute-done((bf16[2,1,128,512]{3,2,1,0:T(8,128)(2,1)}, bf16[2,1,128,512]{3,2,1,0:T(8,128)(2,1)}, u32[]{:S(2)}, u32[]{:S(2)}) %collective-permute-start.37) | collective-permute-done | bytes 262176 | tf_op jit(solution)/shard_map/ppermute | solution.py:29
  297.5 2.5 collective-permute-start.38
  300.0 8.0 %collective-permute-done.42 = bf16[2,1,1,1,1,32,1152]{6,5,4,3,2,1,0:T(8,128)(2,1)S(1)} collective-permute-done((bf16[2,1,1,1,1,32,1152]{6,5,4,3,2,1,0:T(8,128)(2,1)S(1)}, bf16[2,1,1,1,1,32,1152]{6,5,4,3,2,1,0:T(8,128)(2,1)S(1)}, u32[]{:S(2)}, u32[]{:S(2)}) %collective-permute-start.42) | collective-permute-done | bytes 147488 | tf_op jit(solution)/shard_map/ppermute | solution.py:29
  308.1 2.5 collective-permute-start.43
  310.6 7.3 %collective-permute-done.38 = bf16[1,1,128,512]{3,2,1,0:T(8,128)(2,1)S(1)} collective-permute-done((bf16[1,1,128,512]{3,2,1,0:T(8,128)(2,1)S(1)}, bf16[1,1,128,512]{3,2,1,0:T(8,128)(2,1)S(1)}, u32[]{:S(2)}, u32[]{:S(2)}) %collective-permute-start.38) | collective-permute-done | bytes 131104 | tf_op jit(solution)/shard_map/ppermute | solution.py:29
  317.9 3.2 collective-permute-done.43
  326.9 3.5 fusion.47
  330.5 3.3 multiply_reduce_fusion.2
  336.2 2.6 slice.560
  353.7 7.3 %collective-permute-done.45 = bf16[2,2,1,2,1,40,768]{6,5,4,3,2,1,0:T(8,128)(2,1)S(1)} collective-permute-done((bf16[2,2,1,2,1,40,768]{6,5,4,3,2,1,0:T(8,128)(2,1)S(1)}, bf16[2,2,1,2,1,40,768]{6,5,4,3,2,1,0:T(8,128)(2,1)S(1)}, u32[]{:S(2)}, u32[]{:S(2)}) %collective-permute-start.45) | collective-permute-done | bytes 491552 | tf_op jit(solution)/shard_map/ppermute | solution.py:29
  362.6 2.6 collective-permute-done.50
  366.9 2.9 collective-permute-done.46
  369.9 3.1 collective-permute-start.47
  377.6 3.2 collective-permute-start.48
  (434 shorter events, 156.9 us)
Async XLA Ops:
  7.2 138.2 %all-gather.3.cloned.1.call-start = ((), (), s32[]{:S(2)}) async-start(), calls=%async_computation.1 | async-start | bytes 7464960 | tf_op jit(solution)/shard_map/all_gather | solution.py:218
  8.1 12.0 %collective-permute-start = (bf16[1,1,1,1,1,40,768]{6,5,4,3,2,1,0:T(8,128)(2,1)S(1)}, bf16[1,1,1,1,1,40,768]{6,5,4,3,2,1,0:T(8,128)(2,1)S(1)}, u32[]{:S(2)}, u32[]{:S(2)}) collective-permute-start(bf16[1,1,1,1,1,40,768]{6,5,4,3,2,1,0:T(8,128)(2,1)S(1)} %get-tuple-element.78), channel_id=1, source_target_pairs={{0,16},{8,24},{16,0},{24,8},{1,17},{9,25},{17,1},{25,9},{2,18},{10... | collective-permute-start | bytes 184328 | tf_op jit(solution)/shard_map/ppermute | solution.py:29
  12.2 9.5 %collective-permute-start.5 = (bf16[1,1,1,1,1,40,768]{6,5,4,3,2,1,0:T(8,128)(2,1)S(1)}, bf16[1,1,1,1,1,40,768]{6,5,4,3,2,1,0:T(8,128)(2,1)S(1)}, u32[]{:S(2)}, u32[]{:S(2)}) collective-permute-start(bf16[1,1,1,1,1,40,768]{6,5,4,3,2,1,0:T(8,128)(2,1)S(1)} %get-tuple-element.79), channel_id=1, source_target_pairs={{0,16},{8,24},{16,0},{24,8},{1,17},{9,25},{17,1},{25,9},{2,18},{10... | collective-permute-start | bytes 184328 | tf_op jit(solution)/shard_map/ppermute | solution.py:29
  12.3 10.0 %collective-permute-start.12 = (bf16[1,1,1,1,1,32,1152]{6,5,4,3,2,1,0:T(8,128)(2,1)}, bf16[1,1,1,1,1,32,1152]{6,5,4,3,2,1,0:T(8,128)(2,1)S(1)}, u32[]{:S(2)}, u32[]{:S(2)}) collective-permute-start(bf16[1,1,1,1,1,32,1152]{6,5,4,3,2,1,0:T(8,128)(2,1)} %bitcast.225), channel_id=1, source_target_pairs={{0,16},{8,24},{16,0},{24,8},{1,17},{9,25},{17,1},{25,9},{2,18},{10... | collective-permute-start | bytes 221192 | tf_op jit(solution)/shard_map/ppermute | solution.py:29
  17.8 368.9 %reduce-scatter.4.cloned.1.call-start = ((), (), s32[]{:S(2)}) async-start(), calls=%async_computation.2 | async-start | bytes 7464960
  20.1 6.3 %collective-permute-start.1 = (bf16[2,1,1,1,1,40,768]{6,5,4,3,2,1,0:T(8,128)(2,1)S(1)}, bf16[2,1,1,1,1,40,768]{6,5,4,3,2,1,0:T(8,128)(2,1)S(1)}, u32[]{:S(2)}, u32[]{:S(2)}) collective-permute-start(bf16[2,1,1,1,1,40,768]{6,5,4,3,2,1,0:T(8,128)(2,1)S(1)} %pad_maximum_fusion.29), channel_id=1, source_target_pairs={{0,8},{8,0},{16,24},{24,16},{1,9},{9,1},{17,25},{25,17},{2,10},{10... | collective-permute-start | bytes 368648 | tf_op jit(solution)/shard_map/ppermute | solution.py:29
  21.8 7.6 %collective-permute-start.6 = (bf16[2,1,1,1,1,40,768]{6,5,4,3,2,1,0:T(8,128)(2,1)S(1)}, bf16[2,1,1,1,1,40,768]{6,5,4,3,2,1,0:T(8,128)(2,1)S(1)}, u32[]{:S(2)}, u32[]{:S(2)}) collective-permute-start(bf16[2,1,1,1,1,40,768]{6,5,4,3,2,1,0:T(8,128)(2,1)S(1)} %pad_maximum_fusion.30), channel_id=1, source_target_pairs={{0,8},{8,0},{16,24},{24,16},{1,9},{9,1},{17,25},{25,17},{2,10},{10... | collective-permute-start | bytes 368648 | tf_op jit(solution)/shard_map/ppermute | solution.py:29
  22.4 12.0 %collective-permute-start.13 = (bf16[2,1,1,1,1,32,1152]{6,5,4,3,2,1,0:T(8,128)(2,1)S(1)}, bf16[2,1,1,1,1,32,1152]{6,5,4,3,2,1,0:T(8,128)(2,1)S(1)}, u32[]{:S(2)}, u32[]{:S(2)}) collective-permute-start(bf16[2,1,1,1,1,32,1152]{6,5,4,3,2,1,0:T(8,128)(2,1)S(1)} %pad_maximum_fusion.27), channel_id=1, source_target_pairs={{0,8},{8,0},{16,24},{24,16},{1,9},{9,1},{17,25},{25,17},{2,10},{10... | collective-permute-start | bytes 442376 | tf_op jit(solution)/shard_map/ppermute | solution.py:29
  26.4 9.8 %collective-permute-start.2 = (bf16[2,2,1,1,1,40,768]{6,5,4,3,2,1,0:T(8,128)(2,1)S(1)}, bf16[2,2,1,1,1,40,768]{6,5,4,3,2,1,0:T(8,128)(2,1)S(1)}, u32[]{:S(2)}, u32[]{:S(2)}) collective-permute-start(bf16[2,2,1,1,1,40,768]{6,5,4,3,2,1,0:T(8,128)(2,1)S(1)} %pad_maximum_fusion.23), channel_id=1, source_target_pairs={{0,2},{1,3},{2,0},{3,1},{4,6},{5,7},{6,4},{7,5},{8,10},{9,11},{10,... | collective-permute-start | bytes 737288 | tf_op jit(solution)/shard_map/ppermute | solution.py:29
  29.4 8.9 %collective-permute-start.7 = (bf16[2,2,1,1,1,40,768]{6,5,4,3,2,1,0:T(8,128)(2,1)S(1)}, bf16[2,2,1,1,1,40,768]{6,5,4,3,2,1,0:T(8,128)(2,1)S(1)}, u32[]{:S(2)}, u32[]{:S(2)}) collective-permute-start(bf16[2,2,1,1,1,40,768]{6,5,4,3,2,1,0:T(8,128)(2,1)S(1)} %pad_maximum_fusion.24), channel_id=1, source_target_pairs={{0,4},{1,5},{2,6},{3,7},{4,0},{5,1},{6,2},{7,3},{8,12},{9,13},{10,... | collective-permute-start | bytes 737288 | tf_op jit(solution)/shard_map/ppermute | solution.py:29
  34.4 10.2 %collective-permute-start.14 = (bf16[2,2,1,1,1,32,1152]{6,5,4,3,2,1,0:T(8,128)(2,1)S(1)}, bf16[2,2,1,1,1,32,1152]{6,5,4,3,2,1,0:T(8,128)(2,1)S(1)}, u32[]{:S(2)}, u32[]{:S(2)}) collective-permute-start(bf16[2,2,1,1,1,32,1152]{6,5,4,3,2,1,0:T(8,128)(2,1)S(1)} %pad_maximum_fusion.18), channel_id=1, source_target_pairs={{0,4},{1,5},{2,6},{3,7},{4,0},{5,1},{6,2},{7,3},{8,12},{9,13},{10,... | collective-permute-start | bytes 884744 | tf_op jit(solution)/shard_map/ppermute | solution.py:29
  36.2 14.4 %collective-permute-start.3 = (bf16[2,2,1,2,1,40,768]{6,5,4,3,2,1,0:T(8,128)(2,1)S(1)}, bf16[2,2,1,2,1,40,768]{6,5,4,3,2,1,0:T(8,128)(2,1)S(1)}, u32[]{:S(2)}, u32[]{:S(2)}) collective-permute-start(bf16[2,2,1,2,1,40,768]{6,5,4,3,2,1,0:T(8,128)(2,1)S(1)} %pad_maximum_fusion.13), channel_id=1, source_target_pairs={{0,4},{1,5},{2,6},{3,7},{4,0},{5,1},{6,2},{7,3},{8,12},{9,13},{10,... | collective-permute-start | bytes 1474568 | tf_op jit(solution)/shard_map/ppermute | solution.py:29
  38.3 13.4 %collective-permute-start.8 = (bf16[2,2,2,1,1,40,768]{6,5,4,3,2,1,0:T(8,128)(2,1)S(1)}, bf16[2,2,2,1,1,40,768]{6,5,4,3,2,1,0:T(8,128)(2,1)S(1)}, u32[]{:S(2)}, u32[]{:S(2)}) collective-permute-start(bf16[2,2,2,1,1,40,768]{6,5,4,3,2,1,0:T(8,128)(2,1)S(1)} %pad_maximum_fusion.14), channel_id=1, source_target_pairs={{0,2},{1,3},{2,0},{3,1},{4,6},{5,7},{6,4},{7,5},{8,10},{9,11},{10,... | collective-permute-start | bytes 1474568 | tf_op jit(solution)/shard_map/ppermute | solution.py:29
  45.5 12.0 %collective-permute-start.15 = (bf16[2,2,2,1,1,32,1152]{6,5,4,3,2,1,0:T(8,128)(2,1)}, bf16[2,2,2,1,1,32,1152]{6,5,4,3,2,1,0:T(8,128)(2,1)S(1)}, u32[]{:S(2)}, u32[]{:S(2)}) collective-permute-start(bf16[2,2,2,1,1,32,1152]{6,5,4,3,2,1,0:T(8,128)(2,1)} %pad_maximum_fusion.9), channel_id=1, source_target_pairs={{0,2},{1,3},{2,0},{3,1},{4,6},{5,7},{6,4},{7,5},{8,10},{9,11},{10,... | collective-permute-start | bytes 1769480 | tf_op jit(solution)/shard_map/ppermute | solution.py:29
  51.7 6.9 %collective-permute-start.4 = (bf16[2,2,2,2,1,40,768]{6,5,4,3,2,1,0:T(8,128)(2,1)}, bf16[2,2,2,2,1,40,768]{6,5,4,3,2,1,0:T(8,128)(2,1)}, u32[]{:S(2)}, u32[]{:S(2)}) collective-permute-start(bf16[2,2,2,2,1,40,768]{6,5,4,3,2,1,0:T(8,128)(2,1)} %pad_maximum_fusion.7), channel_id=1, source_target_pairs={{0,1},{1,0},{2,3},{3,2},{4,5},{5,4},{6,7},{7,6},{8,9},{9,8},{10,11... | collective-permute-start | bytes 2949128 | tf_op jit(solution)/shard_map/ppermute | solution.py:29
  58.6 29.8 %collective-permute-start.16 = (bf16[2,2,2,2,1,32,1152]{6,5,4,3,2,1,0:T(8,128)(2,1)}, bf16[2,2,2,2,1,32,1152]{6,5,4,3,2,1,0:T(8,128)(2,1)}, u32[]{:S(2)}, u32[]{:S(2)}) collective-permute-start(bf16[2,2,2,2,1,32,1152]{6,5,4,3,2,1,0:T(8,128)(2,1)} %pad_maximum_fusion.5), channel_id=1, source_target_pairs={{0,1},{1,0},{2,3},{3,2},{4,5},{5,4},{6,7},{7,6},{8,9},{9,8},{10,11... | collective-permute-start | bytes 3538952 | tf_op jit(solution)/shard_map/ppermute | solution.py:29
  69.3 19.0 %collective-permute-start.10 = (bf16[1,1,128,512]{3,2,1,0:T(8,128)(2,1)S(1)}, bf16[1,1,128,512]{3,2,1,0:T(8,128)(2,1)S(1)}, u32[]{:S(2)}, u32[]{:S(2)}) collective-permute-start(bf16[1,1,128,512]{3,2,1,0:T(8,128)(2,1)S(1)} %maximum_bitcast_fusion.2), channel_id=1, source_target_pairs={{0,16},{8,24},{16,0},{24,8},{1,17},{9,25},{17,1},{25,9},{2,18},{10... | collective-permute-start | bytes 393224 | tf_op jit(solution)/shard_map/ppermute | solution.py:29
  88.3 32.3 %collective-permute-start.11 = (bf16[2,1,128,512]{3,2,1,0:T(8,128)(2,1)S(1)}, bf16[2,1,128,512]{3,2,1,0:T(8,128)(2,1)S(1)}, u32[]{:S(2)}, u32[]{:S(2)}) collective-permute-start(bf16[2,1,128,512]{3,2,1,0:T(8,128)(2,1)S(1)} %pad_maximum_fusion.19), channel_id=1, source_target_pairs={{0,8},{8,0},{16,24},{24,16},{1,9},{9,1},{17,25},{25,17},{2,10},{10... | collective-permute-start | bytes 786440 | tf_op jit(solution)/shard_map/ppermute | solution.py:29
  125.6 6.6 %collective-permute-start.17 = (bf16[1,1,128,640]{3,2,1,0:T(8,128)(2,1)S(1)}, bf16[1,1,128,640]{3,2,1,0:T(8,128)(2,1)S(1)}, u32[]{:S(2)}, u32[]{:S(2)}) collective-permute-start(bf16[1,1,128,640]{3,2,1,0:T(8,128)(2,1)S(1)} %slice_bitcast_fusion.10), channel_id=1, source_target_pairs={{0,2},{1,3},{2,0},{3,1},{4,6},{5,7},{6,4},{7,5},{8,10},{9,11},{10,... | collective-permute-start | bytes 491528 | tf_op jit(solution)/shard_map/ppermute | solution.py:29
  127.2 7.0 %collective-permute-start.19 = (bf16[1,1,128,512]{3,2,1,0:T(8,128)(2,1)S(1)}, bf16[1,1,128,512]{3,2,1,0:T(8,128)(2,1)S(1)}, u32[]{:S(2)}, u32[]{:S(2)}) collective-permute-start(bf16[1,1,128,512]{3,2,1,0:T(8,128)(2,1)S(1)} %slice_bitcast_fusion.12), channel_id=1, source_target_pairs={{0,4},{1,5},{2,6},{3,7},{4,0},{5,1},{6,2},{7,3},{8,12},{9,13},{10,... | collective-permute-start | bytes 393224 | tf_op jit(solution)/shard_map/ppermute | solution.py:29
  132.2 8.5 %collective-permute-start.18 = (bf16[1,2,128,640]{3,2,1,0:T(8,128)(2,1)S(1)}, bf16[1,2,128,640]{3,2,1,0:T(8,128)(2,1)S(1)}, u32[]{:S(2)}, u32[]{:S(2)}) collective-permute-start(bf16[1,2,128,640]{3,2,1,0:T(8,128)(2,1)S(1)} %pad_maximum_fusion.16), channel_id=1, source_target_pairs={{0,4},{1,5},{2,6},{3,7},{4,0},{5,1},{6,2},{7,3},{8,12},{9,13},{10,... | collective-permute-start | bytes 983048 | tf_op jit(solution)/shard_map/ppermute | solution.py:29
  134.2 6.4 %collective-permute-start.20 = (bf16[2,1,128,512]{3,2,1,0:T(8,128)(2,1)S(1)}, bf16[2,1,128,512]{3,2,1,0:T(8,128)(2,1)S(1)}, u32[]{:S(2)}, u32[]{:S(2)}) collective-permute-start(bf16[2,1,128,512]{3,2,1,0:T(8,128)(2,1)S(1)} %pad_maximum_fusion.20), channel_id=1, source_target_pairs={{0,2},{1,3},{2,0},{3,1},{4,6},{5,7},{6,4},{7,5},{8,10},{9,11},{10,... | collective-permute-start | bytes 786440 | tf_op jit(solution)/shard_map/ppermute | solution.py:29
  160.7 8.4 %collective-permute-start.25 = (bf16[2,1,128,512]{3,2,1,0:T(8,128)(2,1)S(1)}, bf16[2,1,128,512]{3,2,1,0:T(8,128)(2,1)S(1)}, u32[]{:S(2)}, u32[]{:S(2)}) collective-permute-start(bf16[2,1,128,512]{3,2,1,0:T(8,128)(2,1)S(1)} %slice.526), channel_id=1, source_target_pairs={{0,2},{1,3},{2,0},{3,1},{4,6},{5,7},{6,4},{7,5},{8,10},{9,11},{10,... | collective-permute-start | bytes 786440 | tf_op jit(solution)/shard_map/ppermute | solution.py:29
  162.5 10.4 %collective-permute-start.23 = (bf16[1,2,128,640]{3,2,1,0:T(8,128)(2,1)S(1)}, bf16[1,2,128,640]{3,2,1,0:T(8,128)(2,1)S(1)}, u32[]{:S(2)}, u32[]{:S(2)}) collective-permute-start(bf16[1,2,128,640]{3,2,1,0:T(8,128)(2,1)S(1)} %slice.522), channel_id=1, source_target_pairs={{0,4},{1,5},{2,6},{3,7},{4,0},{5,1},{6,2},{7,3},{8,12},{9,13},{10,... | collective-permute-start | bytes 983048 | tf_op jit(solution)/shard_map/ppermute | solution.py:29
  169.2 5.6 %collective-permute-start.26 = (bf16[1,1,128,512]{3,2,1,0:T(8,128)(2,1)S(1)}, bf16[1,1,128,512]{3,2,1,0:T(8,128)(2,1)S(1)}, u32[]{:S(2)}, u32[]{:S(2)}) collective-permute-start(bf16[1,1,128,512]{3,2,1,0:T(8,128)(2,1)S(1)} %slice.712), channel_id=1, source_target_pairs={{0,4},{1,5},{2,6},{3,7},{4,0},{5,1},{6,2},{7,3},{8,12},{9,13},{10,... | collective-permute-start | bytes 393224 | tf_op jit(solution)/shard_map/ppermute | solution.py:29
  172.9 5.4 %collective-permute-start.24 = (bf16[1,1,128,640]{3,2,1,0:T(8,128)(2,1)S(1)}, bf16[1,1,128,640]{3,2,1,0:T(8,128)(2,1)S(1)}, u32[]{:S(2)}, u32[]{:S(2)}) collective-permute-start(bf16[1,1,128,640]{3,2,1,0:T(8,128)(2,1)S(1)} %slice.708), channel_id=1, source_target_pairs={{0,2},{1,3},{2,0},{3,1},{4,6},{5,7},{6,4},{7,5},{8,10},{9,11},{10,... | collective-permute-start | bytes 491528 | tf_op jit(solution)/shard_map/ppermute | solution.py:29
  180.3 6.3 %collective-permute-start.27 = (bf16[1,1,128,640]{3,2,1,0:T(8,128)(2,1)S(1)}, bf16[1,1,128,640]{3,2,1,0:T(8,128)(2,1)S(1)}, u32[]{:S(2)}, u32[]{:S(2)}) collective-permute-start(bf16[1,1,128,640]{3,2,1,0:T(8,128)(2,1)S(1)} %slice_bitcast_fusion.9), channel_id=1, source_target_pairs={{0,2},{1,3},{2,0},{3,1},{4,6},{5,7},{6,4},{7,5},{8,10},{9,11},{10,... | collective-permute-start | bytes 491528 | tf_op jit(solution)/shard_map/ppermute | solution.py:29
  180.4 6.8 %collective-permute-start.29 = (bf16[1,1,128,512]{3,2,1,0:T(8,128)(2,1)S(1)}, bf16[1,1,128,512]{3,2,1,0:T(8,128)(2,1)S(1)}, u32[]{:S(2)}, u32[]{:S(2)}) collective-permute-start(bf16[1,1,128,512]{3,2,1,0:T(8,128)(2,1)S(1)} %slice_bitcast_fusion.11), channel_id=1, source_target_pairs={{0,4},{1,5},{2,6},{3,7},{4,0},{5,1},{6,2},{7,3},{8,12},{9,13},{10,... | collective-permute-start | bytes 393224 | tf_op jit(solution)/shard_map/ppermute | solution.py:29
  186.7 7.1 %collective-permute-start.28 = (bf16[1,2,128,640]{3,2,1,0:T(8,128)(2,1)S(1)}, bf16[1,2,128,640]{3,2,1,0:T(8,128)(2,1)S(1)}, u32[]{:S(2)}, u32[]{:S(2)}) collective-permute-start(bf16[1,2,128,640]{3,2,1,0:T(8,128)(2,1)S(1)} %pad_maximum_fusion.17), channel_id=1, source_target_pairs={{0,4},{1,5},{2,6},{3,7},{4,0},{5,1},{6,2},{7,3},{8,12},{9,13},{10,... | collective-permute-start | bytes 983048 | tf_op jit(solution)/shard_map/ppermute | solution.py:29
  187.3 6.4 %collective-permute-start.30 = (bf16[2,1,128,512]{3,2,1,0:T(8,128)(2,1)S(1)}, bf16[2,1,128,512]{3,2,1,0:T(8,128)(2,1)S(1)}, u32[]{:S(2)}, u32[]{:S(2)}) collective-permute-start(bf16[2,1,128,512]{3,2,1,0:T(8,128)(2,1)S(1)} %pad_maximum_fusion.21), channel_id=1, source_target_pairs={{0,2},{1,3},{2,0},{3,1},{4,6},{5,7},{6,4},{7,5},{8,10},{9,11},{10,... | collective-permute-start | bytes 786440 | tf_op jit(solution)/shard_map/ppermute | solution.py:29
  208.1 7.6 %collective-permute-start.32 = (bf16[1,2,2,128,1152]{4,3,2,1,0:T(8,128)(2,1)S(1)}, bf16[1,2,2,128,1152]{4,3,2,1,0:T(8,128)(2,1)S(1)}, u32[]{:S(2)}, u32[]{:S(2)}) collective-permute-start(bf16[1,2,2,128,1152]{4,3,2,1,0:T(8,128)(2,1)S(1)} %bitcast.231), channel_id=1, source_target_pairs={{0,1},{1,0},{2,3},{3,2},{4,5},{5,4},{6,7},{7,6},{8,9},{9,8},{10,11... | collective-permute-start | bytes 3538952 | tf_op jit(solution)/shard_map/ppermute | solution.py:29
  218.3 12.5 %collective-permute-start.33 = (bf16[1,2,128,640]{3,2,1,0:T(8,128)(2,1)}, bf16[1,2,128,640]{3,2,1,0:T(8,128)(2,1)}, u32[]{:S(2)}, u32[]{:S(2)}) collective-permute-start(bf16[1,2,128,640]{3,2,1,0:T(8,128)(2,1)} %slice.534), channel_id=1, source_target_pairs={{0,4},{1,5},{2,6},{3,7},{4,0},{5,1},{6,2},{7,3},{8,12},{9,13},{10,... | collective-permute-start | bytes 983048 | tf_op jit(solution)/shard_map/ppermute | solution.py:29
  219.8 8.3 %collective-permute-start.35 = (bf16[2,1,128,512]{3,2,1,0:T(8,128)(2,1)S(1)}, bf16[2,1,128,512]{3,2,1,0:T(8,128)(2,1)S(1)}, u32[]{:S(2)}, u32[]{:S(2)}) collective-permute-start(bf16[2,1,128,512]{3,2,1,0:T(8,128)(2,1)S(1)} %slice.538), channel_id=1, source_target_pairs={{0,2},{1,3},{2,0},{3,1},{4,6},{5,7},{6,4},{7,5},{8,10},{9,11},{10,... | collective-permute-start | bytes 786440 | tf_op jit(solution)/shard_map/ppermute | solution.py:29
  232.1 5.4 %collective-permute-start.34 = (bf16[1,1,128,640]{3,2,1,0:T(8,128)(2,1)S(1)}, bf16[1,1,128,640]{3,2,1,0:T(8,128)(2,1)S(1)}, u32[]{:S(2)}, u32[]{:S(2)}) collective-permute-start(bf16[1,1,128,640]{3,2,1,0:T(8,128)(2,1)S(1)} %slice.707), channel_id=1, source_target_pairs={{0,2},{1,3},{2,0},{3,1},{4,6},{5,7},{6,4},{7,5},{8,10},{9,11},{10,... | collective-permute-start | bytes 491528 | tf_op jit(solution)/shard_map/ppermute | solution.py:29
  252.0 16.1 %collective-permute-start.40 = (bf16[2,2,2,1,1,32,1152]{6,5,4,3,2,1,0:T(8,128)(2,1)}, bf16[2,2,2,1,1,32,1152]{6,5,4,3,2,1,0:T(8,128)(2,1)}, u32[]{:S(2)}, u32[]{:S(2)}) collective-permute-start(bf16[2,2,2,1,1,32,1152]{6,5,4,3,2,1,0:T(8,128)(2,1)} %slice.700), channel_id=1, source_target_pairs={{0,2},{1,3},{2,0},{3,1},{4,6},{5,7},{6,4},{7,5},{8,10},{9,11},{10,... | collective-permute-start | bytes 1769480 | tf_op jit(solution)/shard_map/ppermute | solution.py:29
  270.1 10.8 %collective-permute-start.41 = (bf16[2,2,1,1,1,32,1152]{6,5,4,3,2,1,0:T(8,128)(2,1)}, bf16[2,2,1,1,1,32,1152]{6,5,4,3,2,1,0:T(8,128)(2,1)}, u32[]{:S(2)}, u32[]{:S(2)}) collective-permute-start(bf16[2,2,1,1,1,32,1152]{6,5,4,3,2,1,0:T(8,128)(2,1)} %slice.703), channel_id=1, source_target_pairs={{0,4},{1,5},{2,6},{3,7},{4,0},{5,1},{6,2},{7,3},{8,12},{9,13},{10,... | collective-permute-start | bytes 884744 | tf_op jit(solution)/shard_map/ppermute | solution.py:29
  280.0 16.4 %collective-permute-start.37 = (bf16[2,1,128,512]{3,2,1,0:T(8,128)(2,1)}, bf16[2,1,128,512]{3,2,1,0:T(8,128)(2,1)}, u32[]{:S(2)}, u32[]{:S(2)}) collective-permute-start(bf16[2,1,128,512]{3,2,1,0:T(8,128)(2,1)} %slice.704), channel_id=1, source_target_pairs={{0,8},{8,0},{16,24},{24,16},{1,9},{9,1},{17,25},{25,17},{2,10},{10... | collective-permute-start | bytes 786440 | tf_op jit(solution)/shard_map/ppermute | solution.py:29
  282.1 25.9 %collective-permute-start.42 = (bf16[2,1,1,1,1,32,1152]{6,5,4,3,2,1,0:T(8,128)(2,1)S(1)}, bf16[2,1,1,1,1,32,1152]{6,5,4,3,2,1,0:T(8,128)(2,1)S(1)}, u32[]{:S(2)}, u32[]{:S(2)}) collective-permute-start(bf16[2,1,1,1,1,32,1152]{6,5,4,3,2,1,0:T(8,128)(2,1)S(1)} %slice.709), channel_id=1, source_target_pairs={{0,8},{8,0},{16,24},{24,16},{1,9},{9,1},{17,25},{25,17},{2,10},{10... | collective-permute-start | bytes 442376 | tf_op jit(solution)/shard_map/ppermute | solution.py:29
  297.5 20.4 %collective-permute-start.38 = (bf16[1,1,128,512]{3,2,1,0:T(8,128)(2,1)S(1)}, bf16[1,1,128,512]{3,2,1,0:T(8,128)(2,1)S(1)}, u32[]{:S(2)}, u32[]{:S(2)}) collective-permute-start(bf16[1,1,128,512]{3,2,1,0:T(8,128)(2,1)S(1)} %slice.710), channel_id=1, source_target_pairs={{0,16},{8,24},{16,0},{24,8},{1,17},{9,25},{17,1},{25,9},{2,18},{10... | collective-permute-start | bytes 393224 | tf_op jit(solution)/shard_map/ppermute | solution.py:29
  308.1 13.0 %collective-permute-start.43 = (bf16[1,1,1,1,1,32,1152]{6,5,4,3,2,1,0:T(8,128)(2,1)S(1)}, bf16[1,1,1,1,1,32,1152]{6,5,4,3,2,1,0:T(8,128)(2,1)S(1)}, u32[]{:S(2)}, u32[]{:S(2)}) collective-permute-start(bf16[1,1,1,1,1,32,1152]{6,5,4,3,2,1,0:T(8,128)(2,1)S(1)} %slice.715), channel_id=1, source_target_pairs={{0,16},{8,24},{16,0},{24,8},{1,17},{9,25},{17,1},{25,9},{2,18},{10... | collective-permute-start | bytes 221192 | tf_op jit(solution)/shard_map/ppermute | solution.py:29
  347.6 13.3 %collective-permute-start.45 = (bf16[2,2,1,2,1,40,768]{6,5,4,3,2,1,0:T(8,128)(2,1)S(1)}, bf16[2,2,1,2,1,40,768]{6,5,4,3,2,1,0:T(8,128)(2,1)S(1)}, u32[]{:S(2)}, u32[]{:S(2)}) collective-permute-start(bf16[2,2,1,2,1,40,768]{6,5,4,3,2,1,0:T(8,128)(2,1)S(1)} %slice.702), channel_id=1, source_target_pairs={{0,4},{1,5},{2,6},{3,7},{4,0},{5,1},{6,2},{7,3},{8,12},{9,13},{10,... | collective-permute-start | bytes 1474568 | tf_op jit(solution)/shard_map/ppermute | solution.py:29
  351.1 14.2 %collective-permute-start.50 = (bf16[2,2,2,1,1,40,768]{6,5,4,3,2,1,0:T(8,128)(2,1)S(1)}, bf16[2,2,2,1,1,40,768]{6,5,4,3,2,1,0:T(8,128)(2,1)S(1)}, u32[]{:S(2)}, u32[]{:S(2)}) collective-permute-start(bf16[2,2,2,1,1,40,768]{6,5,4,3,2,1,0:T(8,128)(2,1)S(1)} %slice.701), channel_id=1, source_target_pairs={{0,2},{1,3},{2,0},{3,1},{4,6},{5,7},{6,4},{7,5},{8,10},{9,11},{10,... | collective-permute-start | bytes 1474568 | tf_op jit(solution)/shard_map/ppermute | solution.py:29
  361.1 8.7 %collective-permute-start.46 = (bf16[2,2,1,1,1,40,768]{6,5,4,3,2,1,0:T(8,128)(2,1)S(1)}, bf16[2,2,1,1,1,40,768]{6,5,4,3,2,1,0:T(8,128)(2,1)S(1)}, u32[]{:S(2)}, u32[]{:S(2)}) collective-permute-start(bf16[2,2,1,1,1,40,768]{6,5,4,3,2,1,0:T(8,128)(2,1)S(1)} %slice.706), channel_id=1, source_target_pairs={{0,2},{1,3},{2,0},{3,1},{4,6},{5,7},{6,4},{7,5},{8,10},{9,11},{10,... | collective-permute-start | bytes 737288 | tf_op jit(solution)/shard_map/ppermute | solution.py:29
  365.4 7.6 %collective-permute-start.51 = (bf16[2,2,1,1,1,40,768]{6,5,4,3,2,1,0:T(8,128)(2,1)S(1)}, bf16[2,2,1,1,1,40,768]{6,5,4,3,2,1,0:T(8,128)(2,1)S(1)}, u32[]{:S(2)}, u32[]{:S(2)}) collective-permute-start(bf16[2,2,1,1,1,40,768]{6,5,4,3,2,1,0:T(8,128)(2,1)S(1)} %slice.705), channel_id=1, source_target_pairs={{0,4},{1,5},{2,6},{3,7},{4,0},{5,1},{6,2},{7,3},{8,12},{9,13},{10,... | collective-permute-start | bytes 737288 | tf_op jit(solution)/shard_map/ppermute | solution.py:29
  369.9 7.6 %collective-permute-start.47 = (bf16[2,1,1,1,1,40,768]{6,5,4,3,2,1,0:T(8,128)(2,1)S(1)}, bf16[2,1,1,1,1,40,768]{6,5,4,3,2,1,0:T(8,128)(2,1)S(1)}, u32[]{:S(2)}, u32[]{:S(2)}) collective-permute-start(bf16[2,1,1,1,1,40,768]{6,5,4,3,2,1,0:T(8,128)(2,1)S(1)} %slice.714), channel_id=1, source_target_pairs={{0,8},{8,0},{16,24},{24,16},{1,9},{9,1},{17,25},{25,17},{2,10},{10... | collective-permute-start | bytes 368648 | tf_op jit(solution)/shard_map/ppermute | solution.py:29
  373.1 7.6 %collective-permute-start.52 = (bf16[2,1,1,1,1,40,768]{6,5,4,3,2,1,0:T(8,128)(2,1)S(1)}, bf16[2,1,1,1,1,40,768]{6,5,4,3,2,1,0:T(8,128)(2,1)S(1)}, u32[]{:S(2)}, u32[]{:S(2)}) collective-permute-start(bf16[2,1,1,1,1,40,768]{6,5,4,3,2,1,0:T(8,128)(2,1)S(1)} %slice.713), channel_id=1, source_target_pairs={{0,8},{8,0},{16,24},{24,16},{1,9},{9,1},{17,25},{25,17},{2,10},{10... | collective-permute-start | bytes 368648 | tf_op jit(solution)/shard_map/ppermute | solution.py:29
  377.6 7.0 %collective-permute-start.48 = (bf16[1,1,1,1,1,40,768]{6,5,4,3,2,1,0:T(8,128)(2,1)S(1)}, bf16[1,1,1,1,1,40,768]{6,5,4,3,2,1,0:T(8,128)(2,1)S(1)}, u32[]{:S(2)}, u32[]{:S(2)}) collective-permute-start(bf16[1,1,1,1,1,40,768]{6,5,4,3,2,1,0:T(8,128)(2,1)S(1)} %slice.719), channel_id=1, source_target_pairs={{0,16},{8,24},{16,0},{24,8},{1,17},{9,25},{17,1},{25,9},{2,18},{10... | collective-permute-start | bytes 184328 | tf_op jit(solution)/shard_map/ppermute | solution.py:29
  380.8 5.2 %collective-permute-start.53 = (bf16[1,1,1,1,1,40,768]{6,5,4,3,2,1,0:T(8,128)(2,1)S(1)}, bf16[1,1,1,1,1,40,768]{6,5,4,3,2,1,0:T(8,128)(2,1)S(1)}, u32[]{:S(2)}, u32[]{:S(2)}) collective-permute-start(bf16[1,1,1,1,1,40,768]{6,5,4,3,2,1,0:T(8,128)(2,1)S(1)} %slice.718), channel_id=1, source_target_pairs={{0,16},{8,24},{16,0},{24,8},{1,17},{9,25},{17,1},{25,9},{2,18},{10... | collective-permute-start | bytes 184328 | tf_op jit(solution)/shard_map/ppermute | solution.py:29
  (87 other events, 656.9 us)
Sparse Core Ops, SparseCore 0:
  17.9 117.1 all-gather.2
  258.6 118.8 reduce-scatter.3
